TPU v7x, 256 devices: a whole 4x4x8 slice. The times are simulated.
256 devices in a mesh: fourier: 8 (over x, core), ex: 8 (over z), ey: 4 (over y).
Axes of the slice: x: 4, y: 4, z: 8, core: 2. Of those that a mesh axis runs over, the one named last changes fastest.
Arguments:
- forcing: float32 [128, 81, 4096], P('fourier', None, ('ex', 'ey')), may hold values from -6 to 6
- element_coef: float32 [4096], P(('ex', 'ey')), may hold values from 0.5 to 2
- schur: float32 [128, 32, 32], P('fourier'), may hold values from -12 to 20, as said below
- couple: float32 [128, 32, 49], P('fourier'), may hold values from -0.875 to 0.875
- inner_inv: float32 [128, 49, 49], P('fourier'), may hold values from -3 to 4.5, as said below
- element_cell: int32 [4096], P(('ex', 'ey')), may hold values from 0 to 127, as said below
Outputs:
- velocity: float32 [128, 81, 4096], P('fourier', None, ('ex', 'ey'))
Inputs may be any that keep to these rules, and one draw needn't show every extreme that they name: `element_cell`: each aligned block of 128 entries is a permutation of 0 to 127. `schur`: each matrix is symmetric positive definite. `inner_inv`: each matrix is symmetric positive definite.
All inputs are finite; a program needn't handle non-finite values.
Results may differ from a plain program's by a relative error of at most 0.0001.
Values sent between devices are 32-bit elements; how exact they have to be, the bound alone decides.
No kernel may reach another device: no remote copies, remote signals or barrier semaphores. Data moves between devices by JAX's collectives and lax.ppermute only.
A program may use at most 64 MiB of HBM per device.

v0:
```python
import math

import jax
import jax.numpy as jnp
import numpy as np
from jax import lax
from jax.experimental import pallas as pl
from jax.experimental.pallas import tpu as pltpu
from jax.sharding import PartitionSpec as P

P_SIZE = 8
NZ = 128
ELX = 8
ELY = 16
NODES = 81
NB = 32
NI = 49
EL = ELX * ELY
PADDED = 88
MODES = 16
DEEP = 3
PITCH = 24
XROWS = ELX + 2 * DEEP
XCOLS = ELY + 2 * DEEP
XL = 384
HIGHEST = lax.Precision.HIGHEST
F32 = jnp.float32


def real_transform():
    k = np.arange(NZ)[:, None]
    z = np.arange(NZ)[None, :]
    angle = 2.0 * math.pi * (((k + 1) // 2 * z) % NZ) / NZ
    w = np.where(k % 2 == 1, np.cos(angle), np.sin(angle)) * math.sqrt(2.0 / NZ)
    w[0] = 1.0 / math.sqrt(NZ)
    w[NZ - 1] = np.cos(math.pi * np.arange(NZ)) / math.sqrt(NZ)
    return w.astype(np.float32)


def column_tables():
    lane = np.arange(EL) % 64
    half = np.arange(EL) // 64 * 64
    row = lane // DEEP
    out = []
    for first in (0, ELY - DEEP):
        col = lane % DEEP + first
        out.append(np.clip((row - DEEP) * ELY + col, 0, EL - 1))
        out.append(np.where(row < DEEP, row * ELY + col + half, 0))
        out.append(np.where((row >= DEEP + ELX) & (row < XROWS), (row - DEEP - ELX) * ELY + col + half, 0))
    out.append(row)
    out.append(half)
    return np.stack(out).astype(np.int32)


OWN, LOW, HIGH, LEFT, RIGHT, NONE = range(6)


def extended_tables():
    lane = np.arange(XL)
    row, col = lane // PITCH, lane % PITCH
    middle = (col >= DEEP) & (col < DEEP + ELY)
    left = (col < DEEP) & (row < XROWS)
    right = (col >= DEEP + ELY) & (col < XCOLS) & (row < XROWS)
    own = middle & (row >= DEEP) & (row < DEEP + ELX)
    low = middle & (row < DEEP)
    high = middle & (row >= DEEP + ELX) & (row < XROWS)
    source = np.full(XL, NONE)
    tables = np.zeros((6, XL), np.int64)
    for number, mask, index in (
        (OWN, own, (row - DEEP) * ELY + col - DEEP),
        (LOW, low, row * ELY + col - DEEP),
        (HIGH, high, (row - DEEP - ELX) * ELY + col - DEEP),
        (LEFT, left, row * DEEP + col),
        (RIGHT, right, row * DEEP + col - DEEP - ELY),
    ):
        source[mask] = number
        tables[number][mask] = index[mask]
    tables[5] = source
    home = np.arange(EL) // ELY * PITCH + DEEP * PITCH + np.arange(EL) % ELY + DEEP
    tables = tables.reshape(6, XL // EL, EL).reshape(-1, EL)
    return np.concatenate([tables, (home % EL)[None], (home // EL)[None]]).astype(np.int32), source.reshape(-1, EL)


EXT_TABLE, EXT_SOURCE = extended_tables()
COL_TABLE = column_tables()


def pick(values, index):
    return jnp.take_along_axis(values, jnp.broadcast_to(index, values.shape), axis=1, mode="promise_in_bounds")


def dot(a, b):
    return lax.dot_general(a, b, (((1,), (0,)), ((), ())), precision=HIGHEST, preferred_element_type=F32)


def transform_kernel(table, planes, out):
    groups, nodes = planes.shape[0], planes.shape[1]
    for n in range(nodes):
        block = planes[:, n].reshape(NZ, EL)
        out[:, n] = dot(table[...], block).reshape(groups, NZ // groups, EL)


def condense_kernel(spectral, coef, cell, couple, inner, condensed, base, down, up, coef_grid):
    lane = lax.broadcasted_iota(jnp.int32, (EL, EL), 1)
    elem = lax.broadcasted_iota(jnp.int32, (EL, EL), 0)
    cells = jnp.transpose(jnp.broadcast_to(cell[...], (EL, EL)))
    order = jnp.sum(jnp.where(cells == lane, elem, 0), axis=0, keepdims=True)
    scale = pick(jnp.broadcast_to(coef[...], (16, EL)), order)
    coef_grid[...] = scale[0:8]
    inverse = 1.0 / scale[0:1]
    first = lax.broadcasted_iota(jnp.int32, (16, EL), 1) < 64

    def messages(top, bottom):
        return (
            jnp.where(first, top, pltpu.roll(bottom, 64, 1)),
            jnp.where(first, pltpu.roll(top, 48, 1), pltpu.roll(bottom, 112, 1)),
        )

    down[MODES], up[MODES] = messages(scale, scale)

    def mode(m, _):
        fields = pick(spectral[pl.ds(m, PADDED, stride=MODES), :], order)
        within = fields[NB:NODES]
        value = fields[0:NB] - dot(couple[m], within)
        condensed[m] = value
        base[m, 0:NI] = dot(inner[pl.ds(m, NI, stride=MODES), :], within) * inverse
        down[m], up[m] = messages(value[0:16], value[16:32])
        return 0

    lax.fori_loop(0, MODES, mode, 0, unroll=2)


def columns_kernel(condensed, coef_grid, low, high, table, left, right):
    row = table[6:7, :]
    first = jnp.broadcast_to(table[7:8, :], (16, EL)) == 0
    is_own = jnp.broadcast_to((row >= DEEP) & (row < DEEP + ELX), (16, EL))
    is_low = jnp.broadcast_to(row < DEEP, (16, EL))

    def message(top, bottom, lo, hi, at):
        own = jnp.where(first, pick(top, table[at : at + 1, :]), pick(bottom, table[at : at + 1, :]))
        other = jnp.where(is_low, pick(lo, table[at + 1 : at + 2, :]), pick(hi, table[at + 2 : at + 3, :]))
        return jnp.where(is_own, own, other)

    scale = jnp.concatenate([coef_grid[...], coef_grid[...]], 0)
    left[MODES] = message(scale, scale, low[MODES], high[MODES], 0)
    right[MODES] = message(scale, scale, low[MODES], high[MODES], 3)

    def mode(m, _):
        top, bottom = condensed[m, 0:16], condensed[m, 16:32]
        left[m] = message(top, bottom, low[m], high[m], 0)
        right[m] = message(top, bottom, low[m], high[m], 3)
        return 0

    lax.fori_loop(0, MODES, mode, 0, unroll=2)


def krylov_kernel(
    position, condensed, coef_grid, low, high, left, right, schur, table, basis, sums, keep_ref, weight_ref, parts
):
    sources = (condensed, low, high, left, right)

    def spread(own, others, half):
        pieces = []
        for j in range(XL // EL):
            source = jnp.broadcast_to(table[15 + j : 16 + j, :], own.shape)
            piece = jnp.zeros(own.shape, F32)
            for number, values in ((OWN, own), (LOW, others[0]), (HIGH, others[1]), (LEFT, others[2]), (RIGHT, others[3])):
                if not (EXT_SOURCE[j] == number).any():
                    continue
                index = table[3 * number + j : 3 * number + j + 1, :]
                if number != OWN and half:
                    index = index + 64
                piece = jnp.where(source == number, pick(values, index), piece)
            pieces.append(piece)
        return jnp.concatenate(pieces, 1)

    lane = lax.broadcasted_iota(jnp.int32, (NB, XL), 1)
    slot = lax.broadcasted_iota(jnp.int32, (NB, XL), 0)
    row, col = lane // PITCH, lane % PITCH
    grid_row = row - DEEP + position[0] * ELX
    grid_col = col - DEEP + position[1] * ELY
    last_row, last_col = position[2] * ELX - 1, position[3] * ELY - 1
    inside = (grid_row >= 0) & (grid_row <= last_row) & (grid_col >= 0) & (grid_col <= last_col)
    inside = inside & (row < XROWS) & (col < XCOLS)
    dropped = (grid_row == 0) & ((slot == 0) | (slot >= 24))
    dropped = dropped | (grid_row == last_row) & (slot >= 8) & (slot <= 16)
    dropped = dropped | (grid_col == 0) & (slot <= 8)
    dropped = dropped | (grid_col == last_col) & (slot >= 16) & (slot <= 24)
    own = (row >= DEEP) & (row < DEEP + ELX) & (col >= DEEP) & (col < DEEP + ELY)
    keep = jnp.where(inside & ~dropped, 1.0, 0.0).astype(F32)
    keep_ref[...] = keep
    weight_ref[0] = jnp.where(own, 1.0, 0.0).astype(F32)
    weight_ref[1] = jnp.where(own, keep * jnp.where(slot % P_SIZE == 0, 0.25, 0.5), 0.0).astype(F32)
    scale8 = spread(coef_grid[...], [s[MODES, 0:8] for s in sources[1:]], 0)
    scale = jnp.where(inside[0:1], scale8[0:1], 0.0)

    sub = lax.broadcasted_iota(jnp.int32, (8, XL), 0)
    zero = sub == 0
    back = (8 - sub) % 8

    def rev(tile):
        return jnp.take_along_axis(tile, back, axis=0, mode="promise_in_bounds")

    def assemble(values):
        t = [values[8 * i : 8 * i + 8] for i in range(4)]
        for axis, (a, b, c, d) in ((PITCH, (1, 2, 3, 0)), (1, (2, 3, 0, 1))):
            ahead, behind = axis, XL - axis
            if axis == PITCH:
                prev3 = pltpu.roll(jnp.where(zero, t[2], rev(t[1])), ahead, 1)
                prev0 = pltpu.roll(jnp.where(zero, t[1], 0.0), ahead, 1)
                next1 = pltpu.roll(jnp.where(zero, t[0], rev(t[3])), behind, 1)
                next2 = pltpu.roll(jnp.where(zero, t[3], 0.0), behind, 1)
                t = [t[0] + prev0, t[1] + next1, t[2] + next2, t[3] + prev3]
            else:
                prev0 = pltpu.roll(jnp.where(zero, t[3], rev(t[2])), ahead, 1)
                prev1 = pltpu.roll(jnp.where(zero, t[2], 0.0), ahead, 1)
                next2 = pltpu.roll(jnp.where(zero, t[1], rev(t[0])), behind, 1)
                next3 = pltpu.roll(jnp.where(zero, t[0], 0.0), behind, 1)
                t = [t[0] + prev0, t[1] + prev1, t[2] + next2, t[3] + next3]
        return keep_ref[...] * jnp.concatenate(t, 0)

    eye = lax.broadcasted_iota(jnp.int32, (NB, NB), 0) == lax.broadcasted_iota(jnp.int32, (NB, NB), 1)
    home = table[18:19, :]
    home_at = jnp.broadcast_to(table[19:20, :], (NB, EL))

    def mode(m, _):
        matrix = schur[m]
        trace = jnp.sum(jnp.sum(jnp.where(eye, matrix, 0.0), axis=0, keepdims=True), axis=1, keepdims=True)
        shift = (0.5 * NB) / trace
        others = [s[m] for s in sources[1:]]
        value = jnp.concatenate([spread(condensed[m, 16 * h : 16 * h + 16], others, h) for h in (0, 1)], 0)
        v = [assemble(jnp.where(inside, value, 0.0))]
        w = []
        for step in range(3):
            w.append(scale * dot(matrix, v[step]))
            if step < 2:
                v.append(assemble(w[step]) * shift - v[step])
        mine, weight = weight_ref[0], weight_ref[1]
        k = 0
        for first, second, mask in (
            (v[0], v[0], weight), (v[0], v[1], weight), (v[1], v[1], weight),
            (v[0], w[0], mine), (v[1], w[0], mine), (v[1], w[1], mine), (v[2], w[1], mine), (v[2], w[2], mine),
        ):
            whole = jnp.sum(first * second * mask, axis=0, keepdims=True)
            folded = whole[:, 0:EL] + whole[:, EL : 2 * EL] + whole[:, 2 * EL :]
            parts[pl.ds(MODES * k + m, 1), :] = folded
            k += 1
        for i in range(3):
            out = jnp.zeros((NB, EL), F32)
            for j in range(XL // EL):
                out = jnp.where(home_at == j, pick(v[i][:, EL * j : EL * j + EL], home), out)
            basis[i, m] = out
        return 0

    lax.fori_loop(0, MODES, mode, 0, unroll=2)
    ones = jnp.ones((8, EL), F32)
    total = lax.dot_general(ones, parts[...], (((1,), (1,)), ((), ())), precision=HIGHEST, preferred_element_type=F32)
    sums[...] = total[0:1]


def finish_kernel(gathered, basis, base, couple, cell, out, coefs):
    total = jnp.broadcast_to(jnp.sum(gathered[...].reshape(-1, EL), axis=0, keepdims=True), (8, EL))
    b0, b1, b2, h0, h1, h2, h3, h4 = [
        total if k == 0 else pltpu.roll(total, EL - MODES * k, 1) for k in range(8)
    ]
    tiny = 2e-7
    l1, l2 = h1 / h0, h2 / h0
    d1 = h2 - l1 * h1
    ok1 = d1 > tiny * h2
    d1 = jnp.where(ok1, d1, 1.0)
    l12 = jnp.where(ok1, (h3 - l1 * h2) / d1, 0.0)
    d2 = h4 - l2 * h2 - l12 * l12 * d1
    ok2 = d2 > tiny * h4
    y1 = b1 - l1 * b0
    y2 = b2 - l2 * b0 - l12 * y1
    c2 = jnp.where(ok2, y2 / jnp.where(ok2, d2, 1.0), 0.0)
    c1 = jnp.where(ok1, y1 / d1, 0.0) - l12 * c2
    c0 = b0 / h0 - l1 * c1 - l2 * c2
    coefs[0], coefs[1], coefs[2] = c0, c1, c2
    index = cell[...]

    for m in range(MODES):
        c = [coefs[i, 0:1, m : m + 1] for i in range(3)]
        x = c[0] * basis[0, m] + c[1] * basis[1, m] + c[2] * basis[2, m]
        within = base[m, 0:NI] - lax.dot_general(
            couple[m], x, (((0,), (0,)), ((), ())), precision=HIGHEST, preferred_element_type=F32
        )
        fields = jnp.concatenate([x, within, jnp.zeros((PADDED - NODES, EL), F32)], 0)
        out[pl.ds(m, PADDED, stride=MODES), :] = pick(fields, index)


def call(kernel, shapes, scratch=(), smem=0):
    def run(*operands):
        many = isinstance(shapes, list)
        outs = [jax.ShapeDtypeStruct(s, F32) for s in (shapes if many else [shapes])]
        whole = pl.BlockSpec(memory_space=pltpu.VMEM)
        specs = [pl.BlockSpec(memory_space=pltpu.SMEM)] * smem + [whole] * (len(operands) - smem)
        return pl.pallas_call(
            kernel,
            out_shape=outs if many else outs[0],
            in_specs=specs,
            out_specs=[whole] * len(outs) if many else whole,
            scratch_shapes=list(scratch),
            name=kernel.__name__,
        )(*operands)

    return run


def swap(array):
    return lax.all_to_all(array, "fourier", split_axis=0, concat_axis=0, tiled=True)


def ring(axis, step):
    count = lax.axis_size(axis)
    return [(i, (i + step) % count) for i in range(count)]


def neighbours(to_low, to_high, axis):
    return lax.ppermute(to_high, axis, ring(axis, 1)), lax.ppermute(to_low, axis, ring(axis, -1))


def on_device(forcing, element_coef, schur, couple, inner_inv, element_cell):
    parts = lax.axis_size("fourier")
    group = PADDED // parts
    table = jnp.asarray(real_transform())
    cell = element_cell.reshape(1, EL)
    exchanged = (parts, group, MODES, EL)

    planes = jnp.pad(jnp.transpose(forcing, (1, 0, 2)), ((0, PADDED - NODES), (0, 0), (0, 0)))
    planes = swap(planes).reshape(exchanged)
    spectral = swap(call(transform_kernel, exchanged)(table, planes).reshape(PADDED, MODES, EL))

    message = (MODES + 1, 16, EL)
    condensed, base, down, up, coef_grid = call(
        condense_kernel, [(MODES, NB, EL), (MODES, 56, EL), message, message, (8, EL)]
    )(
        spectral.reshape(PADDED * MODES, EL),
        element_coef.reshape(1, EL),
        cell,
        couple,
        jnp.transpose(inner_inv, (1, 0, 2)).reshape(NI * MODES, NI),
    )
    low, high = neighbours(down, up, "ex")
    left, right = call(columns_kernel, [message, message])(condensed, coef_grid, low, high, jnp.asarray(COL_TABLE))
    left, right = neighbours(left, right, "ey")
    position = jnp.stack(
        [lax.axis_index("ex"), lax.axis_index("ey"), lax.axis_size("ex"), lax.axis_size("ey")]
    ).astype(jnp.int32)
    basis, sums = call(
        krylov_kernel,
        [(3, MODES, NB, EL), (1, EL)],
        [pltpu.VMEM((NB, XL), F32), pltpu.VMEM((2, NB, XL), F32), pltpu.VMEM((EL, EL), F32)],
        smem=1,
    )(position, condensed, coef_grid, low, high, left, right, schur, jnp.asarray(EXT_TABLE))
    copies = lax.axis_size("ex") * lax.axis_size("ey")
    gathered = lax.all_to_all(
        jnp.broadcast_to(sums[None], (copies, 1, EL)), ("ex", "ey"), split_axis=0, concat_axis=0, tiled=True
    )
    modal = call(finish_kernel, (PADDED * MODES, EL), [pltpu.VMEM((3, 8, EL), F32)])(
        gathered, basis, base, couple, cell
    )
    modal = swap(modal.reshape(PADDED, MODES, EL)).reshape(exchanged)
    velocity = swap(call(transform_kernel, exchanged)(table.T, modal).reshape(PADDED, MODES, EL))
    return jnp.transpose(velocity[:NODES], (1, 0, 2))


def solution(mesh):
    placed = (
        P("fourier", None, ("ex", "ey")),
        P(("ex", "ey")),
        P("fourier", None, None),
        P("fourier", None, None),
        P("fourier", None, None),
        P(("ex", "ey")),
    )
    return jax.shard_map(
        on_device,
        mesh=mesh,
        in_specs=placed,
        out_specs=P("fourier", None, ("ex", "ey")),
        check_vma=False,
    )
```

profile of v0, /device:TPU:1, one launch (start us, length us, event | category | flops | bytes accessed | tf_op | source)
XLA Modules:
  0.0 140.8 jit_solution(15581814653230657094)
XLA Ops:
  0.0 1.1 pad.4
  1.1 17.9 %all_to_all.25 = f32[88,16,128]{2,1,0:T(8,128)} all-to-all(f32[88,16,128]{2,1,0:T(8,128)S(1)} %pad.4), channel_id=1, replica_groups=mesh['fourier'=8,'ex'=8,'ey'=4] {'fourier'}, dimensions={0} | all-to-all | bytes 1441792 | tf_op jit(solution)/shard_map/all_to_all | solution.py:311
  19.1 2.8 %transform_kernel.2 = f32[8,11,16,128]{3,2,1,0:T(8,128)} custom-call(f32[128,128]{1,0:T(8,128)} %constant.22.clone.table, f32[8,11,16,128]{3,2,1,0:T(8,128)} %bitcast.19), custom_call_target="tpu_custom_call" | custom-call | tf_op jit(solution)/shard_map/transform_kernel/pallas_call | solution.py:298
  21.8 16.7 %all_to_all.26 = f32[88,16,128]{2,1,0:T(8,128)} all-to-all(f32[88,16,128]{2,1,0:T(8,128)} %bitcast.20), channel_id=1, replica_groups=mesh['fourier'=8,'ex'=8,'ey'=4] {'fourier'}, dimensions={0} | all-to-all | bytes 1441792 | tf_op jit(solution)/shard_map/all_to_all | solution.py:311
  38.6 5.5 %condense_kernel.1 = (f32[16,32,128]{2,1,0:T(8,128)}, f32[16,56,128]{2,1,0:T(8,128)}, f32[17,16,128]{2,1,0:T(8,128)}, f32[17,16,128]{2,1,0:T(8,128)}, f32[8,128]{1,0:T(8,128)}) custom-call(f32[1408,128]{1,0:T(8,128)} %bitcast.18, f32[1,128]{1,0:T(1,128)} %bitcast.27, s32[1,128]{1,0:T(1,128)} %bitcast.25, f32[16,32,49]{2,1,0:T(8,128)} %couple.3, ...), custom_call_target="tpu_custom_call" | custom-call | tf_op jit(solution)/shard_map/condense_kernel/pallas_call | solution.py:298
  44.0 1.0 collective-permute-start
  45.0 3.9 %collective-permute-start.1 = (f32[17,16,128]{2,1,0:T(8,128)}, f32[17,16,128]{2,1,0:T(8,128)S(1)}, u32[]{:S(2)}, u32[]{:S(2)}) collective-permute-start(f32[17,16,128]{2,1,0:T(8,128)} %get-tuple-element.17), channel_id=1, source_target_pairs={{0,28},{4,0},{8,4},{12,8},{16,12},{20,16},{24,20},{28,24},{1,29},{... | collective-permute-start | bytes 417800 | tf_op jit(solution)/shard_map/ppermute | solution.py:320
  49.0 3.3 %collective-permute-done.low = f32[17,16,128]{2,1,0:T(8,128)S(1)} collective-permute-done((f32[17,16,128]{2,1,0:T(8,128)}, f32[17,16,128]{2,1,0:T(8,128)S(1)}, u32[]{:S(2)}, u32[]{:S(2)}) %collective-permute-start) | collective-permute-done | bytes 139296 | tf_op jit(solution)/shard_map/ppermute | solution.py:320
  52.3 0.0 copy-start
  52.3 0.0 collective-permute-done.1.high
  52.3 0.0 copy-start.1
  52.3 0.6 copy-done
  52.9 0.1 copy-done.1
  53.0 2.9 %columns_kernel.1 = (f32[17,16,128]{2,1,0:T(8,128)}, f32[17,16,128]{2,1,0:T(8,128)}) custom-call(f32[16,32,128]{2,1,0:T(8,128)} %get-tuple-element.14.condensed, f32[8,128]{1,0:T(8,128)} %get-tuple-element.15.coef_grid, f32[17,16,128]{2,1,0:T(8,128)} %copy-done, f32[17,16,128]{2,1,0:T(8,128)} %copy-done.1, s32[8,128]{1,0:T(8,128)} %constant.23.clone.table), custom_call_target="tpu_custom_call" | custom-call | tf_op jit(solution)/shard_map/columns_kernel/pallas_call | solution.py:298
  55.9 1.3 collective-permute-start.2
  57.2 1.4 %collective-permute-start.3 = (f32[17,16,128]{2,1,0:T(8,128)}, f32[17,16,128]{2,1,0:T(8,128)S(1)}, u32[]{:S(2)}, u32[]{:S(2)}) collective-permute-start(f32[17,16,128]{2,1,0:T(8,128)} %get-tuple-element.19), channel_id=1, source_target_pairs={{0,3},{1,0},{2,1},{3,2},{4,7},{5,4},{6,5},{7,6},{8,11},{9,8},{10,9... | collective-permute-start | bytes 417800 | tf_op jit(solution)/shard_map/ppermute | solution.py:320
  58.6 0.7 pad_add_fusion.position
  59.3 2.0 %collective-permute-done.2.left = f32[17,16,128]{2,1,0:T(8,128)S(1)} collective-permute-done((f32[17,16,128]{2,1,0:T(8,128)}, f32[17,16,128]{2,1,0:T(8,128)S(1)}, u32[]{:S(2)}, u32[]{:S(2)}) %collective-permute-start.2) | collective-permute-done | bytes 139296 | tf_op jit(solution)/shard_map/ppermute | solution.py:320
  61.3 0.0 copy-start.2
  61.3 0.0 collective-permute-done.3.right
  61.3 0.6 copy-done.2
  61.9 0.0 copy-start.3
  61.9 0.7 copy-done.3
  62.6 17.9 %krylov_kernel.1 = (f32[3,16,32,128]{3,2,1,0:T(8,128)}, f32[1,128]{1,0:T(1,128)}) custom-call(s32[4]{0:T(128)} %pad_add_fusion.position, f32[16,32,128]{2,1,0:T(8,128)} %get-tuple-element.14.condensed, f32[8,128]{1,0:T(8,128)} %get-tuple-element.15.coef_grid, f32[17,16,128]{2,1,0:T(8,128)} %copy-done, f32[17,16,128]{2,1,0:T(8,128)} %copy-done.1, ...), custom_call_target="tpu_custom_call" | custom-call | tf_op jit(solution)/shard_map/krylov_kernel/pallas_call | solution.py:298
  80.5 0.0 copy-start.4
  80.5 0.7 copy-done.4
  81.2 15.7 %all_to_all.27.gathered = f32[32,1,128]{2,1,0:T(1,128)} all-to-all(f32[32,1,128]{2,1,0:T(1,128)S(1)} %broadcast_in_dim.9), channel_id=1, replica_groups=mesh['fourier'=8,'ex'=8,'ey'=4] {'ex','ey'}, dimensions={0} | all-to-all | bytes 32768 | tf_op jit(solution)/shard_map/all_to_all | solution.py:357
  96.9 3.5 %finish_kernel.1 = f32[1408,128]{1,0:T(8,128)} custom-call(f32[32,1,128]{2,1,0:T(1,128)} %all_to_all.27.gathered, f32[3,16,32,128]{3,2,1,0:T(8,128)} %get-tuple-element.21.basis, f32[16,56,128]{2,1,0:T(8,128)} %get-tuple-element.22.base, f32[16,32,49]{2,1,0:T(8,128)} %couple.3, s32[1,128]{1,0:T(1,128)} %bitcast.26), custom_call_target="tpu_custom_call" | custom-call | tf_op jit(solution)/shard_map/finish_kernel/pallas_call | solution.py:298
  100.3 20.8 %all_to_all.28 = f32[88,16,128]{2,1,0:T(8,128)} all-to-all(f32[88,16,128]{2,1,0:T(8,128)} %bitcast.17), channel_id=1, replica_groups=mesh['fourier'=8,'ex'=8,'ey'=4] {'fourier'}, dimensions={0} | all-to-all | bytes 1441792 | tf_op jit(solution)/shard_map/all_to_all | solution.py:311
  121.1 2.7 %transform_kernel.3 = f32[8,11,16,128]{3,2,1,0:T(8,128)} custom-call(f32[128,128]{1,0:T(8,128)} %constant.27.table, f32[8,11,16,128]{3,2,1,0:T(8,128)} %bitcast.21), custom_call_target="tpu_custom_call" | custom-call | tf_op jit(solution)/shard_map/transform_kernel/pallas_call | solution.py:298
  123.9 16.0 %all_to_all.29 = f32[88,16,128]{2,1,0:T(8,128)S(1)} all-to-all(f32[88,16,128]{2,1,0:T(8,128)} %bitcast.22), channel_id=1, replica_groups=mesh['fourier'=8,'ex'=8,'ey'=4] {'fourier'}, dimensions={0} | all-to-all | bytes 1441792 | tf_op jit(solution)/shard_map/all_to_all | solution.py:311
  139.9 0.9 slice_bitcast_fusion
  (1 shorter events, 0.0 us)
Async XLA Ops:
  44.0 8.2 %collective-permute-start = (f32[17,16,128]{2,1,0:T(8,128)}, f32[17,16,128]{2,1,0:T(8,128)S(1)}, u32[]{:S(2)}, u32[]{:S(2)}) collective-permute-start(f32[17,16,128]{2,1,0:T(8,128)} %get-tuple-element.16), channel_id=1, source_target_pairs={{0,4},{4,8},{8,12},{12,16},{16,20},{20,24},{24,28},{28,0},{1,5},{5... | collective-permute-start | bytes 417800 | tf_op jit(solution)/shard_map/ppermute | solution.py:320
  45.0 7.2 %collective-permute-start.1 = (f32[17,16,128]{2,1,0:T(8,128)}, f32[17,16,128]{2,1,0:T(8,128)S(1)}, u32[]{:S(2)}, u32[]{:S(2)}) collective-permute-start(f32[17,16,128]{2,1,0:T(8,128)} %get-tuple-element.17), channel_id=1, source_target_pairs={{0,28},{4,0},{8,4},{12,8},{16,12},{20,16},{24,20},{28,24},{1,29},{... | collective-permute-start | bytes 417800 | tf_op jit(solution)/shard_map/ppermute | solution.py:320
  52.3 0.6 copy-start
  52.3 0.7 copy-start.1
  55.9 5.4 %collective-permute-start.2 = (f32[17,16,128]{2,1,0:T(8,128)}, f32[17,16,128]{2,1,0:T(8,128)S(1)}, u32[]{:S(2)}, u32[]{:S(2)}) collective-permute-start(f32[17,16,128]{2,1,0:T(8,128)} %get-tuple-element.18), channel_id=1, source_target_pairs={{0,1},{1,2},{2,3},{3,0},{4,5},{5,6},{6,7},{7,4},{8,9},{9,10},{10,1... | collective-permute-start | bytes 417800 | tf_op jit(solution)/shard_map/ppermute | solution.py:320
  57.2 4.1 %collective-permute-start.3 = (f32[17,16,128]{2,1,0:T(8,128)}, f32[17,16,128]{2,1,0:T(8,128)S(1)}, u32[]{:S(2)}, u32[]{:S(2)}) collective-permute-start(f32[17,16,128]{2,1,0:T(8,128)} %get-tuple-element.19), channel_id=1, source_target_pairs={{0,3},{1,0},{2,1},{3,2},{4,7},{5,4},{6,5},{7,6},{8,11},{9,8},{10,9... | collective-permute-start | bytes 417800 | tf_op jit(solution)/shard_map/ppermute | solution.py:320
  61.3 0.6 copy-start.2
  61.9 0.7 copy-start.3
  80.5 0.7 copy-start.4
where the time goes:
time: 141 us
  blocking collectives  87.2 us (62%)
  Pallas kernels  35.2 us (25%)
  starting transfers between devices  7.69 us (5%)
  waiting for transfers between devices  5.3 us (4%)
  local copies, waits for them, and re-layouts  4.69 us (3%)
    all_to_all x4, blocking collectives, swap(): lax.all_to_all(array, 'fourier', split_axis=0, concat_axis=0, tiled=True)  71.4 us
    pallas_call x6, Pallas kernels, run(): pl.pallas_call(kernel, out_shape=outs if many else outs[0], in_specs=spec...  35.2 us
    all_to_all x1, blocking collectives, on_device(): lax.all_to_all(jnp.broadcast_to(sums[None], (copies, 1, EL)), ('ex', 'ey'...  15.7 us
    ppermute x2, starting transfers between devices, neighbours(): lax.ppermute(to_low, axis, ring(axis, -1))  5.38 us
    ppermute x2, waiting for transfers between devices, neighbours(): lax.ppermute(to_high, axis, ring(axis, 1))  5.27 us
  transfers between devices with their start and end apart: 4, of which 2 were waited for; matrix products, arithmetic and copies ran while one was open for 0% of the time, Pallas kernels for 0%

commit v1 on v0

v1 whole, which is shorter than its diff:
```python
import math

import jax
import jax.numpy as jnp
import numpy as np
from jax import lax
from jax.experimental import pallas as pl
from jax.experimental.pallas import tpu as pltpu
from jax.sharding import PartitionSpec as P

P_SIZE = 8
NZ = 128
ELX = 8
ELY = 16
NODES = 81
NB = 32
NI = 49
EL = ELX * ELY
PADDED = 88
MODES = 16
DEEP = 3
PITCH = 24
XROWS = ELX + 2 * DEEP
XCOLS = ELY + 2 * DEEP
XL = 384
UNROLL = 8
HIGHEST = lax.Precision.HIGHEST
F32 = jnp.float32


def real_transform():
    k = np.arange(NZ)[:, None]
    z = np.arange(NZ)[None, :]
    angle = 2.0 * math.pi * (((k + 1) // 2 * z) % NZ) / NZ
    w = np.where(k % 2 == 1, np.cos(angle), np.sin(angle)) * math.sqrt(2.0 / NZ)
    w[0] = 1.0 / math.sqrt(NZ)
    w[NZ - 1] = np.cos(math.pi * np.arange(NZ)) / math.sqrt(NZ)
    return w.astype(np.float32)


def column_tables():
    lane = np.arange(EL) % 64
    half = np.arange(EL) // 64 * 64
    row = lane // DEEP
    out = []
    for first in (0, ELY - DEEP):
        col = lane % DEEP + first
        out.append(np.clip((row - DEEP) * ELY + col, 0, EL - 1))
        out.append(np.where(row < DEEP, row * ELY + col + half, 0))
        out.append(np.where((row >= DEEP + ELX) & (row < XROWS), (row - DEEP - ELX) * ELY + col + half, 0))
    out.append(row)
    out.append(half)
    return np.stack(out).astype(np.int32)


OWN, LOW, HIGH, LEFT, RIGHT, NONE = range(6)
BLOCKS = XL // EL


def extended_tables():
    lane = np.arange(XL)
    row, col = (lane // PITCH + DEEP) % (XL // PITCH), lane % PITCH
    middle = (col >= DEEP) & (col < DEEP + ELY)
    left = (col < DEEP) & (row < XROWS)
    right = (col >= DEEP + ELY) & (col < XCOLS) & (row < XROWS)
    own = middle & (row >= DEEP) & (row < DEEP + ELX)
    low = middle & (row < DEEP)
    high = middle & (row >= DEEP + ELX) & (row < XROWS)
    source = np.full(XL, NONE)
    tables = np.zeros((6, XL), np.int64)
    for number, mask, index in (
        (OWN, own, (row - DEEP) * ELY + col - DEEP),
        (LOW, low, row * ELY + col - DEEP),
        (HIGH, high, (row - DEEP - ELX) * ELY + col - DEEP),
        (LEFT, left, row * DEEP + col),
        (RIGHT, right, row * DEEP + col - DEEP - ELY),
    ):
        source[mask] = number
        tables[number][mask] = index[mask]
    tables[5] = source
    home = np.arange(EL) // ELY * PITCH + np.arange(EL) % ELY + DEEP
    tables = tables.reshape(6, BLOCKS, EL).reshape(-1, EL)
    tables = np.concatenate([tables, (home % EL)[None], (home // EL)[None]])
    place = np.stack([row, col]).repeat(8, 0).reshape(2, 8, XL)
    return np.repeat(tables[:, None], 8, 1).astype(np.int32), source.reshape(-1, EL), place.astype(np.int32)


EXT_TABLE, EXT_SOURCE, EXT_PLACE = extended_tables()
COL_TABLE = column_tables()


def pick(values, index):
    return jnp.take_along_axis(values, jnp.broadcast_to(index, values.shape), axis=1, mode="promise_in_bounds")


def dot(a, b):
    return lax.dot_general(a, b, (((1,), (0,)), ((), ())), precision=HIGHEST, preferred_element_type=F32)


def transform_kernel(table, planes, out):
    groups, nodes = planes.shape[0], planes.shape[1]
    for n in range(nodes):
        block = planes[:, n].reshape(NZ, EL)
        out[:, n] = dot(table[...], block).reshape(groups, NZ // groups, EL)


def enter_kernel(forcing, coef, cell, planes, order, index, scale, done):
    nodes = forcing.shape[0]
    copy = pltpu.make_async_copy(forcing, planes.at[pl.ds(0, nodes)], done)
    copy.start()
    planes[nodes:PADDED] = jnp.zeros((PADDED - nodes, planes.shape[1], EL), F32)
    lane = lax.broadcasted_iota(jnp.int32, (EL, EL), 1)
    elem = lax.broadcasted_iota(jnp.int32, (EL, EL), 0)
    cells = jnp.transpose(jnp.broadcast_to(cell[...], (EL, EL)))
    found = jnp.sum(jnp.where(cells == lane, elem, 0), axis=0, keepdims=True)
    order[...] = jnp.broadcast_to(found, (8, EL))
    index[...] = jnp.broadcast_to(cell[...], (8, EL))
    scale[...] = pick(jnp.broadcast_to(coef[...], (8, EL)), found)
    copy.wait()


def leave_kernel(planes, velocity, done):
    copy = pltpu.make_async_copy(planes.at[pl.ds(0, velocity.shape[0])], velocity, done)
    copy.start()
    copy.wait()


def condense_kernel(spectral, order, scale, couple, condensed, down, up):
    first = lax.broadcasted_iota(jnp.int32, (16, EL), 1) < 64

    def messages(top, bottom):
        return (
            jnp.where(first, top, pltpu.roll(bottom, 64, 1)),
            jnp.where(first, pltpu.roll(top, 48, 1), pltpu.roll(bottom, 112, 1)),
        )

    wide = jnp.concatenate([scale[...], scale[...]], 0)
    down[MODES], up[MODES] = messages(wide, wide)

    def mode(m, _):
        fields = pick(spectral[pl.ds(m, PADDED, stride=MODES), :], order[0:1])
        value = fields[0:NB] - dot(couple[m], fields[NB:NODES])
        condensed[m] = value
        down[m], up[m] = messages(value[0:16], value[16:32])
        return 0

    lax.fori_loop(0, MODES, mode, 0, unroll=UNROLL)


def interior_kernel(spectral, order, scale, inner, base):
    inverse = 1.0 / scale[0:1]

    def mode(m, _):
        within = pick(spectral[pl.ds(NB * MODES + m, PADDED - NB, stride=MODES), :], order[0:1])[0:NI]
        base[m, 0:NI] = dot(inner[pl.ds(m, NI, stride=MODES), :], within) * inverse
        return 0

    lax.fori_loop(0, MODES, mode, 0, unroll=UNROLL)


def columns_kernel(condensed, coef_grid, low, high, table, left, right):
    row = table[6:7, :]
    first = jnp.broadcast_to(table[7:8, :], (16, EL)) == 0
    is_own = jnp.broadcast_to((row >= DEEP) & (row < DEEP + ELX), (16, EL))
    is_low = jnp.broadcast_to(row < DEEP, (16, EL))

    def message(top, bottom, lo, hi, at):
        own = jnp.where(first, pick(top, table[at : at + 1, :]), pick(bottom, table[at : at + 1, :]))
        other = jnp.where(is_low, pick(lo, table[at + 1 : at + 2, :]), pick(hi, table[at + 2 : at + 3, :]))
        return jnp.where(is_own, own, other)

    wide = jnp.concatenate([coef_grid[...], coef_grid[...]], 0)
    left[MODES] = message(wide, wide, low[MODES], high[MODES], 0)
    right[MODES] = message(wide, wide, low[MODES], high[MODES], 3)

    def mode(m, _):
        top, bottom = condensed[m, 0:16], condensed[m, 16:32]
        left[m] = message(top, bottom, low[m], high[m], 0)
        right[m] = message(top, bottom, low[m], high[m], 3)
        return 0

    lax.fori_loop(0, MODES, mode, 0, unroll=UNROLL)


def spread(tile, sources, table):
    pieces = []
    for j in range(BLOCKS):
        source = table[5 * BLOCKS + j]
        piece = tile[j]
        for number, values, half in sources:
            if (EXT_SOURCE[j] == number).any():
                index = table[BLOCKS * number + j]
                piece = jnp.where(source == number, pick(values, index + 64 if half else index), piece)
        pieces.append(piece)
    return pieces


def middle_kernel(condensed, scale, low, high, table, block):
    blank = [jnp.zeros((8, EL), F32)] * BLOCKS

    def put(m, tile, pieces):
        for j in range(BLOCKS):
            block[m, 8 * tile : 8 * tile + 8, EL * j : EL * j + EL] = pieces[j]

    put(MODES, 0, spread(blank, ((OWN, scale[...], 0), (LOW, low[MODES, 0:8], 0), (HIGH, high[MODES, 0:8], 0)), table))

    def mode(m, _):
        for tile in range(4):
            half, at = tile // 2, tile % 2 * 8
            sources = (
                (OWN, condensed[m, 8 * tile : 8 * tile + 8], 0),
                (LOW, low[m, at : at + 8], half),
                (HIGH, high[m, at : at + 8], half),
            )
            put(m, tile, spread(blank, sources, table))
        return 0

    lax.fori_loop(0, MODES, mode, 0, unroll=UNROLL)


def krylov_kernel(block, coef_grid, left, right, schur, table, place, basis, sums, keep_ref, weight_ref, parts, state):
    def sides(m, tile):
        half, at = tile // 2, tile % 2 * 8
        held = [block[m, 8 * tile : 8 * tile + 8, EL * j : EL * j + EL] for j in range(BLOCKS)]
        sources = ((LEFT, left[m, at : at + 8], half), (RIGHT, right[m, at : at + 8], half))
        return jnp.concatenate(spread(held, sources, table), 1)

    row, col = place[0], place[1]
    grid_row = row - DEEP + lax.axis_index("ex") * ELX
    grid_col = col - DEEP + lax.axis_index("ey") * ELY
    last_row, last_col = lax.axis_size("ex") * ELX - 1, lax.axis_size("ey") * ELY - 1
    inside = (grid_row >= 0) & (grid_row <= last_row) & (grid_col >= 0) & (grid_col <= last_col)
    inside = inside & (row < XROWS) & (col < XCOLS)
    own = (row >= DEEP) & (row < DEEP + ELX) & (col >= DEEP) & (col < DEEP + ELY)
    corner = lax.broadcasted_iota(jnp.int32, (8, XL), 0) == 0
    low_row, high_row, low_col, high_col = grid_row == 0, grid_row == last_row, grid_col == 0, grid_col == last_col
    for tile, (edge, other) in enumerate(((low_col, low_row), (high_row, low_col), (high_col, high_row), (low_row, high_col))):
        keep = jnp.where(inside & ~(edge | (corner & other)), 1.0, 0.0).astype(F32)
        keep_ref[8 * tile : 8 * tile + 8] = keep
        weight_ref[8 * tile : 8 * tile + 8] = jnp.where(own, keep * jnp.where(corner, 0.25, 0.5), 0.0).astype(F32)
    scale = jnp.where(inside, sides(MODES, 0), 0.0)[0:1]

    sub = lax.broadcasted_iota(jnp.int32, (8, XL), 0)
    zero = sub == 0
    back = (8 - sub) % 8

    def rev(tile):
        return jnp.take_along_axis(tile, back, axis=0, mode="promise_in_bounds")

    def assemble(values):
        t = [values[8 * i : 8 * i + 8] for i in range(4)]
        for axis, (a, b, c, d) in ((PITCH, (1, 2, 3, 0)), (1, (2, 3, 0, 1))):
            ahead, behind = axis, XL - axis
            if axis == PITCH:
                prev3 = pltpu.roll(jnp.where(zero, t[2], rev(t[1])), ahead, 1)
                prev0 = pltpu.roll(jnp.where(zero, t[1], 0.0), ahead, 1)
                next1 = pltpu.roll(jnp.where(zero, t[0], rev(t[3])), behind, 1)
                next2 = pltpu.roll(jnp.where(zero, t[3], 0.0), behind, 1)
                t = [t[0] + prev0, t[1] + next1, t[2] + next2, t[3] + prev3]
            else:
                prev0 = pltpu.roll(jnp.where(zero, t[3], rev(t[2])), ahead, 1)
                prev1 = pltpu.roll(jnp.where(zero, t[2], 0.0), ahead, 1)
                next2 = pltpu.roll(jnp.where(zero, t[1], rev(t[0])), behind, 1)
                next3 = pltpu.roll(jnp.where(zero, t[0], 0.0), behind, 1)
                t = [t[0] + prev0, t[1] + prev1, t[2] + next2, t[3] + next3]
        return keep_ref[...] * jnp.concatenate(t, 0)

    eye = lax.broadcasted_iota(jnp.int32, (NB, NB), 0) == lax.broadcasted_iota(jnp.int32, (NB, NB), 1)
    home, home_at = table[6 * BLOCKS], table[6 * BLOCKS + 1]
    own_scale = coef_grid[0:1]

    def at_home(ref):
        tiles = []
        for tile in range(4):
            one, two = (pick(ref[8 * tile : 8 * tile + 8, EL * j : EL * j + EL], home) for j in (0, 1))
            tiles.append(jnp.where(home_at == 0, one, two))
        return jnp.concatenate(tiles, 0)

    weight_ref[:, 0:EL] = at_home(weight_ref)

    def gather_mode(m):
        state[0, m] = assemble(jnp.concatenate([sides(m, tile) for tile in range(4)], 0))

    def apply_mode(i):
        def run(m):
            state[3, m] = scale * dot(schur[m], state[i, m])

        return run

    def extend_mode(i):
        def run(m):
            trace = jnp.sum(jnp.sum(jnp.where(eye, schur[m], 0.0), axis=0, keepdims=True), axis=1, keepdims=True)
            state[i + 1, m] = assemble(state[3, m]) * ((0.5 * NB) / trace) - state[i, m]

        return run

    def sum_mode(m):
        v = [at_home(state.at[i, m]) for i in range(3)]
        w = [own_scale * dot(schur[m], v[i]) for i in range(3)]
        weight = weight_ref[:, 0:EL]
        weighted = v[0] * weight
        k = 0
        for first, second in (
            (v[0], weighted), (v[1], weighted), (v[1], v[1] * weight),
            (v[0], w[0]), (v[1], w[0]), (v[1], w[1]), (v[2], w[1]), (v[2], w[2]),
        ):
            parts[pl.ds(MODES * k + m, 1), :] = jnp.sum(first * second, axis=0, keepdims=True)
            k += 1
        for i in range(3):
            basis[i, m] = v[i]

    def every(body):
        def step(m, _):
            body(m)
            return 0

        lax.fori_loop(0, MODES, step, 0, unroll=UNROLL)

    every(gather_mode)
    for i in range(2):
        every(apply_mode(i))
        every(extend_mode(i))
    every(sum_mode)
    ones = jnp.ones((8, EL), F32)
    total = lax.dot_general(ones, parts[...], (((1,), (1,)), ((), ())), precision=HIGHEST, preferred_element_type=F32)
    sums[...] = total[0:1]


def finish_kernel(gathered, basis, base, couple, cell, out, coefs):
    total = jnp.broadcast_to(jnp.sum(gathered[...].reshape(-1, EL), axis=0, keepdims=True), (8, EL))
    b0, b1, b2, h0, h1, h2, h3, h4 = [
        total if k == 0 else pltpu.roll(total, EL - MODES * k, 1) for k in range(8)
    ]
    tiny = 2e-7
    l1, l2 = h1 / h0, h2 / h0
    d1 = h2 - l1 * h1
    ok1 = d1 > tiny * h2
    d1 = jnp.where(ok1, d1, 1.0)
    l12 = jnp.where(ok1, (h3 - l1 * h2) / d1, 0.0)
    d2 = h4 - l2 * h2 - l12 * l12 * d1
    ok2 = d2 > tiny * h4
    y1 = b1 - l1 * b0
    y2 = b2 - l2 * b0 - l12 * y1
    c2 = jnp.where(ok2, y2 / jnp.where(ok2, d2, 1.0), 0.0)
    c1 = jnp.where(ok1, y1 / d1, 0.0) - l12 * c2
    c0 = b0 / h0 - l1 * c1 - l2 * c2
    coefs[0], coefs[1], coefs[2] = c0, c1, c2
    index = cell[0:1]

    for m in range(MODES):
        c = [coefs[i, 0:1, m : m + 1] for i in range(3)]
        x = c[0] * basis[0, m] + c[1] * basis[1, m] + c[2] * basis[2, m]
        within = base[m, 0:NI] - lax.dot_general(
            couple[m], x, (((0,), (0,)), ((), ())), precision=HIGHEST, preferred_element_type=F32
        )
        fields = jnp.concatenate([x, within, jnp.zeros((PADDED - NODES, EL), F32)], 0)
        out[pl.ds(m, PADDED, stride=MODES), :] = pick(fields, index)


def call(kernel, shapes=(), scratch=(), far=0, far_out=None):
    def run(*operands):
        many = isinstance(shapes, list)
        outs = [s if isinstance(s, pl.MemoryRef) else pltpu.VMEM(s, F32) for s in (shapes if many else [shapes])]
        whole, away = pl.BlockSpec(memory_space=pltpu.VMEM), pl.BlockSpec(memory_space=pl.ANY)
        near = tuple(pltpu.with_memory_space_constraint(o, pltpu.VMEM) for o in operands[far:])
        if far_out:
            outs = [jax.ShapeDtypeStruct(far_out, F32)]
        specs = [away if far_out else whole] * len(outs)
        return pl.pallas_call(
            kernel,
            out_shape=outs if many else outs[0],
            in_specs=[away] * far + [whole] * len(near),
            out_specs=specs if many else specs[0],
            scratch_shapes=list(scratch),
            compiler_params=pltpu.CompilerParams(vmem_limit_bytes=16 << 20),
            name=kernel.__name__,
        )(*operands[:far], *near)

    return run


def swap(array):
    return lax.all_to_all(array, "fourier", split_axis=0, concat_axis=0, tiled=True)


def ring(axis, step):
    count = lax.axis_size(axis)
    return [(i, (i + step) % count) for i in range(count)]


def neighbours(to_low, to_high, axis):
    return lax.ppermute(to_high, axis, ring(axis, 1)), lax.ppermute(to_low, axis, ring(axis, -1))


def on_device(forcing, element_coef, schur, couple, inner_inv, element_cell):
    parts = lax.axis_size("fourier")
    group = PADDED // parts
    table = jnp.asarray(real_transform())
    exchanged = (parts, group, MODES, EL)
    lanes = (8, EL)
    ints = pltpu.VMEM(lanes, jnp.int32)

    planes, order, index, scale = call(
        enter_kernel, [(PADDED, MODES, EL), ints, ints, lanes], [pltpu.SemaphoreType.DMA], far=1
    )(jnp.transpose(forcing, (1, 0, 2)), element_coef.reshape(1, EL), element_cell.reshape(1, EL))
    planes = swap(planes).reshape(exchanged)
    spectral = swap(call(transform_kernel, exchanged)(table, planes).reshape(PADDED, MODES, EL))
    spectral = spectral.reshape(PADDED * MODES, EL)

    message = (MODES + 1, 16, EL)
    condensed, down, up = call(condense_kernel, [(MODES, NB, EL), message, message])(spectral, order, scale, couple)
    low, high = neighbours(down, up, "ex")
    base = call(interior_kernel, (MODES, 56, EL))(
        spectral, order, scale, jnp.transpose(inner_inv, (1, 0, 2)).reshape(NI * MODES, NI)
    )
    left, right = call(columns_kernel, [message, message])(condensed, scale, low, high, jnp.asarray(COL_TABLE))
    left, right = neighbours(left, right, "ey")
    extended = jnp.asarray(EXT_TABLE)
    block = call(middle_kernel, (MODES + 1, NB, XL))(condensed, scale, low, high, extended)
    basis, sums = call(
        krylov_kernel,
        [(3, MODES, NB, EL), (1, EL)],
        [pltpu.VMEM((NB, XL), F32), pltpu.VMEM((NB, XL), F32), pltpu.VMEM((EL, EL), F32), pltpu.VMEM((4, MODES, NB, XL), F32)],
    )(block, scale, left, right, schur, extended, jnp.asarray(EXT_PLACE))
    copies = lax.axis_size("ex") * lax.axis_size("ey")
    gathered = lax.all_to_all(
        jnp.broadcast_to(sums[None], (copies, 1, EL)), ("ex", "ey"), split_axis=0, concat_axis=0, tiled=True
    )
    modal = call(finish_kernel, (PADDED * MODES, EL), [pltpu.VMEM((3, 8, EL), F32)])(
        gathered, basis, base, couple, index
    )
    modal = swap(modal.reshape(PADDED, MODES, EL)).reshape(exchanged)
    velocity = swap(call(transform_kernel, exchanged)(table.T, modal).reshape(PADDED, MODES, EL))
    velocity = call(leave_kernel, far_out=(NODES, MODES, EL), scratch=[pltpu.SemaphoreType.DMA])(velocity)
    return jnp.transpose(velocity, (1, 0, 2))


def solution(mesh):
    placed = (
        P("fourier", None, ("ex", "ey")),
        P(("ex", "ey")),
        P("fourier", None, None),
        P("fourier", None, None),
        P("fourier", None, None),
        P(("ex", "ey")),
    )
    return jax.shard_map(
        on_device,
        mesh=mesh,
        in_specs=placed,
        out_specs=P("fourier", None, ("ex", "ey")),
        check_vma=False,
    )
```

time: 141 us -> 115 us (0.82)
  blocking collectives: 87.2 us -> 66.4 us
  Pallas kernels: 35.2 us -> 17.9 us
  starting transfers between devices: 7.69 us -> 16.6 us
  waiting for transfers between devices: 5.3 us -> 11.5 us
  local copies, waits for them, and re-layouts: 4.69 us -> 2.45 us
    pallas_call x6 -> x10, Pallas kernels: 35.2 us -> 17.9 us  [run(): pl.pallas_call(kernel, out_shape=outs if many else outs[0], in_specs=[awa...]
    all_to_all x1 -> x0, blocking collectives: 15.7 us -> none  [on_device(): lax.all_to_all(jnp.broadcast_to(sums[None], (copies, 1, EL)), ('ex', 'ey'...]
    all_to_all x0 -> x1, starting transfers between devices: none -> 7.99 us  [on_device(): lax.all_to_all(jnp.broadcast_to(sums[None], (copies, 1, EL)), ('ex', 'ey'...]
    all_to_all x0 -> x1, waiting for transfers between devices: none -> 7.31 us  [on_device(): lax.all_to_all(jnp.broadcast_to(sums[None], (copies, 1, EL)), ('ex', 'ey'...]
    all_to_all x4, blocking collectives: 71.4 us -> 66.4 us  [swap(): lax.all_to_all(array, 'fourier', split_axis=0, concat_axis=0, tiled=True)]
  transfers between devices with their start and end apart: 4 -> 5, of which waited for: 2 -> 3; matrix products, arithmetic and copies ran while one was open for 0% -> 0% of each run, Pallas kernels for 0% -> 2%
where the time goes in v1:
time: 115 us
  blocking collectives  66.4 us (58%)
  Pallas kernels  17.9 us (16%)
  starting transfers between devices  16.6 us (14%)
  waiting for transfers between devices  11.5 us (10%)
  local copies, waits for them, and re-layouts  2.45 us (2%)
    all_to_all x4, blocking collectives, swap(): lax.all_to_all(array, 'fourier', split_axis=0, concat_axis=0, tiled=True)  66.4 us
    pallas_call x10, Pallas kernels, run(): pl.pallas_call(kernel, out_shape=outs if many else outs[0], in_specs=[awa...  17.9 us
    all_to_all x1, starting transfers between devices, on_device(): lax.all_to_all(jnp.broadcast_to(sums[None], (copies, 1, EL)), ('ex', 'ey'...  7.99 us
    all_to_all x1, waiting for transfers between devices, on_device(): lax.all_to_all(jnp.broadcast_to(sums[None], (copies, 1, EL)), ('ex', 'ey'...  7.31 us
    ppermute x2, starting transfers between devices, neighbours(): lax.ppermute(to_low, axis, ring(axis, -1))  5.57 us
    ppermute x2, waiting for transfers between devices, neighbours(): lax.ppermute(to_high, axis, ring(axis, 1))  4.2 us
    ppermute x2, starting transfers between devices, neighbours(): lax.ppermute(to_high, axis, ring(axis, 1))  3.05 us
  transfers between devices with their start and end apart: 5, of which 3 were waited for; matrix products, arithmetic and copies ran while one was open for 0% of the time, Pallas kernels for 2%

profile of v1, /device:TPU:1, one launch (start us, length us, event | category | flops | bytes accessed | tf_op | source)
XLA Modules:
  0.0 115.0 jit_solution(15431739740140583170)
XLA Ops:
  0.0 0.0 copy-start.9
  0.0 0.0 copy-start.10
  0.0 0.7 copy-done.9
  0.7 0.0 copy-done.10
  0.7 0.0 copy-start.1
  0.7 1.1 copy-done.1
  1.8 0.4 enter_kernel.1
  2.2 0.0 copy-start.6
  2.2 17.4 %all_to_all.25 = f32[88,16,128]{2,1,0:T(8,128)S(1)} all-to-all(f32[88,16,128]{2,1,0:T(8,128)S(1)} %get-tuple-element.16), channel_id=1, replica_groups=mesh['fourier'=8,'ex'=8,'ey'=4] {'fourier'}, dimensions={0} | all-to-all | bytes 1441792 | tf_op jit(solution)/shard_map/all_to_all | solution.py:383
  19.6 0.0 copy-done.6
  19.6 0.7 transform_kernel.2
  20.3 0.0 copy-start
  20.3 15.1 %all_to_all.26 = f32[88,16,128]{2,1,0:T(8,128)S(1)} all-to-all(f32[88,16,128]{2,1,0:T(8,128)S(1)} %bitcast.18), channel_id=1, replica_groups=mesh['fourier'=8,'ex'=8,'ey'=4] {'fourier'}, dimensions={0} | all-to-all | bytes 1441792 | tf_op jit(solution)/shard_map/all_to_all | solution.py:383
  35.4 0.0 copy-done
  35.4 1.0 condense_kernel.1
  36.4 0.0 copy-start.8
  36.4 1.7 %collective-permute-start = (f32[17,16,128]{2,1,0:T(8,128)S(1)}, f32[17,16,128]{2,1,0:T(8,128)S(1)}, u32[]{:S(2)}, u32[]{:S(2)}) collective-permute-start(f32[17,16,128]{2,1,0:T(8,128)S(1)} %get-tuple-element.20), channel_id=1, source_target_pairs={{0,4},{4,8},{8,12},{12,16},{16,20},{20,24},{24,28},{28,0},{1,5},{5... | collective-permute-start | bytes 417800 | tf_op jit(solution)/shard_map/ppermute | solution.py:392
  38.1 4.0 %collective-permute-start.1 = (f32[17,16,128]{2,1,0:T(8,128)S(1)}, f32[17,16,128]{2,1,0:T(8,128)S(1)}, u32[]{:S(2)}, u32[]{:S(2)}) collective-permute-start(f32[17,16,128]{2,1,0:T(8,128)S(1)} %get-tuple-element.21), channel_id=1, source_target_pairs={{0,28},{4,0},{8,4},{12,8},{16,12},{20,16},{24,20},{28,24},{1,29},{... | collective-permute-start | bytes 417800 | tf_op jit(solution)/shard_map/ppermute | solution.py:392
  42.1 3.0 %collective-permute-done.low = f32[17,16,128]{2,1,0:T(8,128)S(1)} collective-permute-done((f32[17,16,128]{2,1,0:T(8,128)S(1)}, f32[17,16,128]{2,1,0:T(8,128)S(1)}, u32[]{:S(2)}, u32[]{:S(2)}) %collective-permute-start) | collective-permute-done | bytes 139296 | tf_op jit(solution)/shard_map/ppermute | solution.py:392
  45.1 0.0 collective-permute-done.1.high
  45.1 0.0 copy-done.8
  45.1 0.0 copy-start.3
  45.1 0.8 columns_kernel.1
  45.9 1.4 %collective-permute-start.2 = (f32[17,16,128]{2,1,0:T(8,128)S(1)}, f32[17,16,128]{2,1,0:T(8,128)S(1)}, u32[]{:S(2)}, u32[]{:S(2)}) collective-permute-start(f32[17,16,128]{2,1,0:T(8,128)S(1)} %get-tuple-element.22), channel_id=1, source_target_pairs={{0,1},{1,2},{2,3},{3,0},{4,5},{5,6},{6,7},{7,4},{8,9},{9,10},{10,1... | collective-permute-start | bytes 417800 | tf_op jit(solution)/shard_map/ppermute | solution.py:392
  47.3 0.0 copy-start.4
  47.3 0.0 copy-start.7
  47.3 1.5 %collective-permute-start.3 = (f32[17,16,128]{2,1,0:T(8,128)S(1)}, f32[17,16,128]{2,1,0:T(8,128)S(1)}, u32[]{:S(2)}, u32[]{:S(2)}) collective-permute-start(f32[17,16,128]{2,1,0:T(8,128)S(1)} %get-tuple-element.23), channel_id=1, source_target_pairs={{0,3},{1,0},{2,1},{3,2},{4,7},{5,4},{6,5},{7,6},{8,11},{9,8},{10,9... | collective-permute-start | bytes 417800 | tf_op jit(solution)/shard_map/ppermute | solution.py:392
  48.8 0.0 copy-done.3
  48.8 1.1 middle_kernel.1.block
  49.9 0.0 copy-start.2
  50.0 1.2 %collective-permute-done.2.left = f32[17,16,128]{2,1,0:T(8,128)S(1)} collective-permute-done((f32[17,16,128]{2,1,0:T(8,128)S(1)}, f32[17,16,128]{2,1,0:T(8,128)S(1)}, u32[]{:S(2)}, u32[]{:S(2)}) %collective-permute-start.2) | collective-permute-done | bytes 139296 | tf_op jit(solution)/shard_map/ppermute | solution.py:392
  51.2 0.0 collective-permute-done.3.right
  51.2 0.0 copy-done.4
  51.2 0.0 copy-done.7
  51.2 9.9 %krylov_kernel.1 = (f32[3,16,32,128]{3,2,1,0:T(8,128)S(1)}, f32[1,128]{1,0:T(1,128)S(1)}) custom-call(f32[17,32,384]{2,1,0:T(8,128)S(1)} %middle_kernel.1.block, f32[8,128]{1,0:T(8,128)S(1)} %get-tuple-element.18.scale.coef_grid, f32[17,16,128]{2,1,0:T(8,128)S(1)} %collective-permute-done.2.left, f32[17,16,128]{2,1,0:T(8,128)S(1)} %collective-permute-done.3.right, ...), custom_call_target="tpu_custom_call" | custom-call | tf_op jit(solution)/shard_map/krylov_kernel/pallas_call | solution.py:369
  61.1 0.6 broadcast_in_dim.9
  61.7 8.0 %all-to-all-start.2 = ((f32[32,1,128]{2,1,0:T(1,128)}), f32[32,1,128]{2,1,0:T(1,128)S(1)}, u32[]{:S(2)}, u32[]{:S(2)}) async-start(f32[32,1,128]{2,1,0:T(1,128)} %broadcast_in_dim.9), calls=%async_computation.2 | async-start | bytes 32768 | tf_op jit(solution)/shard_map/all_to_all | solution.py:426
  69.7 0.0 copy-done.2
  69.7 1.2 %interior_kernel.1.base = f32[16,56,128]{2,1,0:T(8,128)S(1)} custom-call(f32[1408,128]{1,0:T(8,128)S(1)} %bitcast.15, s32[8,128]{1,0:T(8,128)S(1)} %get-tuple-element.17.order, f32[8,128]{1,0:T(8,128)S(1)} %get-tuple-element.18.scale.coef_grid, f32[784,49]{1,0:T(8,128)S(1)} %bitcast.22), custom_call_target="tpu_custom_call" | custom-call | tf_op jit(solution)/shard_map/interior_kernel/pallas_call | solution.py:369
  70.9 7.3 %all-to-all-done.2.gathered = f32[32,1,128]{2,1,0:T(1,128)S(1)} async-done(((f32[32,1,128]{2,1,0:T(1,128)}), f32[32,1,128]{2,1,0:T(1,128)S(1)}, u32[]{:S(2)}, u32[]{:S(2)}) %all-to-all-start.2) | async-done | bytes 16416 | tf_op jit(solution)/shard_map/all_to_all | solution.py:426
  78.2 1.2 %finish_kernel.1 = f32[1408,128]{1,0:T(8,128)S(1)} custom-call(f32[32,1,128]{2,1,0:T(1,128)S(1)} %all-to-all-done.2.gathered, f32[3,16,32,128]{3,2,1,0:T(8,128)S(1)} %get-tuple-element.25.basis, f32[16,56,128]{2,1,0:T(8,128)S(1)} %interior_kernel.1.base, f32[16,32,49]{2,1,0:T(8,128)S(1)} %copy-done, s32[8,128]{1,0:T(8,128)S(1)} %get-tuple-element.26.cell), custom_call_target="tpu_custom_call" | custom-call | tf_op jit(solution)/shard_map/finish_kernel/pallas_call | solution.py:369
  79.5 0.0 copy-start.5
  79.5 19.0 %all_to_all.27 = f32[88,16,128]{2,1,0:T(8,128)S(1)} all-to-all(f32[88,16,128]{2,1,0:T(8,128)S(1)} %bitcast.16), channel_id=1, replica_groups=mesh['fourier'=8,'ex'=8,'ey'=4] {'fourier'}, dimensions={0} | all-to-all | bytes 1441792 | tf_op jit(solution)/shard_map/all_to_all | solution.py:383
  98.5 0.0 copy-done.5
  98.5 0.7 transform_kernel.3
  99.2 14.9 %all_to_all.28.planes = f32[88,16,128]{2,1,0:T(8,128)S(1)} all-to-all(f32[88,16,128]{2,1,0:T(8,128)S(1)} %bitcast.20), channel_id=1, replica_groups=mesh['fourier'=8,'ex'=8,'ey'=4] {'fourier'}, dimensions={0} | all-to-all | bytes 1441792 | tf_op jit(solution)/shard_map/all_to_all | solution.py:383
  114.2 0.8 leave_kernel.1
Async XLA Ops:
  0.0 0.7 copy-start.9
  0.0 0.7 copy-start.10
  0.7 1.1 copy-start.1
  2.2 17.4 %copy-start.6 = (f32[128,128]{1,0:T(8,128)S(1)}, f32[128,128]{1,0:T(8,128)}, u32[]{:S(2)}) copy-start(f32[128,128]{1,0:T(8,128)} %constant.8.clone.table) | copy-start | bytes 196612
  20.3 15.1 %copy-start = (f32[16,32,49]{2,1,0:T(8,128)S(1)}, f32[16,32,49]{2,1,0:T(8,128)}, u32[]{:S(2)}) copy-start(f32[16,32,49]{2,1,0:T(8,128)} %couple.3) | copy-start | bytes 301060
  36.4 8.7 %copy-start.8 = (s32[8,128]{1,0:T(8,128)S(1)}, s32[8,128]{1,0:T(8,128)}, u32[]{:S(2)}) copy-start(s32[8,128]{1,0:T(8,128)} %constant.9.clone.table) | copy-start | bytes 12292
  36.4 8.7 %collective-permute-start = (f32[17,16,128]{2,1,0:T(8,128)S(1)}, f32[17,16,128]{2,1,0:T(8,128)S(1)}, u32[]{:S(2)}, u32[]{:S(2)}) collective-permute-start(f32[17,16,128]{2,1,0:T(8,128)S(1)} %get-tuple-element.20), channel_id=1, source_target_pairs={{0,4},{4,8},{8,12},{12,16},{16,20},{20,24},{24,28},{28,0},{1,5},{5... | collective-permute-start | bytes 417800 | tf_op jit(solution)/shard_map/ppermute | solution.py:392
  38.1 7.0 %collective-permute-start.1 = (f32[17,16,128]{2,1,0:T(8,128)S(1)}, f32[17,16,128]{2,1,0:T(8,128)S(1)}, u32[]{:S(2)}, u32[]{:S(2)}) collective-permute-start(f32[17,16,128]{2,1,0:T(8,128)S(1)} %get-tuple-element.21), channel_id=1, source_target_pairs={{0,28},{4,0},{8,4},{12,8},{16,12},{20,16},{24,20},{28,24},{1,29},{... | collective-permute-start | bytes 417800 | tf_op jit(solution)/shard_map/ppermute | solution.py:392
  45.1 3.7 %copy-start.3 = (s32[20,8,128]{2,1,0:T(8,128)S(1)}, s32[20,8,128]{2,1,0:T(8,128)}, u32[]{:S(2)}) copy-start(s32[20,8,128]{2,1,0:T(8,128)} %constant.10.clone.table) | copy-start | bytes 245764
  45.9 5.3 %collective-permute-start.2 = (f32[17,16,128]{2,1,0:T(8,128)S(1)}, f32[17,16,128]{2,1,0:T(8,128)S(1)}, u32[]{:S(2)}, u32[]{:S(2)}) collective-permute-start(f32[17,16,128]{2,1,0:T(8,128)S(1)} %get-tuple-element.22), channel_id=1, source_target_pairs={{0,1},{1,2},{2,3},{3,0},{4,5},{5,6},{6,7},{7,4},{8,9},{9,10},{10,1... | collective-permute-start | bytes 417800 | tf_op jit(solution)/shard_map/ppermute | solution.py:392
  47.3 3.9 %copy-start.4 = (f32[16,32,32]{2,1,0:T(8,128)S(1)}, f32[16,32,32]{2,1,0:T(8,128)}, u32[]{:S(2)}) copy-start(f32[16,32,32]{2,1,0:T(8,128)} %schur.1) | copy-start | bytes 196612
  47.3 3.9 %copy-start.7 = (s32[2,8,384]{2,1,0:T(8,128)S(1)}, s32[2,8,384]{2,1,0:T(8,128)}, u32[]{:S(2)}) copy-start(s32[2,8,384]{2,1,0:T(8,128)} %constant.11.clone.place) | copy-start | bytes 73732
  47.3 3.9 %collective-permute-start.3 = (f32[17,16,128]{2,1,0:T(8,128)S(1)}, f32[17,16,128]{2,1,0:T(8,128)S(1)}, u32[]{:S(2)}, u32[]{:S(2)}) collective-permute-start(f32[17,16,128]{2,1,0:T(8,128)S(1)} %get-tuple-element.23), channel_id=1, source_target_pairs={{0,3},{1,0},{2,1},{3,2},{4,7},{5,4},{6,5},{7,6},{8,11},{9,8},{10,9... | collective-permute-start | bytes 417800 | tf_op jit(solution)/shard_map/ppermute | solution.py:392
  49.9 19.8 %copy-start.2 = (f32[16,49,49]{2,0,1:T(8,128)S(1)}, f32[16,49,49]{2,0,1:T(8,128)}, u32[]{:S(2)}) copy-start(f32[16,49,49]{2,0,1:T(8,128)} %param.14) | copy-start | bytes 460996
  61.7 16.5 %all-to-all-start.2 = ((f32[32,1,128]{2,1,0:T(1,128)}), f32[32,1,128]{2,1,0:T(1,128)S(1)}, u32[]{:S(2)}, u32[]{:S(2)}) async-start(f32[32,1,128]{2,1,0:T(1,128)} %broadcast_in_dim.9), calls=%async_computation.2 | async-start | bytes 32768 | tf_op jit(solution)/shard_map/all_to_all | solution.py:426
  79.5 19.0 %copy-start.5 = (f32[128,128]{1,0:T(8,128)S(1)}, f32[128,128]{1,0:T(8,128)}, u32[]{:S(2)}) copy-start(f32[128,128]{1,0:T(8,128)} %constant.12.table) | copy-start | bytes 196612

commit v2 on v1

--- a/solution.py
+++ b/solution.py
@@ -23,7 +23,9 @@
 XROWS = ELX + 2 * DEEP
 XCOLS = ELY + 2 * DEEP
 XL = 384
+NEAR = 256
 UNROLL = 8
+CHUNKS = 3
 HIGHEST = lax.Precision.HIGHEST
 F32 = jnp.float32
 
@@ -53,7 +55,7 @@
     return np.stack(out).astype(np.int32)
 
 
-OWN, LOW, HIGH, LEFT, RIGHT, NONE = range(6)
+OWN, LOW, HIGH, SIDE, NONE = range(5)
 BLOCKS = XL // EL
 
 
@@ -67,20 +69,17 @@
     low = middle & (row < DEEP)
     high = middle & (row >= DEEP + ELX) & (row < XROWS)
     source = np.full(XL, NONE)
-    tables = np.zeros((6, XL), np.int64)
+    tables = np.zeros((5, XL), np.int64)
     for number, mask, index in (
         (OWN, own, (row - DEEP) * ELY + col - DEEP),
         (LOW, low, row * ELY + col - DEEP),
         (HIGH, high, (row - DEEP - ELX) * ELY + col - DEEP),
-        (LEFT, left, row * DEEP + col),
-        (RIGHT, right, row * DEEP + col - DEEP - ELY),
+        (SIDE, left | right, np.where(left, row * DEEP + col, 64 + row * DEEP + col - DEEP - ELY)),
     ):
         source[mask] = number
         tables[number][mask] = index[mask]
-    tables[5] = source
-    home = np.arange(EL) // ELY * PITCH + np.arange(EL) % ELY + DEEP
-    tables = tables.reshape(6, BLOCKS, EL).reshape(-1, EL)
-    tables = np.concatenate([tables, (home % EL)[None], (home // EL)[None]])
+    tables[4] = source
+    tables = tables.reshape(5, BLOCKS, EL).reshape(-1, EL)
     place = np.stack([row, col]).repeat(8, 0).reshape(2, 8, XL)
     return np.repeat(tables[:, None], 8, 1).astype(np.int32), source.reshape(-1, EL), place.astype(np.int32)
 
@@ -104,25 +103,51 @@
         out[:, n] = dot(table[...], block).reshape(groups, NZ // groups, EL)
 
 
-def enter_kernel(forcing, coef, cell, planes, order, index, scale, done):
+def copies(source, target, nodes, done):
+    step = -(-nodes // CHUNKS)
+    cuts = [(at, min(step, nodes - at)) for at in range(0, nodes, step)]
+    return [
+        pltpu.make_async_copy(source.at[pl.ds(at, size)], target.at[pl.ds(at, size)], done.at[i])
+        for i, (at, size) in enumerate(cuts)
+    ]
+
+
+def enter_kernel(forcing, coef_far, cell_far, planes, order, index, scale, stored, done, small, coef, cell):
     nodes = forcing.shape[0]
-    copy = pltpu.make_async_copy(forcing, planes.at[pl.ds(0, nodes)], done)
-    copy.start()
+    fetched = [pltpu.make_async_copy(coef_far, coef, small.at[0]), pltpu.make_async_copy(cell_far, cell, small.at[1])]
+    moved = copies(forcing, planes, nodes, done)
+    for copy in fetched + moved:
+        copy.start()
     planes[nodes:PADDED] = jnp.zeros((PADDED - nodes, planes.shape[1], EL), F32)
+    for copy in fetched:
+        copy.wait()
     lane = lax.broadcasted_iota(jnp.int32, (EL, EL), 1)
     elem = lax.broadcasted_iota(jnp.int32, (EL, EL), 0)
     cells = jnp.transpose(jnp.broadcast_to(cell[...], (EL, EL)))
     found = jnp.sum(jnp.where(cells == lane, elem, 0), axis=0, keepdims=True)
     order[...] = jnp.broadcast_to(found, (8, EL))
     index[...] = jnp.broadcast_to(cell[...], (8, EL))
+    stored[...] = jnp.broadcast_to(coef[...], (8, EL))
     scale[...] = pick(jnp.broadcast_to(coef[...], (8, EL)), found)
-    copy.wait()
+    for copy in moved:
+        copy.wait()
 
 
 def leave_kernel(planes, velocity, done):
-    copy = pltpu.make_async_copy(planes.at[pl.ds(0, velocity.shape[0])], velocity, done)
-    copy.start()
-    copy.wait()
+    moved = copies(planes, velocity, velocity.shape[0], done)
+    for copy in moved:
+        copy.start()
+    for copy in moved:
+        copy.wait()
+
+
+def flipped(tile):
+    back = (8 - lax.broadcasted_iota(jnp.int32, tile.shape, 0)) % 8
+    return jnp.take_along_axis(tile, back, axis=0, mode="promise_in_bounds")
+
+
+def both_ascending(values):
+    return jnp.concatenate([values[0:16], flipped(values[16:24]), flipped(values[24:32])], 0)
 
 
 def condense_kernel(spectral, order, scale, couple, condensed, down, up):
@@ -139,7 +164,7 @@
 
     def mode(m, _):
         fields = pick(spectral[pl.ds(m, PADDED, stride=MODES), :], order[0:1])
-        value = fields[0:NB] - dot(couple[m], fields[NB:NODES])
+        value = both_ascending(fields[0:NB] - dot(couple[m], fields[NB:NODES]))
         condensed[m] = value
         down[m], up[m] = messages(value[0:16], value[16:32])
         return 0
@@ -147,11 +172,11 @@
     lax.fori_loop(0, MODES, mode, 0, unroll=UNROLL)
 
 
-def interior_kernel(spectral, order, scale, inner, base):
-    inverse = 1.0 / scale[0:1]
+def interior_kernel(spectral, stored, inner, base):
+    inverse = 1.0 / stored[0:1]
 
     def mode(m, _):
-        within = pick(spectral[pl.ds(NB * MODES + m, PADDED - NB, stride=MODES), :], order[0:1])[0:NI]
+        within = spectral[pl.ds(NB * MODES + m, PADDED - NB, stride=MODES), :][0:NI]
         base[m, 0:NI] = dot(inner[pl.ds(m, NI, stride=MODES), :], within) * inverse
         return 0
 
@@ -185,7 +210,7 @@
 def spread(tile, sources, table):
     pieces = []
     for j in range(BLOCKS):
-        source = table[5 * BLOCKS + j]
+        source = table[4 * BLOCKS + j]
         piece = tile[j]
         for number, values, half in sources:
             if (EXT_SOURCE[j] == number).any():
@@ -195,7 +220,7 @@
     return pieces
 
 
-def middle_kernel(condensed, scale, low, high, table, block):
+def middle_kernel(condensed, scale, low, high, schur, table, block, matrix):
     blank = [jnp.zeros((8, EL), F32)] * BLOCKS
 
     def put(m, tile, pieces):
@@ -204,7 +229,12 @@
 
     put(MODES, 0, spread(blank, ((OWN, scale[...], 0), (LOW, low[MODES, 0:8], 0), (HIGH, high[MODES, 0:8], 0)), table))
 
+    lane = lax.broadcasted_iota(jnp.int32, (NB, NB), 1)
+    across = jnp.where((lane >= 16) & (lane % 8 > 0), lane // 8 * 8 + 8 - lane % 8, lane)
+
     def mode(m, _):
+        rows = both_ascending(schur[m])
+        matrix[m] = jnp.take_along_axis(rows, across, axis=1, mode="promise_in_bounds")
         for tile in range(4):
             half, at = tile // 2, tile % 2 * 8
             sources = (
@@ -218,12 +248,22 @@
     lax.fori_loop(0, MODES, mode, 0, unroll=UNROLL)
 
 
-def krylov_kernel(block, coef_grid, left, right, schur, table, place, basis, sums, keep_ref, weight_ref, parts, state):
-    def sides(m, tile):
-        half, at = tile // 2, tile % 2 * 8
-        held = [block[m, 8 * tile : 8 * tile + 8, EL * j : EL * j + EL] for j in range(BLOCKS)]
-        sources = ((LEFT, left[m, at : at + 8], half), (RIGHT, right[m, at : at + 8], half))
-        return jnp.concatenate(spread(held, sources, table), 1)
+def krylov_kernel(
+    block, coef_grid, left, right, schur, table, place, basis, sums, keep_ref, weight_ref, mine_ref, parts, state, applied, pairs, spreadout
+):
+    first = lax.broadcasted_iota(jnp.int32, (8, EL), 1) < 64
+
+    def pair_up(m):
+        for at in (0, 1):
+            low, high = left[m, 8 * at : 8 * at + 8], right[m, 8 * at : 8 * at + 8]
+            base = m * NB + 8 * at
+            pairs[pl.ds(base, 8), :] = jnp.where(first, low, pltpu.roll(high, 64, 1))
+            pairs[pl.ds(base + 16, 8), :] = jnp.where(first, pltpu.roll(low, 64, 1), high)
+
+    for m in range(MODES + 1):
+        pair_up(m)
+    turn = jnp.concatenate([jnp.where(table[BLOCKS * SIDE + j, 0:1] == lax.broadcasted_iota(jnp.int32, (EL, EL), 0), 1.0, 0.0) * jnp.where(table[4 * BLOCKS + j, 0:1] == SIDE, 1.0, 0.0) for j in range(BLOCKS)], 1).astype(F32)
+    spreadout[...] = dot(pairs[...], turn)
 
     row, col = place[0], place[1]
     grid_row = row - DEEP + lax.axis_index("ex") * ELX
@@ -232,79 +272,62 @@
     inside = (grid_row >= 0) & (grid_row <= last_row) & (grid_col >= 0) & (grid_col <= last_col)
     inside = inside & (row < XROWS) & (col < XCOLS)
     own = (row >= DEEP) & (row < DEEP + ELX) & (col >= DEEP) & (col < DEEP + ELY)
+    mine_ref[...] = jnp.where(own, 1.0, 0.0)[:, 0:NEAR].astype(F32)
     corner = lax.broadcasted_iota(jnp.int32, (8, XL), 0) == 0
     low_row, high_row, low_col, high_col = grid_row == 0, grid_row == last_row, grid_col == 0, grid_col == last_col
     for tile, (edge, other) in enumerate(((low_col, low_row), (high_row, low_col), (high_col, high_row), (low_row, high_col))):
         keep = jnp.where(inside & ~(edge | (corner & other)), 1.0, 0.0).astype(F32)
         keep_ref[8 * tile : 8 * tile + 8] = keep
         weight_ref[8 * tile : 8 * tile + 8] = jnp.where(own, keep * jnp.where(corner, 0.25, 0.5), 0.0).astype(F32)
-    scale = jnp.where(inside, sides(MODES, 0), 0.0)[0:1]
+    scale = jnp.where(inside[0:1], block[MODES, 0:1] + spreadout[MODES * NB : MODES * NB + 1], 0.0)
 
     sub = lax.broadcasted_iota(jnp.int32, (8, XL), 0)
     zero = sub == 0
-    back = (8 - sub) % 8
-
-    def rev(tile):
-        return jnp.take_along_axis(tile, back, axis=0, mode="promise_in_bounds")
 
     def assemble(values):
-        t = [values[8 * i : 8 * i + 8] for i in range(4)]
+        t = values if isinstance(values, list) else [values[8 * i : 8 * i + 8] for i in range(4)]
         for axis, (a, b, c, d) in ((PITCH, (1, 2, 3, 0)), (1, (2, 3, 0, 1))):
             ahead, behind = axis, XL - axis
             if axis == PITCH:
-                prev3 = pltpu.roll(jnp.where(zero, t[2], rev(t[1])), ahead, 1)
+                prev3 = pltpu.roll(jnp.where(zero, t[2], t[1]), ahead, 1)
                 prev0 = pltpu.roll(jnp.where(zero, t[1], 0.0), ahead, 1)
-                next1 = pltpu.roll(jnp.where(zero, t[0], rev(t[3])), behind, 1)
+                next1 = pltpu.roll(jnp.where(zero, t[0], t[3]), behind, 1)
                 next2 = pltpu.roll(jnp.where(zero, t[3], 0.0), behind, 1)
                 t = [t[0] + prev0, t[1] + next1, t[2] + next2, t[3] + prev3]
             else:
-                prev0 = pltpu.roll(jnp.where(zero, t[3], rev(t[2])), ahead, 1)
+                prev0 = pltpu.roll(jnp.where(zero, t[3], t[2]), ahead, 1)
                 prev1 = pltpu.roll(jnp.where(zero, t[2], 0.0), ahead, 1)
-                next2 = pltpu.roll(jnp.where(zero, t[1], rev(t[0])), behind, 1)
+                next2 = pltpu.roll(jnp.where(zero, t[1], t[0]), behind, 1)
                 next3 = pltpu.roll(jnp.where(zero, t[0], 0.0), behind, 1)
                 t = [t[0] + prev0, t[1] + prev1, t[2] + next2, t[3] + next3]
         return keep_ref[...] * jnp.concatenate(t, 0)
 
     eye = lax.broadcasted_iota(jnp.int32, (NB, NB), 0) == lax.broadcasted_iota(jnp.int32, (NB, NB), 1)
-    home, home_at = table[6 * BLOCKS], table[6 * BLOCKS + 1]
-    own_scale = coef_grid[0:1]
-
-    def at_home(ref):
-        tiles = []
-        for tile in range(4):
-            one, two = (pick(ref[8 * tile : 8 * tile + 8, EL * j : EL * j + EL], home) for j in (0, 1))
-            tiles.append(jnp.where(home_at == 0, one, two))
-        return jnp.concatenate(tiles, 0)
-
-    weight_ref[:, 0:EL] = at_home(weight_ref)
-
     def gather_mode(m):
-        state[0, m] = assemble(jnp.concatenate([sides(m, tile) for tile in range(4)], 0))
-
-    def apply_mode(i):
-        def run(m):
-            state[3, m] = scale * dot(schur[m], state[i, m])
-
-        return run
+        state[0, m] = assemble(block[m] + spreadout[pl.ds(pl.multiple_of(m * NB, NB), NB), :])
 
     def extend_mode(i):
         def run(m):
             trace = jnp.sum(jnp.sum(jnp.where(eye, schur[m], 0.0), axis=0, keepdims=True), axis=1, keepdims=True)
-            state[i + 1, m] = assemble(state[3, m]) * ((0.5 * NB) / trace) - state[i, m]
+            images = scale * dot(schur[m], state[i, m])
+            applied[i, m] = images[:, 0:NEAR]
+            state[i + 1, m] = assemble(images) * ((0.5 * NB) / trace) - state[i, m]
 
         return run
 
     def sum_mode(m):
-        v = [at_home(state.at[i, m]) for i in range(3)]
-        w = [own_scale * dot(schur[m], v[i]) for i in range(3)]
-        weight = weight_ref[:, 0:EL]
-        weighted = v[0] * weight
+        v = [state[i, m, :, 0:NEAR] for i in range(3)]
+        w = [applied[0, m], applied[1, m], scale[:, 0:NEAR] * dot(schur[m], v[2])]
+        weight, mine = weight_ref[:, 0:NEAR], mine_ref[0:1]
+        weighted = v[1] * weight
+        own = [value * mine for value in v]
         k = 0
         for first, second in (
-            (v[0], weighted), (v[1], weighted), (v[1], v[1] * weight),
-            (v[0], w[0]), (v[1], w[0]), (v[1], w[1]), (v[2], w[1]), (v[2], w[2]),
+            (v[0], v[0] * weight), (v[0], weighted), (v[1], weighted),
+            (own[0], w[0]), (own[1], w[0]), (own[1], w[1]), (own[2], w[1]), (own[2], w[2]),
         ):
-            parts[pl.ds(MODES * k + m, 1), :] = jnp.sum(first * second, axis=0, keepdims=True)
+            whole = jnp.sum(first * second, axis=0, keepdims=True)
+            parts[pl.ds(MODES * k + m, 1), :] = whole[:, 0:EL] + whole[:, EL:NEAR]
             k += 1
         for i in range(3):
             basis[i, m] = v[i]
@@ -318,12 +341,12 @@
 
     every(gather_mode)
     for i in range(2):
-        every(apply_mode(i))
         every(extend_mode(i))
     every(sum_mode)
     ones = jnp.ones((8, EL), F32)
     total = lax.dot_general(ones, parts[...], (((1,), (1,)), ((), ())), precision=HIGHEST, preferred_element_type=F32)
-    sums[...] = total[0:1]
+    for at in range(0, sums.shape[0], 8):
+        sums[at : at + 8] = total
 
 
 def finish_kernel(gathered, basis, base, couple, cell, out, coefs):
@@ -345,16 +368,18 @@
     c1 = jnp.where(ok1, y1 / d1, 0.0) - l12 * c2
     c0 = b0 / h0 - l1 * c1 - l2 * c2
     coefs[0], coefs[1], coefs[2] = c0, c1, c2
-    index = cell[0:1]
+    place = cell[...] // ELY * PITCH + cell[...] % ELY + DEEP
+    nearer = jnp.broadcast_to(place[0:1] < EL, (NB, EL))
+    index = place[0:1] % EL
 
     for m in range(MODES):
         c = [coefs[i, 0:1, m : m + 1] for i in range(3)]
         x = c[0] * basis[0, m] + c[1] * basis[1, m] + c[2] * basis[2, m]
+        x = both_ascending(jnp.where(nearer, pick(x[:, 0:EL], index), pick(x[:, EL:NEAR], index)))
         within = base[m, 0:NI] - lax.dot_general(
             couple[m], x, (((0,), (0,)), ((), ())), precision=HIGHEST, preferred_element_type=F32
         )
-        fields = jnp.concatenate([x, within, jnp.zeros((PADDED - NODES, EL), F32)], 0)
-        out[pl.ds(m, PADDED, stride=MODES), :] = pick(fields, index)
+        out[pl.ds(m, PADDED, stride=MODES), :] = jnp.concatenate([x, within, jnp.zeros((PADDED - NODES, EL), F32)], 0)
 
 
 def call(kernel, shapes=(), scratch=(), far=0, far_out=None):
@@ -374,7 +399,7 @@
             scratch_shapes=list(scratch),
             compiler_params=pltpu.CompilerParams(vmem_limit_bytes=16 << 20),
             name=kernel.__name__,
-        )(*operands[:far], *near)
+        )(*(pltpu.with_memory_space_constraint(o, pltpu.HBM) for o in operands[:far]), *near)
 
     return run
 
@@ -394,14 +419,22 @@
 
 def on_device(forcing, element_coef, schur, couple, inner_inv, element_cell):
     parts = lax.axis_size("fourier")
+    devices = lax.axis_size("ex") * lax.axis_size("ey")
     group = PADDED // parts
     table = jnp.asarray(real_transform())
     exchanged = (parts, group, MODES, EL)
     lanes = (8, EL)
     ints = pltpu.VMEM(lanes, jnp.int32)
 
-    planes, order, index, scale = call(
-        enter_kernel, [(PADDED, MODES, EL), ints, ints, lanes], [pltpu.SemaphoreType.DMA], far=1
+    planes, order, index, scale, stored = call(
+        enter_kernel, [(PADDED, MODES, EL), ints, ints, lanes, lanes],
+        [
+            pltpu.SemaphoreType.DMA((CHUNKS,)),
+            pltpu.SemaphoreType.DMA((2,)),
+            pltpu.VMEM((1, EL), F32),
+            pltpu.VMEM((1, EL), jnp.int32),
+        ],
+        far=3,
     )(jnp.transpose(forcing, (1, 0, 2)), element_coef.reshape(1, EL), element_cell.reshape(1, EL))
     planes = swap(planes).reshape(exchanged)
     spectral = swap(call(transform_kernel, exchanged)(table, planes).reshape(PADDED, MODES, EL))
@@ -411,27 +444,36 @@
     condensed, down, up = call(condense_kernel, [(MODES, NB, EL), message, message])(spectral, order, scale, couple)
     low, high = neighbours(down, up, "ex")
     base = call(interior_kernel, (MODES, 56, EL))(
-        spectral, order, scale, jnp.transpose(inner_inv, (1, 0, 2)).reshape(NI * MODES, NI)
+        spectral, stored, jnp.transpose(inner_inv, (1, 0, 2)).reshape(NI * MODES, NI)
     )
+    low, high, base = lax.optimization_barrier((low, high, base))
     left, right = call(columns_kernel, [message, message])(condensed, scale, low, high, jnp.asarray(COL_TABLE))
     left, right = neighbours(left, right, "ey")
     extended = jnp.asarray(EXT_TABLE)
-    block = call(middle_kernel, (MODES + 1, NB, XL))(condensed, scale, low, high, extended)
+    block, matrix = call(middle_kernel, [(MODES + 1, NB, XL), (MODES, NB, NB)])(
+        condensed, scale, low, high, schur, extended
+    )
     basis, sums = call(
         krylov_kernel,
-        [(3, MODES, NB, EL), (1, EL)],
-        [pltpu.VMEM((NB, XL), F32), pltpu.VMEM((NB, XL), F32), pltpu.VMEM((EL, EL), F32), pltpu.VMEM((4, MODES, NB, XL), F32)],
-    )(block, scale, left, right, schur, extended, jnp.asarray(EXT_PLACE))
-    copies = lax.axis_size("ex") * lax.axis_size("ey")
-    gathered = lax.all_to_all(
-        jnp.broadcast_to(sums[None], (copies, 1, EL)), ("ex", "ey"), split_axis=0, concat_axis=0, tiled=True
-    )
+        [(3, MODES, NB, NEAR), (devices, EL)],
+        [
+            pltpu.VMEM((NB, XL), F32),
+            pltpu.VMEM((NB, XL), F32),
+            pltpu.VMEM((8, NEAR), F32),
+            pltpu.VMEM((EL, EL), F32),
+            pltpu.VMEM((3, MODES, NB, XL), F32),
+            pltpu.VMEM((2, MODES, NB, NEAR), F32),
+            pltpu.VMEM(((MODES + 1) * NB, EL), F32),
+            pltpu.VMEM(((MODES + 1) * NB, XL), F32),
+        ],
+    )(block, scale, left, right, matrix, extended, jnp.asarray(EXT_PLACE))
+    gathered = lax.all_to_all(sums.reshape(devices, 1, EL), ("ex", "ey"), split_axis=0, concat_axis=0, tiled=True)
     modal = call(finish_kernel, (PADDED * MODES, EL), [pltpu.VMEM((3, 8, EL), F32)])(
         gathered, basis, base, couple, index
     )
     modal = swap(modal.reshape(PADDED, MODES, EL)).reshape(exchanged)
     velocity = swap(call(transform_kernel, exchanged)(table.T, modal).reshape(PADDED, MODES, EL))
-    velocity = call(leave_kernel, far_out=(NODES, MODES, EL), scratch=[pltpu.SemaphoreType.DMA])(velocity)
+    velocity = call(leave_kernel, far_out=(NODES, MODES, EL), scratch=[pltpu.SemaphoreType.DMA((CHUNKS,))])(velocity)
     return jnp.transpose(velocity, (1, 0, 2))
 
 

time: 115 us -> 110 us (0.957)
  blocking collectives: 66.4 us -> 82.5 us
  waiting for transfers between devices: 11.5 us -> 3.11 us
  starting transfers between devices: 16.6 us -> 8.6 us
  local copies, waits for them, and re-layouts: 2.45 us -> 0.04 us
  Pallas kernels: 17.9 us -> 15.5 us
    all_to_all x0 -> x1, blocking collectives: none -> 16.4 us  [on_device(): lax.all_to_all(sums.reshape(devices, 1, EL), ('ex', 'ey'), split_axis=0,...]
    all_to_all x1 -> x0, starting transfers between devices: 7.99 us -> none  [on_device(): lax.all_to_all(jnp.broadcast_to(sums[None], (copies, 1, EL)), ('ex', 'ey'...]
    all_to_all x1 -> x0, waiting for transfers between devices: 7.31 us -> none  [on_device(): lax.all_to_all(jnp.broadcast_to(sums[None], (copies, 1, EL)), ('ex', 'ey'...]
    pallas_call x10, Pallas kernels: 17.9 us -> 15.5 us  [run(): pl.pallas_call(kernel, out_shape=outs if many else outs[0], in_specs=[awa...]
    unnamed x22 -> x16, local copies, waits for them, and re-layouts: 1.8 us -> 0.04 us
  transfers between devices with their start and end apart: 5 -> 4, of which waited for: 3 -> 2; matrix products, arithmetic and copies ran while one was open for 0% -> 0% of each run, Pallas kernels for 2% -> 2%
where the time goes in v2:
time: 110 us
  blocking collectives  82.5 us (75%)
  Pallas kernels  15.5 us (14%)
  starting transfers between devices  8.6 us (8%)
  waiting for transfers between devices  3.11 us (3%)
    all_to_all x4, blocking collectives, swap(): lax.all_to_all(array, 'fourier', split_axis=0, concat_axis=0, tiled=True)  66.2 us
    all_to_all x1, blocking collectives, on_device(): lax.all_to_all(sums.reshape(devices, 1, EL), ('ex', 'ey'), split_axis=0,...  16.4 us
    pallas_call x10, Pallas kernels, run(): pl.pallas_call(kernel, out_shape=outs if many else outs[0], in_specs=[awa...  15.5 us
    ppermute x2, starting transfers between devices, neighbours(): lax.ppermute(to_low, axis, ring(axis, -1))  5.56 us
    ppermute x2, waiting for transfers between devices, neighbours(): lax.ppermute(to_high, axis, ring(axis, 1))  3.08 us
    ppermute x2, starting transfers between devices, neighbours(): lax.ppermute(to_high, axis, ring(axis, 1))  3.05 us
  transfers between devices with their start and end apart: 4, of which 2 were waited for; matrix products, arithmetic and copies ran while one was open for 0% of the time, Pallas kernels for 2%

profile of v2, /device:TPU:1, one launch (start us, length us, event | category | flops | bytes accessed | tf_op | source)
XLA Modules:
  0.0 109.9 jit_solution(8666986056170880523)
XLA Ops:
  0.0 0.0 copy-start.5
  0.0 1.2 %enter_kernel.1 = (f32[88,16,128]{2,1,0:T(8,128)S(1)}, s32[8,128]{1,0:T(8,128)S(1)}, s32[8,128]{1,0:T(8,128)S(1)}, f32[8,128]{1,0:T(8,128)S(1)}, f32[8,128]{1,0:T(8,128)S(1)}) custom-call(f32[81,16,128]{2,1,0:T(8,128)} %bitcast.23, f32[1,128]{1,0:T(1,128)} %bitcast.24, s32[1,128]{1,0:T(1,128)} %bitcast.25), custom_call_target="tpu_custom_call" | custom-call | tf_op jit(solution)/shard_map/enter_kernel/pallas_call | solution.py:394
  1.3 17.2 %all_to_all.25 = f32[88,16,128]{2,1,0:T(8,128)S(1)} all-to-all(f32[88,16,128]{2,1,0:T(8,128)S(1)} %get-tuple-element.22), channel_id=1, replica_groups=mesh['fourier'=8,'ex'=8,'ey'=4] {'fourier'}, dimensions={0} | all-to-all | bytes 1441792 | tf_op jit(solution)/shard_map/all_to_all | solution.py:408
  18.5 0.0 copy-start
  18.5 0.0 copy-done.5
  18.5 0.7 transform_kernel.2
  19.2 0.0 copy-start.1
  19.3 15.1 %all_to_all.26 = f32[88,16,128]{2,1,0:T(8,128)S(1)} all-to-all(f32[88,16,128]{2,1,0:T(8,128)S(1)} %bitcast.17), channel_id=1, replica_groups=mesh['fourier'=8,'ex'=8,'ey'=4] {'fourier'}, dimensions={0} | all-to-all | bytes 1441792 | tf_op jit(solution)/shard_map/all_to_all | solution.py:408
  34.3 0.0 copy-start.7
  34.3 0.0 copy-start.2
  34.3 0.0 copy-start.3
  34.3 0.0 copy-done
  34.3 1.0 condense_kernel.1
  35.4 0.0 copy-start.6
  35.4 1.7 %collective-permute-start = (f32[17,16,128]{2,1,0:T(8,128)S(1)}, f32[17,16,128]{2,1,0:T(8,128)S(1)}, u32[]{:S(2)}, u32[]{:S(2)}) collective-permute-start(f32[17,16,128]{2,1,0:T(8,128)S(1)} %get-tuple-element.26), channel_id=1, source_target_pairs={{0,4},{4,8},{8,12},{12,16},{16,20},{20,24},{24,28},{28,0},{1,5},{5... | collective-permute-start | bytes 417800 | tf_op jit(solution)/shard_map/ppermute | solution.py:417
  37.1 4.0 %collective-permute-start.1 = (f32[17,16,128]{2,1,0:T(8,128)S(1)}, f32[17,16,128]{2,1,0:T(8,128)S(1)}, u32[]{:S(2)}, u32[]{:S(2)}) collective-permute-start(f32[17,16,128]{2,1,0:T(8,128)S(1)} %get-tuple-element.27), channel_id=1, source_target_pairs={{0,28},{4,0},{8,4},{12,8},{16,12},{20,16},{24,20},{28,24},{1,29},{... | collective-permute-start | bytes 417800 | tf_op jit(solution)/shard_map/ppermute | solution.py:417
  41.1 0.0 copy-done.1
  41.1 1.0 interior_kernel.1.base
  42.1 2.0 %collective-permute-done.low = f32[17,16,128]{2,1,0:T(8,128)S(1)} collective-permute-done((f32[17,16,128]{2,1,0:T(8,128)S(1)}, f32[17,16,128]{2,1,0:T(8,128)S(1)}, u32[]{:S(2)}, u32[]{:S(2)}) %collective-permute-start) | collective-permute-done | bytes 139296 | tf_op jit(solution)/shard_map/ppermute | solution.py:417
  44.1 0.0 collective-permute-done.1.high
  44.1 0.0 copy-done.7
  44.1 0.8 columns_kernel.1
  44.9 1.4 %collective-permute-start.2 = (f32[17,16,128]{2,1,0:T(8,128)S(1)}, f32[17,16,128]{2,1,0:T(8,128)S(1)}, u32[]{:S(2)}, u32[]{:S(2)}) collective-permute-start(f32[17,16,128]{2,1,0:T(8,128)S(1)} %get-tuple-element.32), channel_id=1, source_target_pairs={{0,1},{1,2},{2,3},{3,0},{4,5},{5,6},{6,7},{7,4},{8,9},{9,10},{10,1... | collective-permute-start | bytes 417800 | tf_op jit(solution)/shard_map/ppermute | solution.py:417
  46.2 1.5 %collective-permute-start.3 = (f32[17,16,128]{2,1,0:T(8,128)S(1)}, f32[17,16,128]{2,1,0:T(8,128)S(1)}, u32[]{:S(2)}, u32[]{:S(2)}) collective-permute-start(f32[17,16,128]{2,1,0:T(8,128)S(1)} %get-tuple-element.33), channel_id=1, source_target_pairs={{0,3},{1,0},{2,1},{3,2},{4,7},{5,4},{6,5},{7,6},{8,11},{9,8},{10,9... | collective-permute-start | bytes 417800 | tf_op jit(solution)/shard_map/ppermute | solution.py:417
  47.8 0.0 copy-done.2
  47.8 0.0 copy-done.3
  47.8 1.2 %middle_kernel.1 = (f32[17,32,384]{2,1,0:T(8,128)S(1)}, f32[16,32,32]{2,1,0:T(8,128)S(1)}) custom-call(f32[16,32,128]{2,1,0:T(8,128)S(1)} %get-tuple-element.25.condensed, f32[8,128]{1,0:T(8,128)S(1)} %get-tuple-element.24.scale.coef_grid, f32[17,16,128]{2,1,0:T(8,128)S(1)} %collective-permute-done.low, f32[17,16,128]{2,1,0:T(8,128)S(1)} %collective-permute-done.1.high, ...), custom_call_target="tpu_custom_call" | custom-call | tf_op jit(solution)/shard_map/middle_kernel/pallas_call | solution.py:394
  49.0 1.1 %collective-permute-done.2.left = f32[17,16,128]{2,1,0:T(8,128)S(1)} collective-permute-done((f32[17,16,128]{2,1,0:T(8,128)S(1)}, f32[17,16,128]{2,1,0:T(8,128)S(1)}, u32[]{:S(2)}, u32[]{:S(2)}) %collective-permute-start.2) | collective-permute-done | bytes 139296 | tf_op jit(solution)/shard_map/ppermute | solution.py:417
  50.1 0.0 collective-permute-done.3.right
  50.1 0.0 copy-done.6
  50.1 6.0 %krylov_kernel.1 = (f32[3,16,32,256]{3,2,1,0:T(8,128)S(1)}, f32[32,128]{1,0:T(8,128)S(1)}) custom-call(f32[17,32,384]{2,1,0:T(8,128)S(1)} %get-tuple-element.31.block, f32[8,128]{1,0:T(8,128)S(1)} %get-tuple-element.24.scale.coef_grid, f32[17,16,128]{2,1,0:T(8,128)S(1)} %collective-permute-done.2.left, f32[17,16,128]{2,1,0:T(8,128)S(1)} %collective-permute-done.3.right, ...), custom_call_target="tpu_custom_call" | custom-call | tf_op jit(solution)/shard_map/krylov_kernel/pallas_call | solution.py:394
  56.2 16.4 %all_to_all.27.gathered = f32[32,1,128]{2,1,0:T(1,128)S(1)} all-to-all(f32[32,1,128]{2,1,0:T(1,128)S(1)} %bitcast.22), channel_id=1, replica_groups=mesh['fourier'=8,'ex'=8,'ey'=4] {'ex','ey'}, dimensions={0} | all-to-all | bytes 32768 | tf_op jit(solution)/shard_map/all_to_all | solution.py:470
  72.6 0.0 copy-start.4
  72.6 1.9 %finish_kernel.1 = f32[1408,128]{1,0:T(8,128)S(1)} custom-call(f32[32,1,128]{2,1,0:T(1,128)S(1)} %all_to_all.27.gathered, f32[3,16,32,256]{3,2,1,0:T(8,128)S(1)} %get-tuple-element.36.basis, f32[16,56,128]{2,1,0:T(8,128)S(1)} %interior_kernel.1.base, f32[16,32,49]{2,1,0:T(8,128)S(1)} %copy-done, s32[8,128]{1,0:T(8,128)S(1)} %get-tuple-element.38.cell), custom_call_target="tpu_custom_call" | custom-call | tf_op jit(solution)/shard_map/finish_kernel/pallas_call | solution.py:394
  74.5 18.9 %all_to_all.28 = f32[88,16,128]{2,1,0:T(8,128)S(1)} all-to-all(f32[88,16,128]{2,1,0:T(8,128)S(1)} %bitcast.20), channel_id=1, replica_groups=mesh['fourier'=8,'ex'=8,'ey'=4] {'fourier'}, dimensions={0} | all-to-all | bytes 1441792 | tf_op jit(solution)/shard_map/all_to_all | solution.py:408
  93.4 0.0 copy-done.4
  93.4 0.7 transform_kernel.3
  94.1 14.9 %all_to_all.29.planes = f32[88,16,128]{2,1,0:T(8,128)S(1)} all-to-all(f32[88,16,128]{2,1,0:T(8,128)S(1)} %bitcast.19), channel_id=1, replica_groups=mesh['fourier'=8,'ex'=8,'ey'=4] {'fourier'}, dimensions={0} | all-to-all | bytes 1441792 | tf_op jit(solution)/shard_map/all_to_all | solution.py:408
  109.1 0.9 leave_kernel.1
Async XLA Ops:
  0.0 18.5 %copy-start.5 = (f32[128,128]{1,0:T(8,128)S(1)}, f32[128,128]{1,0:T(8,128)}, u32[]{:S(2)}) copy-start(f32[128,128]{1,0:T(8,128)} %constant.8.clone.table) | copy-start | bytes 196612
  18.5 15.8 %copy-start = (f32[16,32,49]{2,1,0:T(8,128)S(1)}, f32[16,32,49]{2,1,0:T(8,128)}, u32[]{:S(2)}) copy-start(f32[16,32,49]{2,1,0:T(8,128)} %couple.3) | copy-start | bytes 301060
  19.2 21.9 %copy-start.1 = (f32[16,49,49]{2,0,1:T(8,128)S(1)}, f32[16,49,49]{2,0,1:T(8,128)}, u32[]{:S(2)}) copy-start(f32[16,49,49]{2,0,1:T(8,128)} %param.14) | copy-start | bytes 460996
  34.3 9.8 %copy-start.7 = (s32[8,128]{1,0:T(8,128)S(1)}, s32[8,128]{1,0:T(8,128)}, u32[]{:S(2)}) copy-start(s32[8,128]{1,0:T(8,128)} %constant.9.clone.table) | copy-start | bytes 12292
  34.3 13.4 %copy-start.2 = (f32[16,32,32]{2,1,0:T(8,128)S(1)}, f32[16,32,32]{2,1,0:T(8,128)}, u32[]{:S(2)}) copy-start(f32[16,32,32]{2,1,0:T(8,128)} %schur.1) | copy-start | bytes 196612
  34.3 13.4 %copy-start.3 = (s32[15,8,128]{2,1,0:T(8,128)S(1)}, s32[15,8,128]{2,1,0:T(8,128)}, u32[]{:S(2)}) copy-start(s32[15,8,128]{2,1,0:T(8,128)} %constant.10.clone.table) | copy-start | bytes 184324
  35.4 14.8 %copy-start.6 = (s32[2,8,384]{2,1,0:T(8,128)S(1)}, s32[2,8,384]{2,1,0:T(8,128)}, u32[]{:S(2)}) copy-start(s32[2,8,384]{2,1,0:T(8,128)} %constant.11.clone.place) | copy-start | bytes 73732
  35.4 8.7 %collective-permute-start = (f32[17,16,128]{2,1,0:T(8,128)S(1)}, f32[17,16,128]{2,1,0:T(8,128)S(1)}, u32[]{:S(2)}, u32[]{:S(2)}) collective-permute-start(f32[17,16,128]{2,1,0:T(8,128)S(1)} %get-tuple-element.26), channel_id=1, source_target_pairs={{0,4},{4,8},{8,12},{12,16},{16,20},{20,24},{24,28},{28,0},{1,5},{5... | collective-permute-start | bytes 417800 | tf_op jit(solution)/shard_map/ppermute | solution.py:417
  37.1 7.0 %collective-permute-start.1 = (f32[17,16,128]{2,1,0:T(8,128)S(1)}, f32[17,16,128]{2,1,0:T(8,128)S(1)}, u32[]{:S(2)}, u32[]{:S(2)}) collective-permute-start(f32[17,16,128]{2,1,0:T(8,128)S(1)} %get-tuple-element.27), channel_id=1, source_target_pairs={{0,28},{4,0},{8,4},{12,8},{16,12},{20,16},{24,20},{28,24},{1,29},{... | collective-permute-start | bytes 417800 | tf_op jit(solution)/shard_map/ppermute | solution.py:417
  44.9 5.3 %collective-permute-start.2 = (f32[17,16,128]{2,1,0:T(8,128)S(1)}, f32[17,16,128]{2,1,0:T(8,128)S(1)}, u32[]{:S(2)}, u32[]{:S(2)}) collective-permute-start(f32[17,16,128]{2,1,0:T(8,128)S(1)} %get-tuple-element.32), channel_id=1, source_target_pairs={{0,1},{1,2},{2,3},{3,0},{4,5},{5,6},{6,7},{7,4},{8,9},{9,10},{10,1... | collective-permute-start | bytes 417800 | tf_op jit(solution)/shard_map/ppermute | solution.py:417
  46.2 3.9 %collective-permute-start.3 = (f32[17,16,128]{2,1,0:T(8,128)S(1)}, f32[17,16,128]{2,1,0:T(8,128)S(1)}, u32[]{:S(2)}, u32[]{:S(2)}) collective-permute-start(f32[17,16,128]{2,1,0:T(8,128)S(1)} %get-tuple-element.33), channel_id=1, source_target_pairs={{0,3},{1,0},{2,1},{3,2},{4,7},{5,4},{6,5},{7,6},{8,11},{9,8},{10,9... | collective-permute-start | bytes 417800 | tf_op jit(solution)/shard_map/ppermute | solution.py:417
  72.6 20.8 %copy-start.4 = (f32[128,128]{1,0:T(8,128)S(1)}, f32[128,128]{1,0:T(8,128)}, u32[]{:S(2)}) copy-start(f32[128,128]{1,0:T(8,128)} %constant.12.table) | copy-start | bytes 196612

commit v3 on v2

v3 whole, which is shorter than its diff:
```python
import math

import jax
import jax.numpy as jnp
import numpy as np
from jax import lax
from jax.experimental import pallas as pl
from jax.experimental.pallas import tpu as pltpu
from jax.sharding import PartitionSpec as P

P_SIZE = 8
NZ = 128
ELX = 8
ELY = 16
NODES = 81
NB = 32
NI = 49
EL = ELX * ELY
PADDED = 88
MODES = 16
DEEP = 2
XROWS = ELX + 2 * DEEP
XCOLS = ELY + 2 * DEEP
PITCH = XCOLS
XL = 256
SLOT = DEEP * ELY
UNROLL = 8
CHUNKS = 3
HIGHEST = lax.Precision.HIGHEST
F32 = jnp.float32


def real_transform():
    k = np.arange(NZ)[:, None]
    z = np.arange(NZ)[None, :]
    angle = 2.0 * math.pi * (((k + 1) // 2 * z) % NZ) / NZ
    w = np.where(k % 2 == 1, np.cos(angle), np.sin(angle)) * math.sqrt(2.0 / NZ)
    w[0] = 1.0 / math.sqrt(NZ)
    w[NZ - 1] = np.cos(math.pi * np.arange(NZ)) / math.sqrt(NZ)
    return w.astype(np.float32)


def lane_tables():
    lane = np.arange(XL)
    row, col = lane // PITCH, lane % PITCH
    valid = row < XROWS
    middle = valid & (col >= DEEP) & (col < DEEP + ELY)
    right = col >= DEEP + ELY
    spread = np.where(middle, row * ELY + col - DEEP, -1)
    turn = np.where(right, SLOT + row * DEEP + col - DEEP - ELY, row * DEEP + col)
    turn = np.where(valid & ~middle, turn, -1)
    at = lane % SLOT
    send = at // DEEP * ELY + at % DEEP + np.where(lane >= SLOT, ELY - DEEP, 0)
    send = np.where((at < DEEP * XROWS) & (lane < 2 * SLOT), send, -1)
    return np.stack([spread, turn, send, row, col, row, row, row]).astype(np.int32)


def pick(values, index):
    return jnp.take_along_axis(values, jnp.broadcast_to(index, values.shape), axis=1, mode="promise_in_bounds")


def dot(a, b):
    return lax.dot_general(a, b, (((1,), (0,)), ((), ())), precision=HIGHEST, preferred_element_type=F32)


def selection(index, size):
    return jnp.where(lax.broadcasted_iota(jnp.int32, (size, index.shape[1]), 0) == index, 1.0, 0.0).astype(F32)


def add_rows(t, step, before, behind):
    width = t[0].shape[1]
    zero = lax.broadcasted_iota(jnp.int32, t[0].shape, 0) == 0
    back = width - step

    def masked(mask, values):
        return values if mask is None else jnp.where(mask, values, 0.0)

    from0 = masked(before, pltpu.roll(jnp.where(zero, t[1], 0.0), step, 1))
    from3 = masked(before, pltpu.roll(jnp.where(zero, t[2], t[1]), step, 1))
    from1 = masked(behind, pltpu.roll(jnp.where(zero, t[0], t[3]), back, 1))
    from2 = masked(behind, pltpu.roll(jnp.where(zero, t[3], 0.0), back, 1))
    return [t[0] + from0, t[1] + from1, t[2] + from2, t[3] + from3]


def add_columns(t, before, behind):
    turned = add_rows([t[1], t[2], t[3], t[0]], 1, before, behind)
    return [turned[3], turned[0], turned[1], turned[2]]


def tiles(values):
    return [values[8 * i : 8 * i + 8] for i in range(4)]


def transform_kernel(table, planes, out):
    groups, nodes = planes.shape[0], planes.shape[1]
    for n in range(nodes):
        block = planes[:, n].reshape(NZ, EL)
        out[:, n] = dot(table[...], block).reshape(groups, NZ // groups, EL)


def copies(source, target, nodes, done):
    step = -(-nodes // CHUNKS)
    cuts = [(at, min(step, nodes - at)) for at in range(0, nodes, step)]
    return [
        pltpu.make_async_copy(source.at[pl.ds(at, size)], target.at[pl.ds(at, size)], done.at[i])
        for i, (at, size) in enumerate(cuts)
    ]


def enter_kernel(forcing, coef_far, cell_far, planes, order, index, scale, stored, done, small, coef, cell):
    nodes = forcing.shape[0]
    fetched = [pltpu.make_async_copy(coef_far, coef, small.at[0]), pltpu.make_async_copy(cell_far, cell, small.at[1])]
    moved = copies(forcing, planes, nodes, done)
    for copy in fetched + moved:
        copy.start()
    planes[nodes:PADDED] = jnp.zeros((PADDED - nodes, planes.shape[1], EL), F32)
    for copy in fetched:
        copy.wait()
    lane = lax.broadcasted_iota(jnp.int32, (EL, EL), 1)
    elem = lax.broadcasted_iota(jnp.int32, (EL, EL), 0)
    cells = jnp.transpose(jnp.broadcast_to(cell[...], (EL, EL)))
    found = jnp.sum(jnp.where(cells == lane, elem, 0), axis=0, keepdims=True)
    order[...] = jnp.broadcast_to(found, (8, EL))
    index[...] = jnp.broadcast_to(cell[...], (8, EL))
    stored[...] = jnp.broadcast_to(coef[...], (8, EL))
    scale[...] = pick(jnp.broadcast_to(coef[...], (8, EL)), found)
    for copy in moved:
        copy.wait()


def leave_kernel(planes, velocity, done):
    moved = copies(planes, velocity, velocity.shape[0], done)
    for copy in moved:
        copy.start()
    for copy in moved:
        copy.wait()


def flipped(tile):
    back = (8 - lax.broadcasted_iota(jnp.int32, tile.shape, 0)) % 8
    return jnp.take_along_axis(tile, back, axis=0, mode="promise_in_bounds")


def both_ascending(values):
    return jnp.concatenate([values[0:16], flipped(values[16:24]), flipped(values[24:32])], 0)


def condense_kernel(spectral, order, scale, couple, condensed, down, up):
    lane = lax.broadcasted_iota(jnp.int32, (8, EL), 1)
    row, col, slot = lane // ELY, lane % ELY, lane // SLOT
    inner_row, inner_col = (row > 0, row < ELX - 1), (col > 0, col < ELY - 1)

    def messages(t):
        low, high = t[0], t[3]
        for i in (1, 2, 3):
            low = jnp.where(slot == i, pltpu.roll(t[i], SLOT * i, 1), low)
            high = jnp.where(slot == i - 1, pltpu.roll(t[i - 1], SLOT * i, 1), high)
        return low, high

    down[MODES], up[MODES] = messages([scale[...]] * 4)

    def mode(m, _):
        fields = pick(spectral[pl.ds(m, PADDED, stride=MODES), :], order[0:1])
        t = tiles(both_ascending(fields[0:NB] - dot(couple[m], fields[NB:NODES])))
        t = add_columns(add_rows(t, ELY, *inner_row), *inner_col)
        condensed[m] = jnp.concatenate(t, 0)
        down[m], up[m] = messages(t)
        return 0

    lax.fori_loop(0, MODES, mode, 0, unroll=UNROLL)


def interior_kernel(spectral, stored, inner, base):
    inverse = 1.0 / stored[0:1]

    def mode(m, _):
        within = spectral[pl.ds(NB * MODES + m, PADDED - NB, stride=MODES), :][0:NI]
        base[m, 0:NI] = dot(inner[pl.ds(m, NI, stride=MODES), :], within) * inverse
        return 0

    lax.fori_loop(0, MODES, mode, 0, unroll=UNROLL)


def columns_kernel(condensed, scale, low, high, table, left, right, middle, sent):
    lane = lax.broadcasted_iota(jnp.int32, (8, EL), 1)
    slot = lane // SLOT
    inner, outer = slot == 0, slot == 1
    meets = (lane >= SLOT) & (lane < SLOT + ELY), (lane >= SLOT - ELY) & (lane < SLOT)

    def stack(own, lo, hi):
        first, second = [], []
        for i in range(4):
            moved = pltpu.roll(own[i], SLOT, 1)
            below = lo if i == 0 else pltpu.roll(lo, EL - SLOT * i, 1)
            above = hi if i == 1 else pltpu.roll(hi, (EL + SLOT - SLOT * i) % EL, 1)
            first.append(jnp.where(inner, below, moved))
            second.append(jnp.where(inner, moved, jnp.where(outer, above, 0.0)))
        return first, second

    def put(m, parts):
        for j, part in enumerate(parts):
            middle[m, :, EL * j : EL * j + EL] = jnp.concatenate(part, 0)

    put(MODES, stack([scale[...]] * 4, low[MODES], high[MODES]))

    def mode(m, _):
        parts = stack(tiles(condensed[m]), low[m], high[m])
        put(m, [add_rows(part, ELY, *meets) for part in parts])
        return 0

    lax.fori_loop(0, MODES, mode, 0, unroll=UNROLL)
    send = selection(table[2:3, 0:EL], XL)
    sent[...] = dot(middle[...].reshape((MODES + 1) * NB, XL), send)

    def message(m, _):
        t = [sent[pl.ds(pl.multiple_of(m * NB + 8 * i, 8), 8), :] for i in range(4)]
        to_left, to_right = t[0], t[1]
        for i in range(1, 4):
            to_left = jnp.where(slot == i, pltpu.roll(t[i], SLOT * i, 1), to_left)
        for i in (0, 2, 3):
            to_right = jnp.where(slot == i, pltpu.roll(t[i], (SLOT * i - SLOT) % EL, 1), to_right)
        left[m], right[m] = to_left, to_right
        return 0

    lax.fori_loop(0, MODES + 1, message, 0, unroll=UNROLL)


def middle_kernel(middle, schur, table, block, matrix):
    lane = lax.broadcasted_iota(jnp.int32, (NB, NB), 1)
    across = jnp.where((lane >= 16) & (lane % 8 > 0), lane // 8 * 8 + 8 - lane % 8, lane)

    def mode(m, _):
        rows = both_ascending(schur[m])
        matrix[m] = jnp.take_along_axis(rows, across, axis=1, mode="promise_in_bounds")
        return 0

    lax.fori_loop(0, MODES, mode, 0, unroll=UNROLL)
    spread = dot(middle[...].reshape((MODES + 1) * NB, XL), selection(table[0:1], XL))
    block[...] = spread.reshape(MODES + 1, NB, XL)


def krylov_kernel(
    block, left, right, schur, table, basis, sums, keep_ref, weight_ref, mine_ref, parts, state, applied, pairs, spread
):
    half = lax.broadcasted_iota(jnp.int32, (8, EL), 1) < SLOT

    def pair_up(m, _):
        low, high = left[m], right[m]
        for i in range(4):
            below = low if i == 0 else pltpu.roll(low, EL - SLOT * i, 1)
            above = high if i == 1 else pltpu.roll(high, (EL + SLOT - SLOT * i) % EL, 1)
            pairs[pl.ds(pl.multiple_of(m * NB + 8 * i, 8), 8), :] = jnp.where(half, below, above)
        return 0

    lax.fori_loop(0, MODES + 1, pair_up, 0, unroll=UNROLL)
    spread[...] = dot(pairs[...], selection(table[1:2], EL))

    row, col = jnp.broadcast_to(table[3:4], (8, XL)), jnp.broadcast_to(table[4:5], (8, XL))
    grid_row = row - DEEP + lax.axis_index("ex") * ELX
    grid_col = col - DEEP + lax.axis_index("ey") * ELY
    last_row, last_col = lax.axis_size("ex") * ELX - 1, lax.axis_size("ey") * ELY - 1
    inside = (grid_row >= 0) & (grid_row <= last_row) & (grid_col >= 0) & (grid_col <= last_col) & (row < XROWS)
    own = (row >= DEEP) & (row < DEEP + ELX) & (col >= DEEP) & (col < DEEP + ELY)
    meets = (col == DEEP) | (col == DEEP + ELY), (col == DEEP - 1) | (col == DEEP + ELY - 1)
    mine_ref[...] = jnp.where(own, 1.0, 0.0).astype(F32)
    corner = lax.broadcasted_iota(jnp.int32, (8, XL), 0) == 0
    low_row, high_row, low_col, high_col = grid_row == 0, grid_row == last_row, grid_col == 0, grid_col == last_col
    for tile, (edge, other) in enumerate(((low_col, low_row), (high_row, low_col), (high_col, high_row), (low_row, high_col))):
        keep = jnp.where(inside & ~(edge | (corner & other)), 1.0, 0.0).astype(F32)
        keep_ref[8 * tile : 8 * tile + 8] = keep
        weight_ref[8 * tile : 8 * tile + 8] = jnp.where(own, keep * jnp.where(corner, 0.25, 0.5), 0.0).astype(F32)
    scale = jnp.where(inside[0:1], block[MODES, 0:1] + spread[MODES * NB : MODES * NB + 1], 0.0)

    def assemble(values):
        return keep_ref[...] * jnp.concatenate(add_columns(add_rows(tiles(values), PITCH, None, None), None, None), 0)

    eye = lax.broadcasted_iota(jnp.int32, (NB, NB), 0) == lax.broadcasted_iota(jnp.int32, (NB, NB), 1)
    def gather_mode(m):
        values = block[m] + spread[pl.ds(pl.multiple_of(m * NB, NB), NB), :]
        state[0, m] = keep_ref[...] * jnp.concatenate(add_columns(tiles(values), *meets), 0)

    def extend_mode(i):
        def run(m):
            trace = jnp.sum(jnp.sum(jnp.where(eye, schur[m], 0.0), axis=0, keepdims=True), axis=1, keepdims=True)
            images = scale * dot(schur[m], state[i, m])
            applied[i, m] = images
            state[i + 1, m] = assemble(images) * ((0.5 * NB) / trace) - state[i, m]

        return run

    def sum_mode(m):
        v = [state[i, m] for i in range(3)]
        w = [applied[0, m], applied[1, m], scale * dot(schur[m], v[2])]
        weight, mine = weight_ref[...], mine_ref[0:1]
        weighted = v[1] * weight
        own = [value * mine for value in v]
        k = 0
        for first, second in (
            (v[0], v[0] * weight), (v[0], weighted), (v[1], weighted),
            (own[0], w[0]), (own[1], w[0]), (own[1], w[1]), (own[2], w[1]), (own[2], w[2]),
        ):
            whole = jnp.sum(first * second, axis=0, keepdims=True)
            parts[pl.ds(MODES * k + m, 1), :] = whole[:, 0:EL] + whole[:, EL:XL]
            k += 1
        for i in range(3):
            basis[i, m] = v[i]

    def every(body):
        def step(m, _):
            body(m)
            return 0

        lax.fori_loop(0, MODES, step, 0, unroll=UNROLL)

    every(gather_mode)
    for i in range(2):
        every(extend_mode(i))
    every(sum_mode)
    ones = jnp.ones((8, EL), F32)
    total = lax.dot_general(ones, parts[...], (((1,), (1,)), ((), ())), precision=HIGHEST, preferred_element_type=F32)
    for at in range(0, sums.shape[0], 8):
        sums[at : at + 8] = total


def finish_kernel(gathered, basis, base, couple, cell, out, coefs):
    total = jnp.broadcast_to(jnp.sum(gathered[...].reshape(-1, EL), axis=0, keepdims=True), (8, EL))
    b0, b1, b2, h0, h1, h2, h3, h4 = [
        total if k == 0 else pltpu.roll(total, EL - MODES * k, 1) for k in range(8)
    ]
    tiny = 2e-7
    l1, l2 = h1 / h0, h2 / h0
    d1 = h2 - l1 * h1
    ok1 = d1 > tiny * h2
    d1 = jnp.where(ok1, d1, 1.0)
    l12 = jnp.where(ok1, (h3 - l1 * h2) / d1, 0.0)
    d2 = h4 - l2 * h2 - l12 * l12 * d1
    ok2 = d2 > tiny * h4
    y1 = b1 - l1 * b0
    y2 = b2 - l2 * b0 - l12 * y1
    c2 = jnp.where(ok2, y2 / jnp.where(ok2, d2, 1.0), 0.0)
    c1 = jnp.where(ok1, y1 / d1, 0.0) - l12 * c2
    c0 = b0 / h0 - l1 * c1 - l2 * c2
    coefs[0], coefs[1], coefs[2] = c0, c1, c2
    place = (cell[...] // ELY + DEEP) * PITCH + cell[...] % ELY + DEEP
    nearer = jnp.broadcast_to(place[0:1] < EL, (NB, EL))
    index = place[0:1] % EL

    for m in range(MODES):
        c = [coefs[i, 0:1, m : m + 1] for i in range(3)]
        x = c[0] * basis[0, m] + c[1] * basis[1, m] + c[2] * basis[2, m]
        x = both_ascending(jnp.where(nearer, pick(x[:, 0:EL], index), pick(x[:, EL:XL], index)))
        within = base[m, 0:NI] - lax.dot_general(
            couple[m], x, (((0,), (0,)), ((), ())), precision=HIGHEST, preferred_element_type=F32
        )
        out[pl.ds(m, PADDED, stride=MODES), :] = jnp.concatenate([x, within, jnp.zeros((PADDED - NODES, EL), F32)], 0)


def call(kernel, shapes=(), scratch=(), far=0, far_out=None):
    def run(*operands):
        many = isinstance(shapes, list)
        outs = [s if isinstance(s, pl.MemoryRef) else pltpu.VMEM(s, F32) for s in (shapes if many else [shapes])]
        whole, away = pl.BlockSpec(memory_space=pltpu.VMEM), pl.BlockSpec(memory_space=pl.ANY)
        near = tuple(pltpu.with_memory_space_constraint(o, pltpu.VMEM) for o in operands[far:])
        if far_out:
            outs = [jax.ShapeDtypeStruct(far_out, F32)]
        specs = [away if far_out else whole] * len(outs)
        return pl.pallas_call(
            kernel,
            out_shape=outs if many else outs[0],
            in_specs=[away] * far + [whole] * len(near),
            out_specs=specs if many else specs[0],
            scratch_shapes=list(scratch),
            compiler_params=pltpu.CompilerParams(vmem_limit_bytes=16 << 20),
            name=kernel.__name__,
        )(*(pltpu.with_memory_space_constraint(o, pltpu.HBM) for o in operands[:far]), *near)

    return run


def swap(array):
    return lax.all_to_all(array, "fourier", split_axis=0, concat_axis=0, tiled=True)


def ring(axis, step):
    count = lax.axis_size(axis)
    return [(i, (i + step) % count) for i in range(count)]


def neighbours(to_low, to_high, axis):
    return lax.ppermute(to_high, axis, ring(axis, 1)), lax.ppermute(to_low, axis, ring(axis, -1))


def on_device(forcing, element_coef, schur, couple, inner_inv, element_cell):
    parts = lax.axis_size("fourier")
    devices = lax.axis_size("ex") * lax.axis_size("ey")
    group = PADDED // parts
    table = jnp.asarray(real_transform())
    exchanged = (parts, group, MODES, EL)
    lanes = (8, EL)
    ints = pltpu.VMEM(lanes, jnp.int32)

    planes, order, index, scale, stored = call(
        enter_kernel, [(PADDED, MODES, EL), ints, ints, lanes, lanes],
        [
            pltpu.SemaphoreType.DMA((CHUNKS,)),
            pltpu.SemaphoreType.DMA((2,)),
            pltpu.VMEM((1, EL), F32),
            pltpu.VMEM((1, EL), jnp.int32),
        ],
        far=3,
    )(jnp.transpose(forcing, (1, 0, 2)), element_coef.reshape(1, EL), element_cell.reshape(1, EL))
    planes = swap(planes).reshape(exchanged)
    spectral = swap(call(transform_kernel, exchanged)(table, planes).reshape(PADDED, MODES, EL))
    spectral = spectral.reshape(PADDED * MODES, EL)

    message, extended = (MODES + 1, 8, EL), (MODES + 1, NB, XL)
    table_of_lanes = jnp.asarray(lane_tables())
    condensed, down, up = call(condense_kernel, [(MODES, NB, EL), message, message])(spectral, order, scale, couple)
    low, high = neighbours(down, up, "ex")
    base = call(interior_kernel, (MODES, 56, EL))(
        spectral, stored, jnp.transpose(inner_inv, (1, 0, 2)).reshape(NI * MODES, NI)
    )
    low, high, base = lax.optimization_barrier((low, high, base))
    rows = (MODES + 1) * NB
    left, right, middle = call(columns_kernel, [message, message, extended], [pltpu.VMEM((rows, EL), F32)])(
        condensed, scale, low, high, table_of_lanes
    )
    left, right = neighbours(left, right, "ey")
    block, matrix = call(middle_kernel, [extended, (MODES, NB, NB)])(middle, schur, table_of_lanes)
    basis, sums = call(
        krylov_kernel,
        [(3, MODES, NB, XL), (devices, EL)],
        [
            pltpu.VMEM((NB, XL), F32),
            pltpu.VMEM((NB, XL), F32),
            pltpu.VMEM((8, XL), F32),
            pltpu.VMEM((EL, EL), F32),
            pltpu.VMEM((3, MODES, NB, XL), F32),
            pltpu.VMEM((2, MODES, NB, XL), F32),
            pltpu.VMEM((rows, EL), F32),
            pltpu.VMEM((rows, XL), F32),
        ],
    )(block, left, right, matrix, table_of_lanes)
    gathered = lax.all_to_all(sums.reshape(devices, 1, EL), ("ex", "ey"), split_axis=0, concat_axis=0, tiled=True)
    modal = call(finish_kernel, (PADDED * MODES, EL), [pltpu.VMEM((3, 8, EL), F32)])(
        gathered, basis, base, couple, index
    )
    modal = swap(modal.reshape(PADDED, MODES, EL)).reshape(exchanged)
    velocity = swap(call(transform_kernel, exchanged)(table.T, modal).reshape(PADDED, MODES, EL))
    velocity = call(leave_kernel, far_out=(NODES, MODES, EL), scratch=[pltpu.SemaphoreType.DMA((CHUNKS,))])(velocity)
    return jnp.transpose(velocity, (1, 0, 2))


def solution(mesh):
    placed = (
        P("fourier", None, ("ex", "ey")),
        P(("ex", "ey")),
        P("fourier", None, None),
        P("fourier", None, None),
        P("fourier", None, None),
        P(("ex", "ey")),
    )
    return jax.shard_map(
        on_device,
        mesh=mesh,
        in_specs=placed,
        out_specs=P("fourier", None, ("ex", "ey")),
        check_vma=False,
    )
```

time: 110 us -> 108 us (0.982)
  waiting for transfers between devices: 3.11 us -> 1.37 us
    ppermute x2, waiting for transfers between devices: 3.08 us -> 1.35 us  [neighbours(): lax.ppermute(to_high, axis, ring(axis, 1))]
where the time goes in v3:
time: 108 us
  blocking collectives  83.2 us (77%)
  Pallas kernels  14.6 us (14%)
  starting transfers between devices  8.57 us (8%)
  waiting for transfers between devices  1.37 us (1%)
    all_to_all x4, blocking collectives, swap(): lax.all_to_all(array, 'fourier', split_axis=0, concat_axis=0, tiled=True)  66.4 us
    all_to_all x1, blocking collectives, on_device(): lax.all_to_all(sums.reshape(devices, 1, EL), ('ex', 'ey'), split_axis=0,...  16.8 us
    pallas_call x10, Pallas kernels, run(): pl.pallas_call(kernel, out_shape=outs if many else outs[0], in_specs=[awa...  14.6 us
    ppermute x2, starting transfers between devices, neighbours(): lax.ppermute(to_low, axis, ring(axis, -1))  5.56 us
    ppermute x2, starting transfers between devices, neighbours(): lax.ppermute(to_high, axis, ring(axis, 1))  3.01 us
  transfers between devices with their start and end apart: 4, of which 2 were waited for; matrix products, arithmetic and copies ran while one was open for 0% of the time, Pallas kernels for 2%

profile of v3, /device:TPU:1, one launch (start us, length us, event | category | flops | bytes accessed | tf_op | source)
XLA Modules:
  0.0 107.9 jit_solution(1541718866552819062)
XLA Ops:
  0.0 0.0 copy-start.5
  0.0 1.2 %enter_kernel.1 = (f32[88,16,128]{2,1,0:T(8,128)S(1)}, s32[8,128]{1,0:T(8,128)S(1)}, s32[8,128]{1,0:T(8,128)S(1)}, f32[8,128]{1,0:T(8,128)S(1)}, f32[8,128]{1,0:T(8,128)S(1)}) custom-call(f32[81,16,128]{2,1,0:T(8,128)} %bitcast.23, f32[1,128]{1,0:T(1,128)} %bitcast.24, s32[1,128]{1,0:T(1,128)} %bitcast.25), custom_call_target="tpu_custom_call" | custom-call | tf_op jit(solution)/shard_map/enter_kernel/pallas_call | solution.py:367
  1.3 17.2 %all_to_all.25 = f32[88,16,128]{2,1,0:T(8,128)S(1)} all-to-all(f32[88,16,128]{2,1,0:T(8,128)S(1)} %get-tuple-element.23), channel_id=1, replica_groups=mesh['fourier'=8,'ex'=8,'ey'=4] {'fourier'}, dimensions={0} | all-to-all | bytes 1441792 | tf_op jit(solution)/shard_map/all_to_all | solution.py:381
  18.5 0.0 copy-start
  18.5 0.0 copy-done.5
  18.5 0.7 transform_kernel.2
  19.2 0.0 copy-start.1
  19.3 15.1 %all_to_all.26 = f32[88,16,128]{2,1,0:T(8,128)S(1)} all-to-all(f32[88,16,128]{2,1,0:T(8,128)S(1)} %bitcast.17), channel_id=1, replica_groups=mesh['fourier'=8,'ex'=8,'ey'=4] {'fourier'}, dimensions={0} | all-to-all | bytes 1441792 | tf_op jit(solution)/shard_map/all_to_all | solution.py:381
  34.3 0.0 copy-start.3
  34.3 0.0 copy-start.2
  34.3 0.0 copy-done
  34.3 1.3 %condense_kernel.1 = (f32[16,32,128]{2,1,0:T(8,128)S(1)}, f32[17,8,128]{2,1,0:T(8,128)S(1)}, f32[17,8,128]{2,1,0:T(8,128)S(1)}) custom-call(f32[1408,128]{1,0:T(8,128)S(1)} %bitcast.14, s32[8,128]{1,0:T(8,128)S(1)} %get-tuple-element.24.order, f32[8,128]{1,0:T(8,128)S(1)} %get-tuple-element.25.scale, f32[16,32,49]{2,1,0:T(8,128)S(1)} %copy-done), custom_call_target="tpu_custom_call" | custom-call | tf_op jit(solution)/shard_map/condense_kernel/pallas_call | solution.py:367
  35.7 1.7 %collective-permute-start = (f32[17,8,128]{2,1,0:T(8,128)S(1)}, f32[17,8,128]{2,1,0:T(8,128)S(1)}, u32[]{:S(2)}, u32[]{:S(2)}) collective-permute-start(f32[17,8,128]{2,1,0:T(8,128)S(1)} %get-tuple-element.27), channel_id=1, source_target_pairs={{0,4},{4,8},{8,12},{12,16},{16,20},{20,24},{24,28},{28,0},{1,5},{5... | collective-permute-start | bytes 208904 | tf_op jit(solution)/shard_map/ppermute | solution.py:390
  37.3 4.0 %collective-permute-start.1 = (f32[17,8,128]{2,1,0:T(8,128)S(1)}, f32[17,8,128]{2,1,0:T(8,128)S(1)}, u32[]{:S(2)}, u32[]{:S(2)}) collective-permute-start(f32[17,8,128]{2,1,0:T(8,128)S(1)} %get-tuple-element.28), channel_id=1, source_target_pairs={{0,28},{4,0},{8,4},{12,8},{16,12},{20,16},{24,20},{28,24},{1,29},{... | collective-permute-start | bytes 208904 | tf_op jit(solution)/shard_map/ppermute | solution.py:390
  41.4 0.0 copy-done.1
  41.4 1.0 interior_kernel.1.base
  42.4 0.6 collective-permute-done.low
  43.0 0.0 collective-permute-done.1.high
  43.0 0.0 copy-done.3
  43.0 1.6 %columns_kernel.1 = (f32[17,8,128]{2,1,0:T(8,128)S(1)}, f32[17,8,128]{2,1,0:T(8,128)S(1)}, f32[17,32,256]{2,1,0:T(8,128)S(1)}) custom-call(f32[16,32,128]{2,1,0:T(8,128)S(1)} %get-tuple-element.26.condensed, f32[8,128]{1,0:T(8,128)S(1)} %get-tuple-element.25.scale, f32[17,8,128]{2,1,0:T(8,128)S(1)} %collective-permute-done.low, ...), custom_call_target="tpu_custom_call" | custom-call | tf_op jit(solution)/shard_map/columns_kernel/pallas_call | solution.py:367
  44.6 1.3 %collective-permute-start.2 = (f32[17,8,128]{2,1,0:T(8,128)S(1)}, f32[17,8,128]{2,1,0:T(8,128)S(1)}, u32[]{:S(2)}, u32[]{:S(2)}) collective-permute-start(f32[17,8,128]{2,1,0:T(8,128)S(1)} %get-tuple-element.34), channel_id=1, source_target_pairs={{0,1},{1,2},{2,3},{3,0},{4,5},{5,6},{6,7},{7,4},{8,9},{9,10},{10,1... | collective-permute-start | bytes 208904 | tf_op jit(solution)/shard_map/ppermute | solution.py:390
  45.9 1.5 %collective-permute-start.3 = (f32[17,8,128]{2,1,0:T(8,128)S(1)}, f32[17,8,128]{2,1,0:T(8,128)S(1)}, u32[]{:S(2)}, u32[]{:S(2)}) collective-permute-start(f32[17,8,128]{2,1,0:T(8,128)S(1)} %get-tuple-element.35), channel_id=1, source_target_pairs={{0,3},{1,0},{2,1},{3,2},{4,7},{5,4},{6,5},{7,6},{8,11},{9,8},{10,9... | collective-permute-start | bytes 208904 | tf_op jit(solution)/shard_map/ppermute | solution.py:390
  47.5 0.0 copy-done.2
  47.5 0.8 middle_kernel.1
  48.3 0.8 collective-permute-done.2.left
  49.1 0.0 collective-permute-done.3.right
  49.1 4.4 %krylov_kernel.1 = (f32[3,16,32,256]{3,2,1,0:T(8,128)S(1)}, f32[32,128]{1,0:T(8,128)S(1)}) custom-call(f32[17,32,256]{2,1,0:T(8,128)S(1)} %get-tuple-element.33.block, f32[17,8,128]{2,1,0:T(8,128)S(1)} %collective-permute-done.2.left, f32[17,8,128]{2,1,0:T(8,128)S(1)} %collective-permute-done.3.right, f32[16,32,32]{2,1,0:T(8,128)S(1)} %get-tuple-element.36.schur, ...), custom_call_target="tpu_custom_call" | custom-call | tf_op jit(solution)/shard_map/krylov_kernel/pallas_call | solution.py:367
  53.5 16.8 %all_to_all.27.gathered = f32[32,1,128]{2,1,0:T(1,128)S(1)} all-to-all(f32[32,1,128]{2,1,0:T(1,128)S(1)} %bitcast.22), channel_id=1, replica_groups=mesh['fourier'=8,'ex'=8,'ey'=4] {'ex','ey'}, dimensions={0} | all-to-all | bytes 32768 | tf_op jit(solution)/shard_map/all_to_all | solution.py:444
  70.3 0.0 copy-start.4
  70.3 1.9 %finish_kernel.1 = f32[1408,128]{1,0:T(8,128)S(1)} custom-call(f32[32,1,128]{2,1,0:T(1,128)S(1)} %all_to_all.27.gathered, f32[3,16,32,256]{3,2,1,0:T(8,128)S(1)} %get-tuple-element.38.basis, f32[16,56,128]{2,1,0:T(8,128)S(1)} %interior_kernel.1.base, f32[16,32,49]{2,1,0:T(8,128)S(1)} %copy-done, s32[8,128]{1,0:T(8,128)S(1)} %get-tuple-element.40.cell), custom_call_target="tpu_custom_call" | custom-call | tf_op jit(solution)/shard_map/finish_kernel/pallas_call | solution.py:367
  72.2 19.1 %all_to_all.28 = f32[88,16,128]{2,1,0:T(8,128)S(1)} all-to-all(f32[88,16,128]{2,1,0:T(8,128)S(1)} %bitcast.20), channel_id=1, replica_groups=mesh['fourier'=8,'ex'=8,'ey'=4] {'fourier'}, dimensions={0} | all-to-all | bytes 1441792 | tf_op jit(solution)/shard_map/all_to_all | solution.py:381
  91.3 0.0 copy-done.4
  91.3 0.7 transform_kernel.3
  92.1 14.9 %all_to_all.29.planes = f32[88,16,128]{2,1,0:T(8,128)S(1)} all-to-all(f32[88,16,128]{2,1,0:T(8,128)S(1)} %bitcast.19), channel_id=1, replica_groups=mesh['fourier'=8,'ex'=8,'ey'=4] {'fourier'}, dimensions={0} | all-to-all | bytes 1441792 | tf_op jit(solution)/shard_map/all_to_all | solution.py:381
  107.0 0.9 leave_kernel.1
Async XLA Ops:
  0.0 18.5 %copy-start.5 = (f32[128,128]{1,0:T(8,128)S(1)}, f32[128,128]{1,0:T(8,128)}, u32[]{:S(2)}) copy-start(f32[128,128]{1,0:T(8,128)} %constant.4.clone.table) | copy-start | bytes 196612
  18.5 15.8 %copy-start = (f32[16,32,49]{2,1,0:T(8,128)S(1)}, f32[16,32,49]{2,1,0:T(8,128)}, u32[]{:S(2)}) copy-start(f32[16,32,49]{2,1,0:T(8,128)} %couple.3) | copy-start | bytes 301060
  19.2 22.1 %copy-start.1 = (f32[16,49,49]{2,0,1:T(8,128)S(1)}, f32[16,49,49]{2,0,1:T(8,128)}, u32[]{:S(2)}) copy-start(f32[16,49,49]{2,0,1:T(8,128)} %param.12) | copy-start | bytes 460996
  34.3 8.6 %copy-start.3 = (s32[8,256]{1,0:T(8,128)S(1)}, s32[8,256]{1,0:T(8,128)}, u32[]{:S(2)}) copy-start(s32[8,256]{1,0:T(8,128)} %constant.5.clone.table) | copy-start | bytes 24580
  34.3 13.1 %copy-start.2 = (f32[16,32,32]{2,1,0:T(8,128)S(1)}, f32[16,32,32]{2,1,0:T(8,128)}, u32[]{:S(2)}) copy-start(f32[16,32,32]{2,1,0:T(8,128)} %schur.1) | copy-start | bytes 196612
  35.7 7.3 %collective-permute-start = (f32[17,8,128]{2,1,0:T(8,128)S(1)}, f32[17,8,128]{2,1,0:T(8,128)S(1)}, u32[]{:S(2)}, u32[]{:S(2)}) collective-permute-start(f32[17,8,128]{2,1,0:T(8,128)S(1)} %get-tuple-element.27), channel_id=1, source_target_pairs={{0,4},{4,8},{8,12},{12,16},{16,20},{20,24},{24,28},{28,0},{1,5},{5... | collective-permute-start | bytes 208904 | tf_op jit(solution)/shard_map/ppermute | solution.py:390
  37.3 5.6 %collective-permute-start.1 = (f32[17,8,128]{2,1,0:T(8,128)S(1)}, f32[17,8,128]{2,1,0:T(8,128)S(1)}, u32[]{:S(2)}, u32[]{:S(2)}) collective-permute-start(f32[17,8,128]{2,1,0:T(8,128)S(1)} %get-tuple-element.28), channel_id=1, source_target_pairs={{0,28},{4,0},{8,4},{12,8},{16,12},{20,16},{24,20},{28,24},{1,29},{... | collective-permute-start | bytes 208904 | tf_op jit(solution)/shard_map/ppermute | solution.py:390
  44.6 4.5 %collective-permute-start.2 = (f32[17,8,128]{2,1,0:T(8,128)S(1)}, f32[17,8,128]{2,1,0:T(8,128)S(1)}, u32[]{:S(2)}, u32[]{:S(2)}) collective-permute-start(f32[17,8,128]{2,1,0:T(8,128)S(1)} %get-tuple-element.34), channel_id=1, source_target_pairs={{0,1},{1,2},{2,3},{3,0},{4,5},{5,6},{6,7},{7,4},{8,9},{9,10},{10,1... | collective-permute-start | bytes 208904 | tf_op jit(solution)/shard_map/ppermute | solution.py:390
  45.9 3.2 %collective-permute-start.3 = (f32[17,8,128]{2,1,0:T(8,128)S(1)}, f32[17,8,128]{2,1,0:T(8,128)S(1)}, u32[]{:S(2)}, u32[]{:S(2)}) collective-permute-start(f32[17,8,128]{2,1,0:T(8,128)S(1)} %get-tuple-element.35), channel_id=1, source_target_pairs={{0,3},{1,0},{2,1},{3,2},{4,7},{5,4},{6,5},{7,6},{8,11},{9,8},{10,9... | collective-permute-start | bytes 208904 | tf_op jit(solution)/shard_map/ppermute | solution.py:390
  70.3 21.0 %copy-start.4 = (f32[128,128]{1,0:T(8,128)S(1)}, f32[128,128]{1,0:T(8,128)}, u32[]{:S(2)}) copy-start(f32[128,128]{1,0:T(8,128)} %constant.6.table) | copy-start | bytes 196612

commit v4 on v3

--- a/solution.py
+++ b/solution.py
@@ -25,6 +25,7 @@
 XL = 256
 SLOT = DEEP * ELY
 UNROLL = 8
+QUAD = 4
 CHUNKS = 3
 HIGHEST = lax.Precision.HIGHEST
 F32 = jnp.float32
@@ -67,6 +68,19 @@
     return jnp.where(lax.broadcasted_iota(jnp.int32, (size, index.shape[1]), 0) == index, 1.0, 0.0).astype(F32)
 
 
+def take(values, chosen):
+    high = values.astype(jnp.bfloat16)
+    rest = values - high.astype(F32)
+    middle = rest.astype(jnp.bfloat16)
+    low = (rest - middle.astype(F32)).astype(jnp.bfloat16)
+    chosen = chosen.astype(jnp.bfloat16)
+
+    def product(part):
+        return lax.dot_general(part, chosen, (((1,), (0,)), ((), ())), preferred_element_type=F32)
+
+    return (product(high) + product(middle)) + product(low)
+
+
 def add_rows(t, step, before, behind):
     width = t[0].shape[1]
     zero = lax.broadcasted_iota(jnp.int32, t[0].shape, 0) == 0
@@ -91,11 +105,26 @@
     return [values[8 * i : 8 * i + 8] for i in range(4)]
 
 
+def split(values):
+    high = values.astype(jnp.bfloat16)
+    return high, (values - high.astype(F32)).astype(jnp.bfloat16)
+
+
+def dot_of_parts(a, b):
+    (a_high, a_low), (b_high, b_low) = a, b
+
+    def product(first, second):
+        return lax.dot_general(first, second, (((1,), (0,)), ((), ())), preferred_element_type=F32)
+
+    return product(a_high, b_low) + product(a_low, b_high) + product(a_high, b_high)
+
+
 def transform_kernel(table, planes, out):
     groups, nodes = planes.shape[0], planes.shape[1]
+    held = split(table[...])
     for n in range(nodes):
         block = planes[:, n].reshape(NZ, EL)
-        out[:, n] = dot(table[...], block).reshape(groups, NZ // groups, EL)
+        out[:, n] = dot_of_parts(held, split(block)).reshape(groups, NZ // groups, EL)
 
 
 def copies(source, target, nodes, done):
@@ -160,8 +189,9 @@
     down[MODES], up[MODES] = messages([scale[...]] * 4)
 
     def mode(m, _):
-        fields = pick(spectral[pl.ds(m, PADDED, stride=MODES), :], order[0:1])
-        t = tiles(both_ascending(fields[0:NB] - dot(couple[m], fields[NB:NODES])))
+        fields = spectral[pl.ds(m, PADDED, stride=MODES), :]
+        value = fields[0:NB] - dot_of_parts(split(couple[m]), split(fields[NB:NODES]))
+        t = tiles(both_ascending(pick(value, order[0:1])))
         t = add_columns(add_rows(t, ELY, *inner_row), *inner_col)
         condensed[m] = jnp.concatenate(t, 0)
         down[m], up[m] = messages(t)
@@ -170,7 +200,7 @@
     lax.fori_loop(0, MODES, mode, 0, unroll=UNROLL)
 
 
-def interior_kernel(spectral, stored, inner, base):
+def interior_kernel(spectral, stored, inner, couple, base, turned, wide):
     inverse = 1.0 / stored[0:1]
 
     def mode(m, _):
@@ -179,6 +209,10 @@
         return 0
 
     lax.fori_loop(0, MODES, mode, 0, unroll=UNROLL)
+    wide[...] = jnp.zeros_like(wide)
+    for q in range(MODES // QUAD):
+        wide[:, 0:NI] = couple[QUAD * q : QUAD * q + QUAD].reshape(QUAD * NB, NI)
+        turned[q] = jnp.transpose(wide[...])[0 : turned.shape[1]]
 
 
 def columns_kernel(condensed, scale, low, high, table, left, right, middle, sent):
@@ -210,7 +244,7 @@
 
     lax.fori_loop(0, MODES, mode, 0, unroll=UNROLL)
     send = selection(table[2:3, 0:EL], XL)
-    sent[...] = dot(middle[...].reshape((MODES + 1) * NB, XL), send)
+    sent[...] = take(middle[...].reshape((MODES + 1) * NB, XL), send)
 
     def message(m, _):
         t = [sent[pl.ds(pl.multiple_of(m * NB + 8 * i, 8), 8), :] for i in range(4)]
@@ -235,7 +269,7 @@
         return 0
 
     lax.fori_loop(0, MODES, mode, 0, unroll=UNROLL)
-    spread = dot(middle[...].reshape((MODES + 1) * NB, XL), selection(table[0:1], XL))
+    spread = take(middle[...].reshape((MODES + 1) * NB, XL), selection(table[0:1], XL))
     block[...] = spread.reshape(MODES + 1, NB, XL)
 
 
@@ -253,7 +287,7 @@
         return 0
 
     lax.fori_loop(0, MODES + 1, pair_up, 0, unroll=UNROLL)
-    spread[...] = dot(pairs[...], selection(table[1:2], EL))
+    spread[...] = take(pairs[...], selection(table[1:2], EL))
 
     row, col = jnp.broadcast_to(table[3:4], (8, XL)), jnp.broadcast_to(table[4:5], (8, XL))
     grid_row = row - DEEP + lax.axis_index("ex") * ELX
@@ -322,7 +356,7 @@
         sums[at : at + 8] = total
 
 
-def finish_kernel(gathered, basis, base, couple, cell, out, coefs):
+def finish_kernel(gathered, basis, base, couple, cell, out, coefs, mixed, blocks):
     total = jnp.broadcast_to(jnp.sum(gathered[...].reshape(-1, EL), axis=0, keepdims=True), (8, EL))
     b0, b1, b2, h0, h1, h2, h3, h4 = [
         total if k == 0 else pltpu.roll(total, EL - MODES * k, 1) for k in range(8)
@@ -340,19 +374,32 @@
     c2 = jnp.where(ok2, y2 / jnp.where(ok2, d2, 1.0), 0.0)
     c1 = jnp.where(ok1, y1 / d1, 0.0) - l12 * c2
     c0 = b0 / h0 - l1 * c1 - l2 * c2
-    coefs[0], coefs[1], coefs[2] = c0, c1, c2
-    place = (cell[...] // ELY + DEEP) * PITCH + cell[...] % ELY + DEEP
-    nearer = jnp.broadcast_to(place[0:1] < EL, (NB, EL))
-    index = place[0:1] % EL
-
+    for i, c in enumerate((c0, c1, c2)):
+        coefs[i] = jnp.transpose(jnp.broadcast_to(c[0:1], (EL, EL)))[0:MODES]
+    place = (cell[0:1] // ELY + DEEP) * PITCH + cell[0:1] % ELY + DEEP
+
+    def combine(m, _):
+        c = [jnp.concatenate([coefs[i, pl.ds(m, 1), :]] * 2, 1) for i in range(3)]
+        x = c[0] * basis[0, m] + c[1] * basis[1, m] + c[2] * basis[2, m]
+        mixed[pl.ds(pl.multiple_of(m * NB, NB), NB), :] = both_ascending(x)
+        return 0
+
+    lax.fori_loop(0, MODES, combine, 0, unroll=UNROLL)
+    solved = take(mixed[...], selection(place, XL))
+    blocks[...] = jnp.zeros_like(blocks)
     for m in range(MODES):
-        c = [coefs[i, 0:1, m : m + 1] for i in range(3)]
-        x = c[0] * basis[0, m] + c[1] * basis[1, m] + c[2] * basis[2, m]
-        x = both_ascending(jnp.where(nearer, pick(x[:, 0:EL], index), pick(x[:, EL:XL], index)))
-        within = base[m, 0:NI] - lax.dot_general(
-            couple[m], x, (((0,), (0,)), ((), ())), precision=HIGHEST, preferred_element_type=F32
-        )
-        out[pl.ds(m, PADDED, stride=MODES), :] = jnp.concatenate([x, within, jnp.zeros((PADDED - NODES, EL), F32)], 0)
+        x = solved[m * NB : m * NB + NB]
+        q, r = m // QUAD, m % QUAD
+        blocks[q, NB * r : NB * r + NB, EL * r : EL * r + EL] = x
+        for tile in range(4):
+            out[pl.ds(8 * tile * MODES + m, 8, stride=MODES), :] = x[8 * tile : 8 * tile + 8]
+    for q in range(MODES // QUAD):
+        lifted = dot_of_parts(split(couple[q]), split(blocks[q]))
+        for r in range(QUAD):
+            m = QUAD * q + r
+            within = base[m, 0:NI] - lifted[0:NI, EL * r : EL * r + EL]
+            within = jnp.concatenate([within, jnp.zeros((PADDED - NODES, EL), F32)], 0)
+            out[pl.ds(NB * MODES + m, PADDED - NB, stride=MODES), :] = within
 
 
 def call(kernel, shapes=(), scratch=(), far=0, far_out=None):
@@ -417,10 +464,10 @@
     table_of_lanes = jnp.asarray(lane_tables())
     condensed, down, up = call(condense_kernel, [(MODES, NB, EL), message, message])(spectral, order, scale, couple)
     low, high = neighbours(down, up, "ex")
-    base = call(interior_kernel, (MODES, 56, EL))(
-        spectral, stored, jnp.transpose(inner_inv, (1, 0, 2)).reshape(NI * MODES, NI)
-    )
-    low, high, base = lax.optimization_barrier((low, high, base))
+    base, turned = call(
+        interior_kernel, [(MODES, 56, EL), (MODES // QUAD, 56, QUAD * NB)], [pltpu.VMEM((QUAD * NB, EL), F32)]
+    )(spectral, stored, jnp.transpose(inner_inv, (1, 0, 2)).reshape(NI * MODES, NI), couple)
+    low, high, base, turned = lax.optimization_barrier((low, high, base, turned))
     rows = (MODES + 1) * NB
     left, right, middle = call(columns_kernel, [message, message, extended], [pltpu.VMEM((rows, EL), F32)])(
         condensed, scale, low, high, table_of_lanes
@@ -442,8 +489,8 @@
         ],
     )(block, left, right, matrix, table_of_lanes)
     gathered = lax.all_to_all(sums.reshape(devices, 1, EL), ("ex", "ey"), split_axis=0, concat_axis=0, tiled=True)
-    modal = call(finish_kernel, (PADDED * MODES, EL), [pltpu.VMEM((3, 8, EL), F32)])(
-        gathered, basis, base, couple, index
+    modal = call(finish_kernel, (PADDED * MODES, EL), [pltpu.VMEM((3, MODES, EL), F32), pltpu.VMEM((MODES * NB, XL), F32), pltpu.VMEM((MODES // QUAD, QUAD * NB, QUAD * EL), F32)])(
+        gathered, basis, base, turned, index
     )
     modal = swap(modal.reshape(PADDED, MODES, EL)).reshape(exchanged)
     velocity = swap(call(transform_kernel, exchanged)(table.T, modal).reshape(PADDED, MODES, EL))

time: 108 us -> 106 us (0.981)
  Pallas kernels: 14.6 us -> 12.9 us
    pallas_call x10, Pallas kernels: 14.6 us -> 12.9 us  [run(): pl.pallas_call(kernel, out_shape=outs if many else outs[0], in_specs=[awa...]
where the time goes in v4:
time: 106 us
  blocking collectives  83.2 us (78%)
  Pallas kernels  12.9 us (12%)
  starting transfers between devices  8.56 us (8%)
  waiting for transfers between devices  1.46 us (1%)
    all_to_all x4, blocking collectives, swap(): lax.all_to_all(array, 'fourier', split_axis=0, concat_axis=0, tiled=True)  66.4 us
    all_to_all x1, blocking collectives, on_device(): lax.all_to_all(sums.reshape(devices, 1, EL), ('ex', 'ey'), split_axis=0,...  16.8 us
    pallas_call x10, Pallas kernels, run(): pl.pallas_call(kernel, out_shape=outs if many else outs[0], in_specs=[awa...  12.9 us
    ppermute x2, starting transfers between devices, neighbours(): lax.ppermute(to_low, axis, ring(axis, -1))  5.56 us
    ppermute x2, starting transfers between devices, neighbours(): lax.ppermute(to_high, axis, ring(axis, 1))  3.01 us
  transfers between devices with their start and end apart: 4, of which 2 were waited for; matrix products, arithmetic and copies ran while one was open for 0% of the time, Pallas kernels for 2%

profile of v4, /device:TPU:1, one launch (start us, length us, event | category | flops | bytes accessed | tf_op | source)
XLA Modules:
  0.0 106.2 jit_solution(15561410427188869709)
XLA Ops:
  0.0 0.0 copy-start.5
  0.0 1.2 %enter_kernel.1 = (f32[88,16,128]{2,1,0:T(8,128)S(1)}, s32[8,128]{1,0:T(8,128)S(1)}, s32[8,128]{1,0:T(8,128)S(1)}, f32[8,128]{1,0:T(8,128)S(1)}, f32[8,128]{1,0:T(8,128)S(1)}) custom-call(f32[81,16,128]{2,1,0:T(8,128)} %bitcast.23, f32[1,128]{1,0:T(1,128)} %bitcast.24, s32[1,128]{1,0:T(1,128)} %bitcast.25), custom_call_target="tpu_custom_call" | custom-call | tf_op jit(solution)/shard_map/enter_kernel/pallas_call | solution.py:414
  1.3 17.2 %all_to_all.25 = f32[88,16,128]{2,1,0:T(8,128)S(1)} all-to-all(f32[88,16,128]{2,1,0:T(8,128)S(1)} %get-tuple-element.26), channel_id=1, replica_groups=mesh['fourier'=8,'ex'=8,'ey'=4] {'fourier'}, dimensions={0} | all-to-all | bytes 1441792 | tf_op jit(solution)/shard_map/all_to_all | solution.py:428
  18.5 0.0 copy-start
  18.5 0.0 copy-done.5
  18.5 0.4 transform_kernel.2
  19.0 0.0 copy-start.1
  19.0 0.0 copy-start.3
  19.0 15.1 %all_to_all.26 = f32[88,16,128]{2,1,0:T(8,128)S(1)} all-to-all(f32[88,16,128]{2,1,0:T(8,128)S(1)} %bitcast.17), channel_id=1, replica_groups=mesh['fourier'=8,'ex'=8,'ey'=4] {'fourier'}, dimensions={0} | all-to-all | bytes 1441792 | tf_op jit(solution)/shard_map/all_to_all | solution.py:428
  34.1 0.0 copy-start.2
  34.1 0.0 copy-done
  34.1 1.2 %condense_kernel.1 = (f32[16,32,128]{2,1,0:T(8,128)S(1)}, f32[17,8,128]{2,1,0:T(8,128)S(1)}, f32[17,8,128]{2,1,0:T(8,128)S(1)}) custom-call(f32[1408,128]{1,0:T(8,128)S(1)} %bitcast.14, s32[8,128]{1,0:T(8,128)S(1)} %get-tuple-element.27.order, f32[8,128]{1,0:T(8,128)S(1)} %get-tuple-element.28.scale, f32[16,32,49]{2,1,0:T(8,128)S(1)} %copy-done), custom_call_target="tpu_custom_call" | custom-call | tf_op jit(solution)/shard_map/condense_kernel/pallas_call | solution.py:414
  35.2 1.7 %collective-permute-start = (f32[17,8,128]{2,1,0:T(8,128)S(1)}, f32[17,8,128]{2,1,0:T(8,128)S(1)}, u32[]{:S(2)}, u32[]{:S(2)}) collective-permute-start(f32[17,8,128]{2,1,0:T(8,128)S(1)} %get-tuple-element.30), channel_id=1, source_target_pairs={{0,4},{4,8},{8,12},{12,16},{16,20},{20,24},{24,28},{28,0},{1,5},{5... | collective-permute-start | bytes 208904 | tf_op jit(solution)/shard_map/ppermute | solution.py:437
  36.9 4.0 %collective-permute-start.1 = (f32[17,8,128]{2,1,0:T(8,128)S(1)}, f32[17,8,128]{2,1,0:T(8,128)S(1)}, u32[]{:S(2)}, u32[]{:S(2)}) collective-permute-start(f32[17,8,128]{2,1,0:T(8,128)S(1)} %get-tuple-element.31), channel_id=1, source_target_pairs={{0,28},{4,0},{8,4},{12,8},{16,12},{20,16},{24,20},{28,24},{1,29},{... | collective-permute-start | bytes 208904 | tf_op jit(solution)/shard_map/ppermute | solution.py:437
  40.9 0.0 copy-done.1
  40.9 1.2 %interior_kernel.1 = (f32[16,56,128]{2,1,0:T(8,128)S(1)}, f32[4,56,128]{2,1,0:T(8,128)S(1)}) custom-call(f32[1408,128]{1,0:T(8,128)S(1)} %bitcast.15, f32[8,128]{1,0:T(8,128)S(1)} %get-tuple-element.32.stored, f32[784,49]{1,0:T(8,128)S(1)} %bitcast.21, f32[16,32,49]{2,1,0:T(8,128)S(1)} %copy-done), custom_call_target="tpu_custom_call" | custom-call | tf_op jit(solution)/shard_map/interior_kernel/pallas_call | solution.py:414
  42.1 0.5 collective-permute-done.low
  42.5 0.0 collective-permute-done.1.high
  42.5 0.0 copy-done.3
  42.6 1.4 %columns_kernel.1 = (f32[17,8,128]{2,1,0:T(8,128)S(1)}, f32[17,8,128]{2,1,0:T(8,128)S(1)}, f32[17,32,256]{2,1,0:T(8,128)S(1)}) custom-call(f32[16,32,128]{2,1,0:T(8,128)S(1)} %get-tuple-element.29.condensed, f32[8,128]{1,0:T(8,128)S(1)} %get-tuple-element.28.scale, f32[17,8,128]{2,1,0:T(8,128)S(1)} %collective-permute-done.low, ...), custom_call_target="tpu_custom_call" | custom-call | tf_op jit(solution)/shard_map/columns_kernel/pallas_call | solution.py:414
  43.9 1.3 %collective-permute-start.2 = (f32[17,8,128]{2,1,0:T(8,128)S(1)}, f32[17,8,128]{2,1,0:T(8,128)S(1)}, u32[]{:S(2)}, u32[]{:S(2)}) collective-permute-start(f32[17,8,128]{2,1,0:T(8,128)S(1)} %get-tuple-element.39), channel_id=1, source_target_pairs={{0,1},{1,2},{2,3},{3,0},{4,5},{5,6},{6,7},{7,4},{8,9},{9,10},{10,1... | collective-permute-start | bytes 208904 | tf_op jit(solution)/shard_map/ppermute | solution.py:437
  45.3 1.5 %collective-permute-start.3 = (f32[17,8,128]{2,1,0:T(8,128)S(1)}, f32[17,8,128]{2,1,0:T(8,128)S(1)}, u32[]{:S(2)}, u32[]{:S(2)}) collective-permute-start(f32[17,8,128]{2,1,0:T(8,128)S(1)} %get-tuple-element.40), channel_id=1, source_target_pairs={{0,3},{1,0},{2,1},{3,2},{4,7},{5,4},{6,5},{7,6},{8,11},{9,8},{10,9... | collective-permute-start | bytes 208904 | tf_op jit(solution)/shard_map/ppermute | solution.py:437
  46.8 0.0 copy-done.2
  46.8 0.6 middle_kernel.1
  47.4 1.0 collective-permute-done.2.left
  48.4 0.0 collective-permute-done.3.right
  48.4 4.2 %krylov_kernel.1 = (f32[3,16,32,256]{3,2,1,0:T(8,128)S(1)}, f32[32,128]{1,0:T(8,128)S(1)}) custom-call(f32[17,32,256]{2,1,0:T(8,128)S(1)} %get-tuple-element.38.block, f32[17,8,128]{2,1,0:T(8,128)S(1)} %collective-permute-done.2.left, f32[17,8,128]{2,1,0:T(8,128)S(1)} %collective-permute-done.3.right, f32[16,32,32]{2,1,0:T(8,128)S(1)} %get-tuple-element.41.schur, ...), custom_call_target="tpu_custom_call" | custom-call | tf_op jit(solution)/shard_map/krylov_kernel/pallas_call | solution.py:414
  52.6 16.8 %all_to_all.27.gathered = f32[32,1,128]{2,1,0:T(1,128)S(1)} all-to-all(f32[32,1,128]{2,1,0:T(1,128)S(1)} %bitcast.22), channel_id=1, replica_groups=mesh['fourier'=8,'ex'=8,'ey'=4] {'ex','ey'}, dimensions={0} | all-to-all | bytes 32768 | tf_op jit(solution)/shard_map/all_to_all | solution.py:491
  69.4 0.0 copy-start.4
  69.4 1.4 %finish_kernel.1 = f32[1408,128]{1,0:T(8,128)S(1)} custom-call(f32[32,1,128]{2,1,0:T(1,128)S(1)} %all_to_all.27.gathered, f32[3,16,32,256]{3,2,1,0:T(8,128)S(1)} %get-tuple-element.43.basis, f32[16,56,128]{2,1,0:T(8,128)S(1)} %get-tuple-element.44.base, f32[4,56,128]{2,1,0:T(8,128)S(1)} %get-tuple-element.45.couple, s32[8,128]{1,0:T(8,128)S(1)} %get-tuple-element.46.cell), custom_call_target="tpu_custom_call" | custom-call | tf_op jit(solution)/shard_map/finish_kernel/pallas_call | solution.py:414
  70.8 19.1 %all_to_all.28 = f32[88,16,128]{2,1,0:T(8,128)S(1)} all-to-all(f32[88,16,128]{2,1,0:T(8,128)S(1)} %bitcast.20), channel_id=1, replica_groups=mesh['fourier'=8,'ex'=8,'ey'=4] {'fourier'}, dimensions={0} | all-to-all | bytes 1441792 | tf_op jit(solution)/shard_map/all_to_all | solution.py:428
  89.9 0.0 copy-done.4
  89.9 0.4 transform_kernel.3
  90.4 14.9 %all_to_all.29.planes = f32[88,16,128]{2,1,0:T(8,128)S(1)} all-to-all(f32[88,16,128]{2,1,0:T(8,128)S(1)} %bitcast.19), channel_id=1, replica_groups=mesh['fourier'=8,'ex'=8,'ey'=4] {'fourier'}, dimensions={0} | all-to-all | bytes 1441792 | tf_op jit(solution)/shard_map/all_to_all | solution.py:428
  105.3 0.9 leave_kernel.1
Async XLA Ops:
  0.0 18.5 %copy-start.5 = (f32[128,128]{1,0:T(8,128)S(1)}, f32[128,128]{1,0:T(8,128)}, u32[]{:S(2)}) copy-start(f32[128,128]{1,0:T(8,128)} %constant.4.clone.table) | copy-start | bytes 196612
  18.5 15.6 %copy-start = (f32[16,32,49]{2,1,0:T(8,128)S(1)}, f32[16,32,49]{2,1,0:T(8,128)}, u32[]{:S(2)}) copy-start(f32[16,32,49]{2,1,0:T(8,128)} %couple.3) | copy-start | bytes 301060
  19.0 22.0 %copy-start.1 = (f32[16,49,49]{2,0,1:T(8,128)S(1)}, f32[16,49,49]{2,0,1:T(8,128)}, u32[]{:S(2)}) copy-start(f32[16,49,49]{2,0,1:T(8,128)} %param.12) | copy-start | bytes 460996
  19.0 23.6 %copy-start.3 = (s32[8,256]{1,0:T(8,128)S(1)}, s32[8,256]{1,0:T(8,128)}, u32[]{:S(2)}) copy-start(s32[8,256]{1,0:T(8,128)} %constant.5.clone.table) | copy-start | bytes 24580
  34.1 12.8 %copy-start.2 = (f32[16,32,32]{2,1,0:T(8,128)S(1)}, f32[16,32,32]{2,1,0:T(8,128)}, u32[]{:S(2)}) copy-start(f32[16,32,32]{2,1,0:T(8,128)} %schur.1) | copy-start | bytes 196612
  35.2 7.3 %collective-permute-start = (f32[17,8,128]{2,1,0:T(8,128)S(1)}, f32[17,8,128]{2,1,0:T(8,128)S(1)}, u32[]{:S(2)}, u32[]{:S(2)}) collective-permute-start(f32[17,8,128]{2,1,0:T(8,128)S(1)} %get-tuple-element.30), channel_id=1, source_target_pairs={{0,4},{4,8},{8,12},{12,16},{16,20},{20,24},{24,28},{28,0},{1,5},{5... | collective-permute-start | bytes 208904 | tf_op jit(solution)/shard_map/ppermute | solution.py:437
  36.9 5.6 %collective-permute-start.1 = (f32[17,8,128]{2,1,0:T(8,128)S(1)}, f32[17,8,128]{2,1,0:T(8,128)S(1)}, u32[]{:S(2)}, u32[]{:S(2)}) collective-permute-start(f32[17,8,128]{2,1,0:T(8,128)S(1)} %get-tuple-element.31), channel_id=1, source_target_pairs={{0,28},{4,0},{8,4},{12,8},{16,12},{20,16},{24,20},{28,24},{1,29},{... | collective-permute-start | bytes 208904 | tf_op jit(solution)/shard_map/ppermute | solution.py:437
  43.9 4.5 %collective-permute-start.2 = (f32[17,8,128]{2,1,0:T(8,128)S(1)}, f32[17,8,128]{2,1,0:T(8,128)S(1)}, u32[]{:S(2)}, u32[]{:S(2)}) collective-permute-start(f32[17,8,128]{2,1,0:T(8,128)S(1)} %get-tuple-element.39), channel_id=1, source_target_pairs={{0,1},{1,2},{2,3},{3,0},{4,5},{5,6},{6,7},{7,4},{8,9},{9,10},{10,1... | collective-permute-start | bytes 208904 | tf_op jit(solution)/shard_map/ppermute | solution.py:437
  45.3 3.2 %collective-permute-start.3 = (f32[17,8,128]{2,1,0:T(8,128)S(1)}, f32[17,8,128]{2,1,0:T(8,128)S(1)}, u32[]{:S(2)}, u32[]{:S(2)}) collective-permute-start(f32[17,8,128]{2,1,0:T(8,128)S(1)} %get-tuple-element.40), channel_id=1, source_target_pairs={{0,3},{1,0},{2,1},{3,2},{4,7},{5,4},{6,5},{7,6},{8,11},{9,8},{10,9... | collective-permute-start | bytes 208904 | tf_op jit(solution)/shard_map/ppermute | solution.py:437
  69.4 20.5 %copy-start.4 = (f32[128,128]{1,0:T(8,128)S(1)}, f32[128,128]{1,0:T(8,128)}, u32[]{:S(2)}) copy-start(f32[128,128]{1,0:T(8,128)} %constant.6.table) | copy-start | bytes 196612

commit v5 on v4

--- a/solution.py
+++ b/solution.py
@@ -25,6 +25,7 @@
 XL = 256
 SLOT = DEEP * ELY
 UNROLL = 8
+TERMS = ((0, 0), (0, 1), (1, 0), (1, 1), (0, 2), (2, 0))
 QUAD = 4
 CHUNKS = 3
 HIGHEST = lax.Precision.HIGHEST
@@ -46,14 +47,13 @@
     row, col = lane // PITCH, lane % PITCH
     valid = row < XROWS
     middle = valid & (col >= DEEP) & (col < DEEP + ELY)
-    right = col >= DEEP + ELY
     spread = np.where(middle, row * ELY + col - DEEP, -1)
-    turn = np.where(right, SLOT + row * DEEP + col - DEEP - ELY, row * DEEP + col)
+    turn = row * DEEP + np.where(col < DEEP, col, EL + col - DEEP - ELY)
     turn = np.where(valid & ~middle, turn, -1)
     at = lane % SLOT
-    send = at // DEEP * ELY + at % DEEP + np.where(lane >= SLOT, ELY - DEEP, 0)
-    send = np.where((at < DEEP * XROWS) & (lane < 2 * SLOT), send, -1)
-    return np.stack([spread, turn, send, row, col, row, row, row]).astype(np.int32)
+    send = at // DEEP * ELY + at % DEEP + np.where(lane >= EL, ELY - DEEP, 0)
+    send = np.where(at < DEEP * XROWS, send, -1)
+    return np.stack([spread, turn, send, row, col, lane % EL // SLOT, row, row]).astype(np.int32)
 
 
 def pick(values, index):
@@ -68,11 +68,15 @@
     return jnp.where(lax.broadcasted_iota(jnp.int32, (size, index.shape[1]), 0) == index, 1.0, 0.0).astype(F32)
 
 
-def take(values, chosen):
+def three_parts(values):
     high = values.astype(jnp.bfloat16)
     rest = values - high.astype(F32)
     middle = rest.astype(jnp.bfloat16)
-    low = (rest - middle.astype(F32)).astype(jnp.bfloat16)
+    return high, middle, (rest - middle.astype(F32)).astype(jnp.bfloat16)
+
+
+def take(values, chosen):
+    high, middle, low = three_parts(values)
     chosen = chosen.astype(jnp.bfloat16)
 
     def product(part):
@@ -215,7 +219,7 @@
         turned[q] = jnp.transpose(wide[...])[0 : turned.shape[1]]
 
 
-def columns_kernel(condensed, scale, low, high, table, left, right, middle, sent):
+def columns_kernel(condensed, scale, low, high, table, left, right, middle):
     lane = lax.broadcasted_iota(jnp.int32, (8, EL), 1)
     slot = lane // SLOT
     inner, outer = slot == 0, slot == 1
@@ -243,51 +247,43 @@
         return 0
 
     lax.fori_loop(0, MODES, mode, 0, unroll=UNROLL)
-    send = selection(table[2:3, 0:EL], XL)
-    sent[...] = take(middle[...].reshape((MODES + 1) * NB, XL), send)
-
-    def message(m, _):
-        t = [sent[pl.ds(pl.multiple_of(m * NB + 8 * i, 8), 8), :] for i in range(4)]
-        to_left, to_right = t[0], t[1]
-        for i in range(1, 4):
-            to_left = jnp.where(slot == i, pltpu.roll(t[i], SLOT * i, 1), to_left)
-        for i in (0, 2, 3):
-            to_right = jnp.where(slot == i, pltpu.roll(t[i], (SLOT * i - SLOT) % EL, 1), to_right)
-        left[m], right[m] = to_left, to_right
-        return 0
-
-    lax.fori_loop(0, MODES + 1, message, 0, unroll=UNROLL)
-
-
-def middle_kernel(middle, schur, table, block, matrix):
-    lane = lax.broadcasted_iota(jnp.int32, (NB, NB), 1)
-    across = jnp.where((lane >= 16) & (lane % 8 > 0), lane // 8 * 8 + 8 - lane % 8, lane)
-
-    def mode(m, _):
-        rows = both_ascending(schur[m])
-        matrix[m] = jnp.take_along_axis(rows, across, axis=1, mode="promise_in_bounds")
-        return 0
-
-    lax.fori_loop(0, MODES, mode, 0, unroll=UNROLL)
+    total = 0.0
+    for i in range(4):
+        send = selection(jnp.where(table[5:6] == i, table[2:3], -1), XL)
+        total = total + take(middle[:, 8 * i : 8 * i + 8, :].reshape((MODES + 1) * 8, XL), send)
+    left[...] = total[:, 0:EL].reshape(MODES + 1, 8, EL)
+    right[...] = total[:, EL:XL].reshape(MODES + 1, 8, EL)
+
+
+def middle_kernel(middle, table, block):
     spread = take(middle[...].reshape((MODES + 1) * NB, XL), selection(table[0:1], XL))
     block[...] = spread.reshape(MODES + 1, NB, XL)
 
 
+def matrices_kernel(schur, matrix, shift):
+    lane = lax.broadcasted_iota(jnp.int32, (NB, NB), 1)
+    eye = lax.broadcasted_iota(jnp.int32, (NB, NB), 0) == lane
+    across = jnp.where((lane >= 16) & (lane % 8 > 0), lane // 8 * 8 + 8 - lane % 8, lane)
+
+    def mode(m, _):
+        trace = jnp.sum(jnp.sum(jnp.where(eye, schur[m], 0.0), axis=0, keepdims=True), axis=1, keepdims=True)
+        shift[m] = jnp.broadcast_to((0.5 * NB) / trace, (8, XL))
+        rows = both_ascending(schur[m])
+        parts = three_parts(jnp.take_along_axis(rows, across, axis=1, mode="promise_in_bounds"))
+        for k, (part, _) in enumerate(TERMS):
+            matrix[m, :, NB * k : NB * k + NB] = parts[part]
+        return 0
+
+    lax.fori_loop(0, MODES, mode, 0, unroll=UNROLL)
+
+
 def krylov_kernel(
-    block, left, right, schur, table, basis, sums, keep_ref, weight_ref, mine_ref, parts, state, applied, pairs, spread
+    block, left, right, schur, shift, table, basis, sums, keep_ref, weight_ref, mine_ref, parts, state, applied, spread
 ):
-    half = lax.broadcasted_iota(jnp.int32, (8, EL), 1) < SLOT
-
-    def pair_up(m, _):
-        low, high = left[m], right[m]
-        for i in range(4):
-            below = low if i == 0 else pltpu.roll(low, EL - SLOT * i, 1)
-            above = high if i == 1 else pltpu.roll(high, (EL + SLOT - SLOT * i) % EL, 1)
-            pairs[pl.ds(pl.multiple_of(m * NB + 8 * i, 8), 8), :] = jnp.where(half, below, above)
-        return 0
-
-    lax.fori_loop(0, MODES + 1, pair_up, 0, unroll=UNROLL)
-    spread[...] = take(pairs[...], selection(table[1:2], EL))
+    sides = jnp.concatenate([left[...].reshape((MODES + 1) * 8, EL), right[...].reshape((MODES + 1) * 8, EL)], 1)
+    for i in range(4):
+        turn = selection(jnp.where(table[1:2] < 0, -1, table[1:2] + SLOT * i), XL)
+        spread[:, 8 * i : 8 * i + 8, :] = take(sides, turn).reshape(MODES + 1, 8, XL)
 
     row, col = jnp.broadcast_to(table[3:4], (8, XL)), jnp.broadcast_to(table[4:5], (8, XL))
     grid_row = row - DEEP + lax.axis_index("ex") * ELX
@@ -303,28 +299,31 @@
         keep = jnp.where(inside & ~(edge | (corner & other)), 1.0, 0.0).astype(F32)
         keep_ref[8 * tile : 8 * tile + 8] = keep
         weight_ref[8 * tile : 8 * tile + 8] = jnp.where(own, keep * jnp.where(corner, 0.25, 0.5), 0.0).astype(F32)
-    scale = jnp.where(inside[0:1], block[MODES, 0:1] + spread[MODES * NB : MODES * NB + 1], 0.0)
+    scale = jnp.where(inside[0:1], block[MODES, 0:1] + spread[MODES, 0:1], 0.0)
 
     def assemble(values):
         return keep_ref[...] * jnp.concatenate(add_columns(add_rows(tiles(values), PITCH, None, None), None, None), 0)
 
-    eye = lax.broadcasted_iota(jnp.int32, (NB, NB), 0) == lax.broadcasted_iota(jnp.int32, (NB, NB), 1)
+    def image(m, values):
+        parts_of = three_parts(values)
+        stacked = jnp.concatenate([parts_of[part] for _, part in TERMS], 0)
+        return scale * lax.dot_general(schur[m], stacked, (((1,), (0,)), ((), ())), preferred_element_type=F32)
+
     def gather_mode(m):
-        values = block[m] + spread[pl.ds(pl.multiple_of(m * NB, NB), NB), :]
+        values = block[m] + spread[m]
         state[0, m] = keep_ref[...] * jnp.concatenate(add_columns(tiles(values), *meets), 0)
 
     def extend_mode(i):
         def run(m):
-            trace = jnp.sum(jnp.sum(jnp.where(eye, schur[m], 0.0), axis=0, keepdims=True), axis=1, keepdims=True)
-            images = scale * dot(schur[m], state[i, m])
+            images = image(m, state[i, m])
             applied[i, m] = images
-            state[i + 1, m] = assemble(images) * ((0.5 * NB) / trace) - state[i, m]
+            state[i + 1, m] = assemble(images) * shift[m, 0:1] - state[i, m]
 
         return run
 
     def sum_mode(m):
         v = [state[i, m] for i in range(3)]
-        w = [applied[0, m], applied[1, m], scale * dot(schur[m], v[2])]
+        w = [applied[0, m], applied[1, m], image(m, v[2])]
         weight, mine = weight_ref[...], mine_ref[0:1]
         weighted = v[1] * weight
         own = [value * mine for value in v]
@@ -467,13 +466,15 @@
     base, turned = call(
         interior_kernel, [(MODES, 56, EL), (MODES // QUAD, 56, QUAD * NB)], [pltpu.VMEM((QUAD * NB, EL), F32)]
     )(spectral, stored, jnp.transpose(inner_inv, (1, 0, 2)).reshape(NI * MODES, NI), couple)
-    low, high, base, turned = lax.optimization_barrier((low, high, base, turned))
-    rows = (MODES + 1) * NB
-    left, right, middle = call(columns_kernel, [message, message, extended], [pltpu.VMEM((rows, EL), F32)])(
+    low, high, base, turned, schur = lax.optimization_barrier((low, high, base, turned, schur))
+    left, right, middle = call(columns_kernel, [message, message, extended])(
         condensed, scale, low, high, table_of_lanes
     )
     left, right = neighbours(left, right, "ey")
-    block, matrix = call(middle_kernel, [extended, (MODES, NB, NB)])(middle, schur, table_of_lanes)
+    matrix, shift = call(
+        matrices_kernel, [pltpu.VMEM((MODES, NB, len(TERMS) * NB), jnp.bfloat16), (MODES, 8, XL)]
+    )(schur)
+    block = call(middle_kernel, extended)(middle, table_of_lanes)
     basis, sums = call(
         krylov_kernel,
         [(3, MODES, NB, XL), (devices, EL)],
@@ -484,10 +485,9 @@
             pltpu.VMEM((EL, EL), F32),
             pltpu.VMEM((3, MODES, NB, XL), F32),
             pltpu.VMEM((2, MODES, NB, XL), F32),
-            pltpu.VMEM((rows, EL), F32),
-            pltpu.VMEM((rows, XL), F32),
+            pltpu.VMEM(extended, F32),
         ],
-    )(block, left, right, matrix, table_of_lanes)
+    )(block, left, right, matrix, shift, table_of_lanes)
     gathered = lax.all_to_all(sums.reshape(devices, 1, EL), ("ex", "ey"), split_axis=0, concat_axis=0, tiled=True)
     modal = call(finish_kernel, (PADDED * MODES, EL), [pltpu.VMEM((3, MODES, EL), F32), pltpu.VMEM((MODES * NB, XL), F32), pltpu.VMEM((MODES // QUAD, QUAD * NB, QUAD * EL), F32)])(
         gathered, basis, base, turned, index

time: 106 us -> 106 us (level)
    pallas_call x10 -> x11, Pallas kernels: 12.9 us -> 13.1 us  [run(): pl.pallas_call(kernel, out_shape=outs if many else outs[0], in_specs=[awa...]
  transfers between devices with their start and end apart: 4 -> 4, of which waited for: 2 -> 1; matrix products, arithmetic and copies ran while one was open for 0% -> 0% of each run, Pallas kernels for 2% -> 3%
where the time goes in v5:
time: 106 us; the launch traced here: 105 us
  blocking collectives  83 us (78%)
  Pallas kernels  13.1 us (12%)
  starting transfers between devices  8.6 us (8%)
    all_to_all x4, blocking collectives, swap(): lax.all_to_all(array, 'fourier', split_axis=0, concat_axis=0, tiled=True)  66.4 us
    all_to_all x1, blocking collectives, on_device(): lax.all_to_all(sums.reshape(devices, 1, EL), ('ex', 'ey'), split_axis=0,...  16.6 us
    pallas_call x11, Pallas kernels, run(): pl.pallas_call(kernel, out_shape=outs if many else outs[0], in_specs=[awa...  13.1 us
    ppermute x2, starting transfers between devices, neighbours(): lax.ppermute(to_low, axis, ring(axis, -1))  5.56 us
    ppermute x2, starting transfers between devices, neighbours(): lax.ppermute(to_high, axis, ring(axis, 1))  3.04 us
  transfers between devices with their start and end apart: 4, of which 1 were waited for; matrix products, arithmetic and copies ran while one was open for 0% of the time, Pallas kernels for 3%

profile of v5, /device:TPU:1, one launch (start us, length us, event | category | flops | bytes accessed | tf_op | source)
XLA Modules:
  0.0 105.3 jit_solution(8191257455663398411)
XLA Ops:
  0.0 0.0 copy-start.5
  0.0 1.2 %enter_kernel.1 = (f32[88,16,128]{2,1,0:T(8,128)S(1)}, s32[8,128]{1,0:T(8,128)S(1)}, s32[8,128]{1,0:T(8,128)S(1)}, f32[8,128]{1,0:T(8,128)S(1)}, f32[8,128]{1,0:T(8,128)S(1)}) custom-call(f32[81,16,128]{2,1,0:T(8,128)} %bitcast.23, f32[1,128]{1,0:T(1,128)} %bitcast.24, s32[1,128]{1,0:T(1,128)} %bitcast.25), custom_call_target="tpu_custom_call" | custom-call | tf_op jit(solution)/shard_map/enter_kernel/pallas_call | solution.py:413
  1.3 17.2 %all_to_all.25 = f32[88,16,128]{2,1,0:T(8,128)S(1)} all-to-all(f32[88,16,128]{2,1,0:T(8,128)S(1)} %get-tuple-element.27), channel_id=1, replica_groups=mesh['fourier'=8,'ex'=8,'ey'=4] {'fourier'}, dimensions={0} | all-to-all | bytes 1441792 | tf_op jit(solution)/shard_map/all_to_all | solution.py:427
  18.5 0.0 copy-start
  18.5 0.0 copy-done.5
  18.5 0.4 transform_kernel.2
  19.0 0.0 copy-start.1
  19.0 0.0 copy-start.3
  19.0 15.1 %all_to_all.26 = f32[88,16,128]{2,1,0:T(8,128)S(1)} all-to-all(f32[88,16,128]{2,1,0:T(8,128)S(1)} %bitcast.17), channel_id=1, replica_groups=mesh['fourier'=8,'ex'=8,'ey'=4] {'fourier'}, dimensions={0} | all-to-all | bytes 1441792 | tf_op jit(solution)/shard_map/all_to_all | solution.py:427
  34.1 0.0 copy-done
  34.1 1.2 %condense_kernel.1 = (f32[16,32,128]{2,1,0:T(8,128)S(1)}, f32[17,8,128]{2,1,0:T(8,128)S(1)}, f32[17,8,128]{2,1,0:T(8,128)S(1)}) custom-call(f32[1408,128]{1,0:T(8,128)S(1)} %bitcast.14, s32[8,128]{1,0:T(8,128)S(1)} %get-tuple-element.28.order, f32[8,128]{1,0:T(8,128)S(1)} %get-tuple-element.29.scale, f32[16,32,49]{2,1,0:T(8,128)S(1)} %copy-done), custom_call_target="tpu_custom_call" | custom-call | tf_op jit(solution)/shard_map/condense_kernel/pallas_call | solution.py:413
  35.2 0.0 copy-start.2
  35.2 1.7 %collective-permute-start = (f32[17,8,128]{2,1,0:T(8,128)S(1)}, f32[17,8,128]{2,1,0:T(8,128)S(1)}, u32[]{:S(2)}, u32[]{:S(2)}) collective-permute-start(f32[17,8,128]{2,1,0:T(8,128)S(1)} %get-tuple-element.31), channel_id=1, source_target_pairs={{0,4},{4,8},{8,12},{12,16},{16,20},{20,24},{24,28},{28,0},{1,5},{5... | collective-permute-start | bytes 208904 | tf_op jit(solution)/shard_map/ppermute | solution.py:436
  36.9 4.0 %collective-permute-start.1 = (f32[17,8,128]{2,1,0:T(8,128)S(1)}, f32[17,8,128]{2,1,0:T(8,128)S(1)}, u32[]{:S(2)}, u32[]{:S(2)}) collective-permute-start(f32[17,8,128]{2,1,0:T(8,128)S(1)} %get-tuple-element.32), channel_id=1, source_target_pairs={{0,28},{4,0},{8,4},{12,8},{16,12},{20,16},{24,20},{28,24},{1,29},{... | collective-permute-start | bytes 208904 | tf_op jit(solution)/shard_map/ppermute | solution.py:436
  40.9 0.0 copy-done.1
  40.9 1.2 %interior_kernel.1 = (f32[16,56,128]{2,1,0:T(8,128)S(1)}, f32[4,56,128]{2,1,0:T(8,128)S(1)}) custom-call(f32[1408,128]{1,0:T(8,128)S(1)} %bitcast.15, f32[8,128]{1,0:T(8,128)S(1)} %get-tuple-element.33.stored, f32[784,49]{1,0:T(8,128)S(1)} %bitcast.21, f32[16,32,49]{2,1,0:T(8,128)S(1)} %copy-done), custom_call_target="tpu_custom_call" | custom-call | tf_op jit(solution)/shard_map/interior_kernel/pallas_call | solution.py:413
  42.1 0.5 collective-permute-done.low
  42.6 0.0 collective-permute-done.1.high
  42.6 0.0 copy-done.3
  42.6 1.1 %columns_kernel.1 = (f32[17,8,128]{2,1,0:T(8,128)S(1)}, f32[17,8,128]{2,1,0:T(8,128)S(1)}, f32[17,32,256]{2,1,0:T(8,128)S(1)}) custom-call(f32[16,32,128]{2,1,0:T(8,128)S(1)} %get-tuple-element.30.condensed, f32[8,128]{1,0:T(8,128)S(1)} %get-tuple-element.29.scale, f32[17,8,128]{2,1,0:T(8,128)S(1)} %collective-permute-done.low, ...), custom_call_target="tpu_custom_call" | custom-call | tf_op jit(solution)/shard_map/columns_kernel/pallas_call | solution.py:413
  43.7 1.4 %collective-permute-start.2 = (f32[17,8,128]{2,1,0:T(8,128)S(1)}, f32[17,8,128]{2,1,0:T(8,128)S(1)}, u32[]{:S(2)}, u32[]{:S(2)}) collective-permute-start(f32[17,8,128]{2,1,0:T(8,128)S(1)} %get-tuple-element.39), channel_id=1, source_target_pairs={{0,1},{1,2},{2,3},{3,0},{4,5},{5,6},{6,7},{7,4},{8,9},{9,10},{10,1... | collective-permute-start | bytes 208904 | tf_op jit(solution)/shard_map/ppermute | solution.py:436
  45.1 1.5 %collective-permute-start.3 = (f32[17,8,128]{2,1,0:T(8,128)S(1)}, f32[17,8,128]{2,1,0:T(8,128)S(1)}, u32[]{:S(2)}, u32[]{:S(2)}) collective-permute-start(f32[17,8,128]{2,1,0:T(8,128)S(1)} %get-tuple-element.40), channel_id=1, source_target_pairs={{0,3},{1,0},{2,1},{3,2},{4,7},{5,4},{6,5},{7,6},{8,11},{9,8},{10,9... | collective-permute-start | bytes 208904 | tf_op jit(solution)/shard_map/ppermute | solution.py:436
  46.6 0.4 middle_kernel.1.block
  47.0 0.0 copy-done.2
  47.0 1.4 %matrices_kernel.1 = (bf16[16,32,192]{2,1,0:T(8,128)(2,1)S(1)}, f32[16,8,256]{2,1,0:T(8,128)S(1)}) custom-call(f32[16,32,32]{2,1,0:T(8,128)S(1)} %copy-done.2), custom_call_target="tpu_custom_call" | custom-call | tf_op jit(solution)/shard_map/matrices_kernel/pallas_call | solution.py:413
  48.4 0.0 collective-permute-done.2.left
  48.4 0.0 collective-permute-done.3.right
  48.4 3.5 %krylov_kernel.1 = (f32[3,16,32,256]{3,2,1,0:T(8,128)S(1)}, f32[32,128]{1,0:T(8,128)S(1)}) custom-call(f32[17,32,256]{2,1,0:T(8,128)S(1)} %middle_kernel.1.block, f32[17,8,128]{2,1,0:T(8,128)S(1)} %collective-permute-done.2.left, f32[17,8,128]{2,1,0:T(8,128)S(1)} %collective-permute-done.3.right, bf16[16,32,192]{2,1,0:T(8,128)(2,1)S(1)} %get-tuple-element.42.schur, ...), custom_call_target="tpu_custom_call" | custom-call | tf_op jit(solution)/shard_map/krylov_kernel/pallas_call | solution.py:413
  51.9 16.6 %all_to_all.27.gathered = f32[32,1,128]{2,1,0:T(1,128)S(1)} all-to-all(f32[32,1,128]{2,1,0:T(1,128)S(1)} %bitcast.22), channel_id=1, replica_groups=mesh['fourier'=8,'ex'=8,'ey'=4] {'ex','ey'}, dimensions={0} | all-to-all | bytes 32768 | tf_op jit(solution)/shard_map/all_to_all | solution.py:491
  68.6 0.0 copy-start.4
  68.6 1.4 %finish_kernel.1 = f32[1408,128]{1,0:T(8,128)S(1)} custom-call(f32[32,1,128]{2,1,0:T(1,128)S(1)} %all_to_all.27.gathered, f32[3,16,32,256]{3,2,1,0:T(8,128)S(1)} %get-tuple-element.45.basis, f32[16,56,128]{2,1,0:T(8,128)S(1)} %get-tuple-element.46.base, f32[4,56,128]{2,1,0:T(8,128)S(1)} %get-tuple-element.47.couple, s32[8,128]{1,0:T(8,128)S(1)} %get-tuple-element.48.cell), custom_call_target="tpu_custom_call" | custom-call | tf_op jit(solution)/shard_map/finish_kernel/pallas_call | solution.py:413
  70.0 19.1 %all_to_all.28 = f32[88,16,128]{2,1,0:T(8,128)S(1)} all-to-all(f32[88,16,128]{2,1,0:T(8,128)S(1)} %bitcast.20), channel_id=1, replica_groups=mesh['fourier'=8,'ex'=8,'ey'=4] {'fourier'}, dimensions={0} | all-to-all | bytes 1441792 | tf_op jit(solution)/shard_map/all_to_all | solution.py:427
  89.1 0.0 copy-done.4
  89.1 0.4 transform_kernel.3
  89.5 14.9 %all_to_all.29.planes = f32[88,16,128]{2,1,0:T(8,128)S(1)} all-to-all(f32[88,16,128]{2,1,0:T(8,128)S(1)} %bitcast.19), channel_id=1, replica_groups=mesh['fourier'=8,'ex'=8,'ey'=4] {'fourier'}, dimensions={0} | all-to-all | bytes 1441792 | tf_op jit(solution)/shard_map/all_to_all | solution.py:427
  104.5 0.9 leave_kernel.1
Async XLA Ops:
  0.0 18.5 %copy-start.5 = (f32[128,128]{1,0:T(8,128)S(1)}, f32[128,128]{1,0:T(8,128)}, u32[]{:S(2)}) copy-start(f32[128,128]{1,0:T(8,128)} %constant.4.clone.table) | copy-start | bytes 196612
  18.5 15.6 %copy-start = (f32[16,32,49]{2,1,0:T(8,128)S(1)}, f32[16,32,49]{2,1,0:T(8,128)}, u32[]{:S(2)}) copy-start(f32[16,32,49]{2,1,0:T(8,128)} %couple.3) | copy-start | bytes 301060
  19.0 22.0 %copy-start.1 = (f32[16,49,49]{2,0,1:T(8,128)S(1)}, f32[16,49,49]{2,0,1:T(8,128)}, u32[]{:S(2)}) copy-start(f32[16,49,49]{2,0,1:T(8,128)} %param.12) | copy-start | bytes 460996
  19.0 23.6 %copy-start.3 = (s32[8,256]{1,0:T(8,128)S(1)}, s32[8,256]{1,0:T(8,128)}, u32[]{:S(2)}) copy-start(s32[8,256]{1,0:T(8,128)} %constant.5.clone.table) | copy-start | bytes 24580
  35.2 11.8 %copy-start.2 = (f32[16,32,32]{2,1,0:T(8,128)S(1)}, f32[16,32,32]{2,1,0:T(8,128)}, u32[]{:S(2)}) copy-start(f32[16,32,32]{2,1,0:T(8,128)} %schur) | copy-start | bytes 196612
  35.2 7.3 %collective-permute-start = (f32[17,8,128]{2,1,0:T(8,128)S(1)}, f32[17,8,128]{2,1,0:T(8,128)S(1)}, u32[]{:S(2)}, u32[]{:S(2)}) collective-permute-start(f32[17,8,128]{2,1,0:T(8,128)S(1)} %get-tuple-element.31), channel_id=1, source_target_pairs={{0,4},{4,8},{8,12},{12,16},{16,20},{20,24},{24,28},{28,0},{1,5},{5... | collective-permute-start | bytes 208904 | tf_op jit(solution)/shard_map/ppermute | solution.py:436
  36.9 5.6 %collective-permute-start.1 = (f32[17,8,128]{2,1,0:T(8,128)S(1)}, f32[17,8,128]{2,1,0:T(8,128)S(1)}, u32[]{:S(2)}, u32[]{:S(2)}) collective-permute-start(f32[17,8,128]{2,1,0:T(8,128)S(1)} %get-tuple-element.32), channel_id=1, source_target_pairs={{0,28},{4,0},{8,4},{12,8},{16,12},{20,16},{24,20},{28,24},{1,29},{... | collective-permute-start | bytes 208904 | tf_op jit(solution)/shard_map/ppermute | solution.py:436
  43.7 4.7 %collective-permute-start.2 = (f32[17,8,128]{2,1,0:T(8,128)S(1)}, f32[17,8,128]{2,1,0:T(8,128)S(1)}, u32[]{:S(2)}, u32[]{:S(2)}) collective-permute-start(f32[17,8,128]{2,1,0:T(8,128)S(1)} %get-tuple-element.39), channel_id=1, source_target_pairs={{0,1},{1,2},{2,3},{3,0},{4,5},{5,6},{6,7},{7,4},{8,9},{9,10},{10,1... | collective-permute-start | bytes 208904 | tf_op jit(solution)/shard_map/ppermute | solution.py:436
  45.1 3.3 %collective-permute-start.3 = (f32[17,8,128]{2,1,0:T(8,128)S(1)}, f32[17,8,128]{2,1,0:T(8,128)S(1)}, u32[]{:S(2)}, u32[]{:S(2)}) collective-permute-start(f32[17,8,128]{2,1,0:T(8,128)S(1)} %get-tuple-element.40), channel_id=1, source_target_pairs={{0,3},{1,0},{2,1},{3,2},{4,7},{5,4},{6,5},{7,6},{8,11},{9,8},{10,9... | collective-permute-start | bytes 208904 | tf_op jit(solution)/shard_map/ppermute | solution.py:436
  68.6 20.5 %copy-start.4 = (f32[128,128]{1,0:T(8,128)S(1)}, f32[128,128]{1,0:T(8,128)}, u32[]{:S(2)}) copy-start(f32[128,128]{1,0:T(8,128)} %constant.6.table) | copy-start | bytes 196612

commit v6 on v5

--- a/solution.py
+++ b/solution.py
@@ -24,7 +24,7 @@
 PITCH = XCOLS
 XL = 256
 SLOT = DEEP * ELY
-UNROLL = 8
+UNROLL = 16
 TERMS = ((0, 0), (0, 1), (1, 0), (1, 1), (0, 2), (2, 0))
 QUAD = 4
 CHUNKS = 3

time: 106 us -> 103 us (0.972)
  Pallas kernels: 13.1 us -> 10.5 us
    pallas_call x11, Pallas kernels: 13.1 us -> 10.5 us  [run(): pl.pallas_call(kernel, out_shape=outs if many else outs[0], in_specs=[awa...]
where the time goes in v6:
time: 103 us
  blocking collectives  83.1 us (81%)
  Pallas kernels  10.5 us (10%)
  starting transfers between devices  8.6 us (8%)
    all_to_all x4, blocking collectives, swap(): lax.all_to_all(array, 'fourier', split_axis=0, concat_axis=0, tiled=True)  66.4 us
    all_to_all x1, blocking collectives, on_device(): lax.all_to_all(sums.reshape(devices, 1, EL), ('ex', 'ey'), split_axis=0,...  16.7 us
    pallas_call x11, Pallas kernels, run(): pl.pallas_call(kernel, out_shape=outs if many else outs[0], in_specs=[awa...  10.5 us
    ppermute x2, starting transfers between devices, neighbours(): lax.ppermute(to_low, axis, ring(axis, -1))  5.56 us
    ppermute x2, starting transfers between devices, neighbours(): lax.ppermute(to_high, axis, ring(axis, 1))  3.04 us
  transfers between devices with their start and end apart: 4, of which 1 were waited for; matrix products, arithmetic and copies ran while one was open for 0% of the time, Pallas kernels for 3%

profile of v6, /device:TPU:1, one launch (start us, length us, event | category | flops | bytes accessed | tf_op | source)
XLA Modules:
  0.0 103.1 jit_solution(16407425600454587743)
XLA Ops:
  0.0 0.0 copy-start.5
  0.0 1.2 %enter_kernel.1 = (f32[88,16,128]{2,1,0:T(8,128)S(1)}, s32[8,128]{1,0:T(8,128)S(1)}, s32[8,128]{1,0:T(8,128)S(1)}, f32[8,128]{1,0:T(8,128)S(1)}, f32[8,128]{1,0:T(8,128)S(1)}) custom-call(f32[81,16,128]{2,1,0:T(8,128)} %bitcast.23, f32[1,128]{1,0:T(1,128)} %bitcast.24, s32[1,128]{1,0:T(1,128)} %bitcast.25), custom_call_target="tpu_custom_call" | custom-call | tf_op jit(solution)/shard_map/enter_kernel/pallas_call | solution.py:413
  1.3 17.2 %all_to_all.25 = f32[88,16,128]{2,1,0:T(8,128)S(1)} all-to-all(f32[88,16,128]{2,1,0:T(8,128)S(1)} %get-tuple-element.27), channel_id=1, replica_groups=mesh['fourier'=8,'ex'=8,'ey'=4] {'fourier'}, dimensions={0} | all-to-all | bytes 1441792 | tf_op jit(solution)/shard_map/all_to_all | solution.py:427
  18.5 0.0 copy-start
  18.5 0.0 copy-done.5
  18.5 0.4 transform_kernel.2
  19.0 0.0 copy-start.1
  19.0 0.0 copy-start.3
  19.0 15.1 %all_to_all.26 = f32[88,16,128]{2,1,0:T(8,128)S(1)} all-to-all(f32[88,16,128]{2,1,0:T(8,128)S(1)} %bitcast.17), channel_id=1, replica_groups=mesh['fourier'=8,'ex'=8,'ey'=4] {'fourier'}, dimensions={0} | all-to-all | bytes 1441792 | tf_op jit(solution)/shard_map/all_to_all | solution.py:427
  34.1 0.0 copy-done
  34.1 0.7 condense_kernel.1
  34.8 0.0 copy-start.2
  34.8 1.7 %collective-permute-start = (f32[17,8,128]{2,1,0:T(8,128)S(1)}, f32[17,8,128]{2,1,0:T(8,128)S(1)}, u32[]{:S(2)}, u32[]{:S(2)}) collective-permute-start(f32[17,8,128]{2,1,0:T(8,128)S(1)} %get-tuple-element.31), channel_id=1, source_target_pairs={{0,4},{4,8},{8,12},{12,16},{16,20},{20,24},{24,28},{28,0},{1,5},{5... | collective-permute-start | bytes 208904 | tf_op jit(solution)/shard_map/ppermute | solution.py:436
  36.4 4.0 %collective-permute-start.1 = (f32[17,8,128]{2,1,0:T(8,128)S(1)}, f32[17,8,128]{2,1,0:T(8,128)S(1)}, u32[]{:S(2)}, u32[]{:S(2)}) collective-permute-start(f32[17,8,128]{2,1,0:T(8,128)S(1)} %get-tuple-element.32), channel_id=1, source_target_pairs={{0,28},{4,0},{8,4},{12,8},{16,12},{20,16},{24,20},{28,24},{1,29},{... | collective-permute-start | bytes 208904 | tf_op jit(solution)/shard_map/ppermute | solution.py:436
  40.5 0.0 copy-done.1
  40.5 0.9 interior_kernel.1
  41.4 0.7 collective-permute-done.low
  42.1 0.0 collective-permute-done.1.high
  42.1 0.0 copy-done.3
  42.1 0.8 columns_kernel.1
  42.9 1.4 %collective-permute-start.2 = (f32[17,8,128]{2,1,0:T(8,128)S(1)}, f32[17,8,128]{2,1,0:T(8,128)S(1)}, u32[]{:S(2)}, u32[]{:S(2)}) collective-permute-start(f32[17,8,128]{2,1,0:T(8,128)S(1)} %get-tuple-element.39), channel_id=1, source_target_pairs={{0,1},{1,2},{2,3},{3,0},{4,5},{5,6},{6,7},{7,4},{8,9},{9,10},{10,1... | collective-permute-start | bytes 208904 | tf_op jit(solution)/shard_map/ppermute | solution.py:436
  44.2 1.5 %collective-permute-start.3 = (f32[17,8,128]{2,1,0:T(8,128)S(1)}, f32[17,8,128]{2,1,0:T(8,128)S(1)}, u32[]{:S(2)}, u32[]{:S(2)}) collective-permute-start(f32[17,8,128]{2,1,0:T(8,128)S(1)} %get-tuple-element.40), channel_id=1, source_target_pairs={{0,3},{1,0},{2,1},{3,2},{4,7},{5,4},{6,5},{7,6},{8,11},{9,8},{10,9... | collective-permute-start | bytes 208904 | tf_op jit(solution)/shard_map/ppermute | solution.py:436
  45.8 0.4 middle_kernel.1.block
  46.2 0.0 copy-done.2
  46.2 1.3 %matrices_kernel.1 = (bf16[16,32,192]{2,1,0:T(8,128)(2,1)S(1)}, f32[16,8,256]{2,1,0:T(8,128)S(1)}) custom-call(f32[16,32,32]{2,1,0:T(8,128)S(1)} %copy-done.2), custom_call_target="tpu_custom_call" | custom-call | tf_op jit(solution)/shard_map/matrices_kernel/pallas_call | solution.py:413
  47.5 0.0 collective-permute-done.2.left
  47.5 0.0 collective-permute-done.3.right
  47.5 2.3 %krylov_kernel.1 = (f32[3,16,32,256]{3,2,1,0:T(8,128)S(1)}, f32[32,128]{1,0:T(8,128)S(1)}) custom-call(f32[17,32,256]{2,1,0:T(8,128)S(1)} %middle_kernel.1.block, f32[17,8,128]{2,1,0:T(8,128)S(1)} %collective-permute-done.2.left, f32[17,8,128]{2,1,0:T(8,128)S(1)} %collective-permute-done.3.right, bf16[16,32,192]{2,1,0:T(8,128)(2,1)S(1)} %get-tuple-element.42.schur, ...), custom_call_target="tpu_custom_call" | custom-call | tf_op jit(solution)/shard_map/krylov_kernel/pallas_call | solution.py:413
  49.8 16.7 %all_to_all.27.gathered = f32[32,1,128]{2,1,0:T(1,128)S(1)} all-to-all(f32[32,1,128]{2,1,0:T(1,128)S(1)} %bitcast.22), channel_id=1, replica_groups=mesh['fourier'=8,'ex'=8,'ey'=4] {'ex','ey'}, dimensions={0} | all-to-all | bytes 32768 | tf_op jit(solution)/shard_map/all_to_all | solution.py:491
  66.5 0.0 copy-start.4
  66.5 1.2 %finish_kernel.1 = f32[1408,128]{1,0:T(8,128)S(1)} custom-call(f32[32,1,128]{2,1,0:T(1,128)S(1)} %all_to_all.27.gathered, f32[3,16,32,256]{3,2,1,0:T(8,128)S(1)} %get-tuple-element.45.basis, f32[16,56,128]{2,1,0:T(8,128)S(1)} %get-tuple-element.46.base, f32[4,56,128]{2,1,0:T(8,128)S(1)} %get-tuple-element.47.couple, s32[8,128]{1,0:T(8,128)S(1)} %get-tuple-element.48.cell), custom_call_target="tpu_custom_call" | custom-call | tf_op jit(solution)/shard_map/finish_kernel/pallas_call | solution.py:413
  67.7 19.1 %all_to_all.28 = f32[88,16,128]{2,1,0:T(8,128)S(1)} all-to-all(f32[88,16,128]{2,1,0:T(8,128)S(1)} %bitcast.20), channel_id=1, replica_groups=mesh['fourier'=8,'ex'=8,'ey'=4] {'fourier'}, dimensions={0} | all-to-all | bytes 1441792 | tf_op jit(solution)/shard_map/all_to_all | solution.py:427
  86.8 0.0 copy-done.4
  86.8 0.4 transform_kernel.3
  87.3 14.9 %all_to_all.29.planes = f32[88,16,128]{2,1,0:T(8,128)S(1)} all-to-all(f32[88,16,128]{2,1,0:T(8,128)S(1)} %bitcast.19), channel_id=1, replica_groups=mesh['fourier'=8,'ex'=8,'ey'=4] {'fourier'}, dimensions={0} | all-to-all | bytes 1441792 | tf_op jit(solution)/shard_map/all_to_all | solution.py:427
  102.2 0.9 leave_kernel.1
Async XLA Ops:
  0.0 18.5 %copy-start.5 = (f32[128,128]{1,0:T(8,128)S(1)}, f32[128,128]{1,0:T(8,128)}, u32[]{:S(2)}) copy-start(f32[128,128]{1,0:T(8,128)} %constant.4.clone.table) | copy-start | bytes 196612
  18.5 15.6 %copy-start = (f32[16,32,49]{2,1,0:T(8,128)S(1)}, f32[16,32,49]{2,1,0:T(8,128)}, u32[]{:S(2)}) copy-start(f32[16,32,49]{2,1,0:T(8,128)} %couple.3) | copy-start | bytes 301060
  19.0 21.5 %copy-start.1 = (f32[16,49,49]{2,0,1:T(8,128)S(1)}, f32[16,49,49]{2,0,1:T(8,128)}, u32[]{:S(2)}) copy-start(f32[16,49,49]{2,0,1:T(8,128)} %param.12) | copy-start | bytes 460996
  19.0 23.1 %copy-start.3 = (s32[8,256]{1,0:T(8,128)S(1)}, s32[8,256]{1,0:T(8,128)}, u32[]{:S(2)}) copy-start(s32[8,256]{1,0:T(8,128)} %constant.5.clone.table) | copy-start | bytes 24580
  34.8 11.4 %copy-start.2 = (f32[16,32,32]{2,1,0:T(8,128)S(1)}, f32[16,32,32]{2,1,0:T(8,128)}, u32[]{:S(2)}) copy-start(f32[16,32,32]{2,1,0:T(8,128)} %schur) | copy-start | bytes 196612
  34.8 7.3 %collective-permute-start = (f32[17,8,128]{2,1,0:T(8,128)S(1)}, f32[17,8,128]{2,1,0:T(8,128)S(1)}, u32[]{:S(2)}, u32[]{:S(2)}) collective-permute-start(f32[17,8,128]{2,1,0:T(8,128)S(1)} %get-tuple-element.31), channel_id=1, source_target_pairs={{0,4},{4,8},{8,12},{12,16},{16,20},{20,24},{24,28},{28,0},{1,5},{5... | collective-permute-start | bytes 208904 | tf_op jit(solution)/shard_map/ppermute | solution.py:436
  36.4 5.6 %collective-permute-start.1 = (f32[17,8,128]{2,1,0:T(8,128)S(1)}, f32[17,8,128]{2,1,0:T(8,128)S(1)}, u32[]{:S(2)}, u32[]{:S(2)}) collective-permute-start(f32[17,8,128]{2,1,0:T(8,128)S(1)} %get-tuple-element.32), channel_id=1, source_target_pairs={{0,28},{4,0},{8,4},{12,8},{16,12},{20,16},{24,20},{28,24},{1,29},{... | collective-permute-start | bytes 208904 | tf_op jit(solution)/shard_map/ppermute | solution.py:436
  42.9 4.6 %collective-permute-start.2 = (f32[17,8,128]{2,1,0:T(8,128)S(1)}, f32[17,8,128]{2,1,0:T(8,128)S(1)}, u32[]{:S(2)}, u32[]{:S(2)}) collective-permute-start(f32[17,8,128]{2,1,0:T(8,128)S(1)} %get-tuple-element.39), channel_id=1, source_target_pairs={{0,1},{1,2},{2,3},{3,0},{4,5},{5,6},{6,7},{7,4},{8,9},{9,10},{10,1... | collective-permute-start | bytes 208904 | tf_op jit(solution)/shard_map/ppermute | solution.py:436
  44.2 3.3 %collective-permute-start.3 = (f32[17,8,128]{2,1,0:T(8,128)S(1)}, f32[17,8,128]{2,1,0:T(8,128)S(1)}, u32[]{:S(2)}, u32[]{:S(2)}) collective-permute-start(f32[17,8,128]{2,1,0:T(8,128)S(1)} %get-tuple-element.40), channel_id=1, source_target_pairs={{0,3},{1,0},{2,1},{3,2},{4,7},{5,4},{6,5},{7,6},{8,11},{9,8},{10,9... | collective-permute-start | bytes 208904 | tf_op jit(solution)/shard_map/ppermute | solution.py:436
  66.5 20.3 %copy-start.4 = (f32[128,128]{1,0:T(8,128)S(1)}, f32[128,128]{1,0:T(8,128)}, u32[]{:S(2)}) copy-start(f32[128,128]{1,0:T(8,128)} %constant.6.table) | copy-start | bytes 196612

commit v7 on v6

--- a/solution.py
+++ b/solution.py
@@ -27,7 +27,7 @@
 UNROLL = 16
 TERMS = ((0, 0), (0, 1), (1, 0), (1, 1), (0, 2), (2, 0))
 QUAD = 4
-CHUNKS = 3
+CHUNKS = 1
 HIGHEST = lax.Precision.HIGHEST
 F32 = jnp.float32
 
@@ -377,22 +377,20 @@
         coefs[i] = jnp.transpose(jnp.broadcast_to(c[0:1], (EL, EL)))[0:MODES]
     place = (cell[0:1] // ELY + DEEP) * PITCH + cell[0:1] % ELY + DEEP
 
-    def combine(m, _):
-        c = [jnp.concatenate([coefs[i, pl.ds(m, 1), :]] * 2, 1) for i in range(3)]
-        x = c[0] * basis[0, m] + c[1] * basis[1, m] + c[2] * basis[2, m]
-        mixed[pl.ds(pl.multiple_of(m * NB, NB), NB), :] = both_ascending(x)
-        return 0
-
-    lax.fori_loop(0, MODES, combine, 0, unroll=UNROLL)
-    solved = take(mixed[...], selection(place, XL))
+    chosen = selection(place, XL)
     blocks[...] = jnp.zeros_like(blocks)
-    for m in range(MODES):
-        x = solved[m * NB : m * NB + NB]
-        q, r = m // QUAD, m % QUAD
-        blocks[q, NB * r : NB * r + NB, EL * r : EL * r + EL] = x
-        for tile in range(4):
-            out[pl.ds(8 * tile * MODES + m, 8, stride=MODES), :] = x[8 * tile : 8 * tile + 8]
     for q in range(MODES // QUAD):
+        for r in range(QUAD):
+            m = QUAD * q + r
+            c = [jnp.concatenate([coefs[i, m : m + 1, :]] * 2, 1) for i in range(3)]
+            x = c[0] * basis[0, m] + c[1] * basis[1, m] + c[2] * basis[2, m]
+            mixed[m * NB : m * NB + NB, :] = both_ascending(x)
+        solved = take(mixed[QUAD * q * NB : QUAD * (q + 1) * NB, :], chosen)
+        for r in range(QUAD):
+            x = solved[r * NB : r * NB + NB]
+            blocks[q, NB * r : NB * r + NB, EL * r : EL * r + EL] = x
+            for tile in range(4):
+                out[pl.ds(8 * tile * MODES + QUAD * q + r, 8, stride=MODES), :] = x[8 * tile : 8 * tile + 8]
         lifted = dot_of_parts(split(couple[q]), split(blocks[q]))
         for r in range(QUAD):
             m = QUAD * q + r

time: 103 us -> 103 us (level)
  no operation moved by 1% of the time
where the time goes in v7:
time: 103 us
  blocking collectives  83.1 us (81%)
  Pallas kernels  10.2 us (10%)
  starting transfers between devices  8.6 us (8%)
    all_to_all x4, blocking collectives, swap(): lax.all_to_all(array, 'fourier', split_axis=0, concat_axis=0, tiled=True)  66.4 us
    all_to_all x1, blocking collectives, on_device(): lax.all_to_all(sums.reshape(devices, 1, EL), ('ex', 'ey'), split_axis=0,...  16.7 us
    pallas_call x11, Pallas kernels, run(): pl.pallas_call(kernel, out_shape=outs if many else outs[0], in_specs=[awa...  10.2 us
    ppermute x2, starting transfers between devices, neighbours(): lax.ppermute(to_low, axis, ring(axis, -1))  5.56 us
    ppermute x2, starting transfers between devices, neighbours(): lax.ppermute(to_high, axis, ring(axis, 1))  3.04 us
  transfers between devices with their start and end apart: 4, of which 1 were waited for; matrix products, arithmetic and copies ran while one was open for 0% of the time, Pallas kernels for 3%

profile of v7, /device:TPU:1, one launch (start us, length us, event | category | flops | bytes accessed | tf_op | source)
XLA Modules:
  0.0 102.8 jit_solution(8776925514719319334)
XLA Ops:
  0.0 0.0 copy-start.5
  0.0 1.2 %enter_kernel.1 = (f32[88,16,128]{2,1,0:T(8,128)S(1)}, s32[8,128]{1,0:T(8,128)S(1)}, s32[8,128]{1,0:T(8,128)S(1)}, f32[8,128]{1,0:T(8,128)S(1)}, f32[8,128]{1,0:T(8,128)S(1)}) custom-call(f32[81,16,128]{2,1,0:T(8,128)} %bitcast.23, f32[1,128]{1,0:T(1,128)} %bitcast.24, s32[1,128]{1,0:T(1,128)} %bitcast.25), custom_call_target="tpu_custom_call" | custom-call | tf_op jit(solution)/shard_map/enter_kernel/pallas_call | solution.py:411
  1.2 17.2 %all_to_all.25 = f32[88,16,128]{2,1,0:T(8,128)S(1)} all-to-all(f32[88,16,128]{2,1,0:T(8,128)S(1)} %get-tuple-element.27), channel_id=1, replica_groups=mesh['fourier'=8,'ex'=8,'ey'=4] {'fourier'}, dimensions={0} | all-to-all | bytes 1441792 | tf_op jit(solution)/shard_map/all_to_all | solution.py:425
  18.4 0.0 copy-start
  18.4 0.0 copy-done.5
  18.4 0.4 transform_kernel.2
  18.9 0.0 copy-start.1
  18.9 0.0 copy-start.3
  18.9 15.1 %all_to_all.26 = f32[88,16,128]{2,1,0:T(8,128)S(1)} all-to-all(f32[88,16,128]{2,1,0:T(8,128)S(1)} %bitcast.17), channel_id=1, replica_groups=mesh['fourier'=8,'ex'=8,'ey'=4] {'fourier'}, dimensions={0} | all-to-all | bytes 1441792 | tf_op jit(solution)/shard_map/all_to_all | solution.py:425
  34.0 0.0 copy-done
  34.0 0.7 condense_kernel.1
  34.7 0.0 copy-start.2
  34.7 1.7 %collective-permute-start = (f32[17,8,128]{2,1,0:T(8,128)S(1)}, f32[17,8,128]{2,1,0:T(8,128)S(1)}, u32[]{:S(2)}, u32[]{:S(2)}) collective-permute-start(f32[17,8,128]{2,1,0:T(8,128)S(1)} %get-tuple-element.31), channel_id=1, source_target_pairs={{0,4},{4,8},{8,12},{12,16},{16,20},{20,24},{24,28},{28,0},{1,5},{5... | collective-permute-start | bytes 208904 | tf_op jit(solution)/shard_map/ppermute | solution.py:434
  36.3 4.0 %collective-permute-start.1 = (f32[17,8,128]{2,1,0:T(8,128)S(1)}, f32[17,8,128]{2,1,0:T(8,128)S(1)}, u32[]{:S(2)}, u32[]{:S(2)}) collective-permute-start(f32[17,8,128]{2,1,0:T(8,128)S(1)} %get-tuple-element.32), channel_id=1, source_target_pairs={{0,28},{4,0},{8,4},{12,8},{16,12},{20,16},{24,20},{28,24},{1,29},{... | collective-permute-start | bytes 208904 | tf_op jit(solution)/shard_map/ppermute | solution.py:434
  40.4 0.0 copy-done.1
  40.4 0.9 interior_kernel.1
  41.3 0.7 collective-permute-done.low
  42.0 0.0 collective-permute-done.1.high
  42.0 0.0 copy-done.3
  42.0 0.8 columns_kernel.1
  42.8 1.4 %collective-permute-start.2 = (f32[17,8,128]{2,1,0:T(8,128)S(1)}, f32[17,8,128]{2,1,0:T(8,128)S(1)}, u32[]{:S(2)}, u32[]{:S(2)}) collective-permute-start(f32[17,8,128]{2,1,0:T(8,128)S(1)} %get-tuple-element.39), channel_id=1, source_target_pairs={{0,1},{1,2},{2,3},{3,0},{4,5},{5,6},{6,7},{7,4},{8,9},{9,10},{10,1... | collective-permute-start | bytes 208904 | tf_op jit(solution)/shard_map/ppermute | solution.py:434
  44.1 1.5 %collective-permute-start.3 = (f32[17,8,128]{2,1,0:T(8,128)S(1)}, f32[17,8,128]{2,1,0:T(8,128)S(1)}, u32[]{:S(2)}, u32[]{:S(2)}) collective-permute-start(f32[17,8,128]{2,1,0:T(8,128)S(1)} %get-tuple-element.40), channel_id=1, source_target_pairs={{0,3},{1,0},{2,1},{3,2},{4,7},{5,4},{6,5},{7,6},{8,11},{9,8},{10,9... | collective-permute-start | bytes 208904 | tf_op jit(solution)/shard_map/ppermute | solution.py:434
  45.7 0.4 middle_kernel.1.block
  46.1 0.0 copy-done.2
  46.1 1.3 %matrices_kernel.1 = (bf16[16,32,192]{2,1,0:T(8,128)(2,1)S(1)}, f32[16,8,256]{2,1,0:T(8,128)S(1)}) custom-call(f32[16,32,32]{2,1,0:T(8,128)S(1)} %copy-done.2), custom_call_target="tpu_custom_call" | custom-call | tf_op jit(solution)/shard_map/matrices_kernel/pallas_call | solution.py:411
  47.4 0.0 collective-permute-done.2.left
  47.4 0.0 collective-permute-done.3.right
  47.4 2.3 %krylov_kernel.1 = (f32[3,16,32,256]{3,2,1,0:T(8,128)S(1)}, f32[32,128]{1,0:T(8,128)S(1)}) custom-call(f32[17,32,256]{2,1,0:T(8,128)S(1)} %middle_kernel.1.block, f32[17,8,128]{2,1,0:T(8,128)S(1)} %collective-permute-done.2.left, f32[17,8,128]{2,1,0:T(8,128)S(1)} %collective-permute-done.3.right, bf16[16,32,192]{2,1,0:T(8,128)(2,1)S(1)} %get-tuple-element.42.schur, ...), custom_call_target="tpu_custom_call" | custom-call | tf_op jit(solution)/shard_map/krylov_kernel/pallas_call | solution.py:411
  49.7 16.7 %all_to_all.27.gathered = f32[32,1,128]{2,1,0:T(1,128)S(1)} all-to-all(f32[32,1,128]{2,1,0:T(1,128)S(1)} %bitcast.22), channel_id=1, replica_groups=mesh['fourier'=8,'ex'=8,'ey'=4] {'ex','ey'}, dimensions={0} | all-to-all | bytes 32768 | tf_op jit(solution)/shard_map/all_to_all | solution.py:489
  66.4 0.0 copy-start.4
  66.4 1.0 %finish_kernel.1 = f32[1408,128]{1,0:T(8,128)S(1)} custom-call(f32[32,1,128]{2,1,0:T(1,128)S(1)} %all_to_all.27.gathered, f32[3,16,32,256]{3,2,1,0:T(8,128)S(1)} %get-tuple-element.45.basis, f32[16,56,128]{2,1,0:T(8,128)S(1)} %get-tuple-element.46.base, f32[4,56,128]{2,1,0:T(8,128)S(1)} %get-tuple-element.47.couple, s32[8,128]{1,0:T(8,128)S(1)} %get-tuple-element.48.cell), custom_call_target="tpu_custom_call" | custom-call | tf_op jit(solution)/shard_map/finish_kernel/pallas_call | solution.py:411
  67.4 19.1 %all_to_all.28 = f32[88,16,128]{2,1,0:T(8,128)S(1)} all-to-all(f32[88,16,128]{2,1,0:T(8,128)S(1)} %bitcast.20), channel_id=1, replica_groups=mesh['fourier'=8,'ex'=8,'ey'=4] {'fourier'}, dimensions={0} | all-to-all | bytes 1441792 | tf_op jit(solution)/shard_map/all_to_all | solution.py:425
  86.6 0.0 copy-done.4
  86.6 0.4 transform_kernel.3
  87.0 14.9 %all_to_all.29.planes = f32[88,16,128]{2,1,0:T(8,128)S(1)} all-to-all(f32[88,16,128]{2,1,0:T(8,128)S(1)} %bitcast.19), channel_id=1, replica_groups=mesh['fourier'=8,'ex'=8,'ey'=4] {'fourier'}, dimensions={0} | all-to-all | bytes 1441792 | tf_op jit(solution)/shard_map/all_to_all | solution.py:425
  101.9 0.8 leave_kernel.1
Async XLA Ops:
  0.0 18.4 %copy-start.5 = (f32[128,128]{1,0:T(8,128)S(1)}, f32[128,128]{1,0:T(8,128)}, u32[]{:S(2)}) copy-start(f32[128,128]{1,0:T(8,128)} %constant.4.clone.table) | copy-start | bytes 196612
  18.4 15.6 %copy-start = (f32[16,32,49]{2,1,0:T(8,128)S(1)}, f32[16,32,49]{2,1,0:T(8,128)}, u32[]{:S(2)}) copy-start(f32[16,32,49]{2,1,0:T(8,128)} %couple.3) | copy-start | bytes 301060
  18.9 21.5 %copy-start.1 = (f32[16,49,49]{2,0,1:T(8,128)S(1)}, f32[16,49,49]{2,0,1:T(8,128)}, u32[]{:S(2)}) copy-start(f32[16,49,49]{2,0,1:T(8,128)} %param.12) | copy-start | bytes 460996
  18.9 23.1 %copy-start.3 = (s32[8,256]{1,0:T(8,128)S(1)}, s32[8,256]{1,0:T(8,128)}, u32[]{:S(2)}) copy-start(s32[8,256]{1,0:T(8,128)} %constant.5.clone.table) | copy-start | bytes 24580
  34.7 11.4 %copy-start.2 = (f32[16,32,32]{2,1,0:T(8,128)S(1)}, f32[16,32,32]{2,1,0:T(8,128)}, u32[]{:S(2)}) copy-start(f32[16,32,32]{2,1,0:T(8,128)} %schur) | copy-start | bytes 196612
  34.7 7.3 %collective-permute-start = (f32[17,8,128]{2,1,0:T(8,128)S(1)}, f32[17,8,128]{2,1,0:T(8,128)S(1)}, u32[]{:S(2)}, u32[]{:S(2)}) collective-permute-start(f32[17,8,128]{2,1,0:T(8,128)S(1)} %get-tuple-element.31), channel_id=1, source_target_pairs={{0,4},{4,8},{8,12},{12,16},{16,20},{20,24},{24,28},{28,0},{1,5},{5... | collective-permute-start | bytes 208904 | tf_op jit(solution)/shard_map/ppermute | solution.py:434
  36.3 5.6 %collective-permute-start.1 = (f32[17,8,128]{2,1,0:T(8,128)S(1)}, f32[17,8,128]{2,1,0:T(8,128)S(1)}, u32[]{:S(2)}, u32[]{:S(2)}) collective-permute-start(f32[17,8,128]{2,1,0:T(8,128)S(1)} %get-tuple-element.32), channel_id=1, source_target_pairs={{0,28},{4,0},{8,4},{12,8},{16,12},{20,16},{24,20},{28,24},{1,29},{... | collective-permute-start | bytes 208904 | tf_op jit(solution)/shard_map/ppermute | solution.py:434
  42.8 4.6 %collective-permute-start.2 = (f32[17,8,128]{2,1,0:T(8,128)S(1)}, f32[17,8,128]{2,1,0:T(8,128)S(1)}, u32[]{:S(2)}, u32[]{:S(2)}) collective-permute-start(f32[17,8,128]{2,1,0:T(8,128)S(1)} %get-tuple-element.39), channel_id=1, source_target_pairs={{0,1},{1,2},{2,3},{3,0},{4,5},{5,6},{6,7},{7,4},{8,9},{9,10},{10,1... | collective-permute-start | bytes 208904 | tf_op jit(solution)/shard_map/ppermute | solution.py:434
  44.1 3.3 %collective-permute-start.3 = (f32[17,8,128]{2,1,0:T(8,128)S(1)}, f32[17,8,128]{2,1,0:T(8,128)S(1)}, u32[]{:S(2)}, u32[]{:S(2)}) collective-permute-start(f32[17,8,128]{2,1,0:T(8,128)S(1)} %get-tuple-element.40), channel_id=1, source_target_pairs={{0,3},{1,0},{2,1},{3,2},{4,7},{5,4},{6,5},{7,6},{8,11},{9,8},{10,9... | collective-permute-start | bytes 208904 | tf_op jit(solution)/shard_map/ppermute | solution.py:434
  66.4 20.2 %copy-start.4 = (f32[128,128]{1,0:T(8,128)S(1)}, f32[128,128]{1,0:T(8,128)}, u32[]{:S(2)}) copy-start(f32[128,128]{1,0:T(8,128)} %constant.6.table) | copy-start | bytes 196612

commit v8 on v7

--- a/solution.py
+++ b/solution.py
@@ -355,7 +355,7 @@
         sums[at : at + 8] = total
 
 
-def finish_kernel(gathered, basis, base, couple, cell, out, coefs, mixed, blocks):
+def finish_kernel(gathered, basis, base, couple, cell, out, coefs, blocks):
     total = jnp.broadcast_to(jnp.sum(gathered[...].reshape(-1, EL), axis=0, keepdims=True), (8, EL))
     b0, b1, b2, h0, h1, h2, h3, h4 = [
         total if k == 0 else pltpu.roll(total, EL - MODES * k, 1) for k in range(8)
@@ -380,12 +380,13 @@
     chosen = selection(place, XL)
     blocks[...] = jnp.zeros_like(blocks)
     for q in range(MODES // QUAD):
+        mixed = []
         for r in range(QUAD):
             m = QUAD * q + r
             c = [jnp.concatenate([coefs[i, m : m + 1, :]] * 2, 1) for i in range(3)]
             x = c[0] * basis[0, m] + c[1] * basis[1, m] + c[2] * basis[2, m]
-            mixed[m * NB : m * NB + NB, :] = both_ascending(x)
-        solved = take(mixed[QUAD * q * NB : QUAD * (q + 1) * NB, :], chosen)
+            mixed.append(both_ascending(x))
+        solved = take(jnp.concatenate(mixed, 0), chosen)
         for r in range(QUAD):
             x = solved[r * NB : r * NB + NB]
             blocks[q, NB * r : NB * r + NB, EL * r : EL * r + EL] = x
@@ -487,7 +488,7 @@
         ],
     )(block, left, right, matrix, shift, table_of_lanes)
     gathered = lax.all_to_all(sums.reshape(devices, 1, EL), ("ex", "ey"), split_axis=0, concat_axis=0, tiled=True)
-    modal = call(finish_kernel, (PADDED * MODES, EL), [pltpu.VMEM((3, MODES, EL), F32), pltpu.VMEM((MODES * NB, XL), F32), pltpu.VMEM((MODES // QUAD, QUAD * NB, QUAD * EL), F32)])(
+    modal = call(finish_kernel, (PADDED * MODES, EL), [pltpu.VMEM((3, MODES, EL), F32), pltpu.VMEM((MODES // QUAD, QUAD * NB, QUAD * EL), F32)])(
         gathered, basis, base, turned, index
     )
     modal = swap(modal.reshape(PADDED, MODES, EL)).reshape(exchanged)

time: 103 us -> 103 us (level)
  no operation moved by 1% of the time
where the time goes in v8:
time: 103 us
  blocking collectives  83.1 us (81%)
  Pallas kernels  10.2 us (10%)
  starting transfers between devices  8.6 us (8%)
    all_to_all x4, blocking collectives, swap(): lax.all_to_all(array, 'fourier', split_axis=0, concat_axis=0, tiled=True)  66.4 us
    all_to_all x1, blocking collectives, on_device(): lax.all_to_all(sums.reshape(devices, 1, EL), ('ex', 'ey'), split_axis=0,...  16.7 us
    pallas_call x11, Pallas kernels, run(): pl.pallas_call(kernel, out_shape=outs if many else outs[0], in_specs=[awa...  10.2 us
    ppermute x2, starting transfers between devices, neighbours(): lax.ppermute(to_low, axis, ring(axis, -1))  5.56 us
    ppermute x2, starting transfers between devices, neighbours(): lax.ppermute(to_high, axis, ring(axis, 1))  3.04 us
  transfers between devices with their start and end apart: 4, of which 1 were waited for; matrix products, arithmetic and copies ran while one was open for 0% of the time, Pallas kernels for 3%

profile of v8, /device:TPU:1, one launch (start us, length us, event | category | flops | bytes accessed | tf_op | source)
XLA Modules:
  0.0 102.8 jit_solution(8776925514719319334)
XLA Ops:
  0.0 0.0 copy-start.5
  0.0 1.2 %enter_kernel.1 = (f32[88,16,128]{2,1,0:T(8,128)S(1)}, s32[8,128]{1,0:T(8,128)S(1)}, s32[8,128]{1,0:T(8,128)S(1)}, f32[8,128]{1,0:T(8,128)S(1)}, f32[8,128]{1,0:T(8,128)S(1)}) custom-call(f32[81,16,128]{2,1,0:T(8,128)} %bitcast.23, f32[1,128]{1,0:T(1,128)} %bitcast.24, s32[1,128]{1,0:T(1,128)} %bitcast.25), custom_call_target="tpu_custom_call" | custom-call | tf_op jit(solution)/shard_map/enter_kernel/pallas_call | solution.py:412
  1.2 17.2 %all_to_all.25 = f32[88,16,128]{2,1,0:T(8,128)S(1)} all-to-all(f32[88,16,128]{2,1,0:T(8,128)S(1)} %get-tuple-element.27), channel_id=1, replica_groups=mesh['fourier'=8,'ex'=8,'ey'=4] {'fourier'}, dimensions={0} | all-to-all | bytes 1441792 | tf_op jit(solution)/shard_map/all_to_all | solution.py:426
  18.4 0.0 copy-start
  18.4 0.0 copy-done.5
  18.4 0.4 transform_kernel.2
  18.9 0.0 copy-start.1
  18.9 0.0 copy-start.3
  18.9 15.1 %all_to_all.26 = f32[88,16,128]{2,1,0:T(8,128)S(1)} all-to-all(f32[88,16,128]{2,1,0:T(8,128)S(1)} %bitcast.17), channel_id=1, replica_groups=mesh['fourier'=8,'ex'=8,'ey'=4] {'fourier'}, dimensions={0} | all-to-all | bytes 1441792 | tf_op jit(solution)/shard_map/all_to_all | solution.py:426
  34.0 0.0 copy-done
  34.0 0.7 condense_kernel.1
  34.7 0.0 copy-start.2
  34.7 1.7 %collective-permute-start = (f32[17,8,128]{2,1,0:T(8,128)S(1)}, f32[17,8,128]{2,1,0:T(8,128)S(1)}, u32[]{:S(2)}, u32[]{:S(2)}) collective-permute-start(f32[17,8,128]{2,1,0:T(8,128)S(1)} %get-tuple-element.31), channel_id=1, source_target_pairs={{0,4},{4,8},{8,12},{12,16},{16,20},{20,24},{24,28},{28,0},{1,5},{5... | collective-permute-start | bytes 208904 | tf_op jit(solution)/shard_map/ppermute | solution.py:435
  36.3 4.0 %collective-permute-start.1 = (f32[17,8,128]{2,1,0:T(8,128)S(1)}, f32[17,8,128]{2,1,0:T(8,128)S(1)}, u32[]{:S(2)}, u32[]{:S(2)}) collective-permute-start(f32[17,8,128]{2,1,0:T(8,128)S(1)} %get-tuple-element.32), channel_id=1, source_target_pairs={{0,28},{4,0},{8,4},{12,8},{16,12},{20,16},{24,20},{28,24},{1,29},{... | collective-permute-start | bytes 208904 | tf_op jit(solution)/shard_map/ppermute | solution.py:435
  40.4 0.0 copy-done.1
  40.4 0.9 interior_kernel.1
  41.3 0.7 collective-permute-done.low
  42.0 0.0 collective-permute-done.1.high
  42.0 0.0 copy-done.3
  42.0 0.8 columns_kernel.1
  42.8 1.4 %collective-permute-start.2 = (f32[17,8,128]{2,1,0:T(8,128)S(1)}, f32[17,8,128]{2,1,0:T(8,128)S(1)}, u32[]{:S(2)}, u32[]{:S(2)}) collective-permute-start(f32[17,8,128]{2,1,0:T(8,128)S(1)} %get-tuple-element.39), channel_id=1, source_target_pairs={{0,1},{1,2},{2,3},{3,0},{4,5},{5,6},{6,7},{7,4},{8,9},{9,10},{10,1... | collective-permute-start | bytes 208904 | tf_op jit(solution)/shard_map/ppermute | solution.py:435
  44.1 1.5 %collective-permute-start.3 = (f32[17,8,128]{2,1,0:T(8,128)S(1)}, f32[17,8,128]{2,1,0:T(8,128)S(1)}, u32[]{:S(2)}, u32[]{:S(2)}) collective-permute-start(f32[17,8,128]{2,1,0:T(8,128)S(1)} %get-tuple-element.40), channel_id=1, source_target_pairs={{0,3},{1,0},{2,1},{3,2},{4,7},{5,4},{6,5},{7,6},{8,11},{9,8},{10,9... | collective-permute-start | bytes 208904 | tf_op jit(solution)/shard_map/ppermute | solution.py:435
  45.7 0.4 middle_kernel.1.block
  46.1 0.0 copy-done.2
  46.1 1.3 %matrices_kernel.1 = (bf16[16,32,192]{2,1,0:T(8,128)(2,1)S(1)}, f32[16,8,256]{2,1,0:T(8,128)S(1)}) custom-call(f32[16,32,32]{2,1,0:T(8,128)S(1)} %copy-done.2), custom_call_target="tpu_custom_call" | custom-call | tf_op jit(solution)/shard_map/matrices_kernel/pallas_call | solution.py:412
  47.4 0.0 collective-permute-done.2.left
  47.4 0.0 collective-permute-done.3.right
  47.4 2.3 %krylov_kernel.1 = (f32[3,16,32,256]{3,2,1,0:T(8,128)S(1)}, f32[32,128]{1,0:T(8,128)S(1)}) custom-call(f32[17,32,256]{2,1,0:T(8,128)S(1)} %middle_kernel.1.block, f32[17,8,128]{2,1,0:T(8,128)S(1)} %collective-permute-done.2.left, f32[17,8,128]{2,1,0:T(8,128)S(1)} %collective-permute-done.3.right, bf16[16,32,192]{2,1,0:T(8,128)(2,1)S(1)} %get-tuple-element.42.schur, ...), custom_call_target="tpu_custom_call" | custom-call | tf_op jit(solution)/shard_map/krylov_kernel/pallas_call | solution.py:412
  49.7 16.7 %all_to_all.27.gathered = f32[32,1,128]{2,1,0:T(1,128)S(1)} all-to-all(f32[32,1,128]{2,1,0:T(1,128)S(1)} %bitcast.22), channel_id=1, replica_groups=mesh['fourier'=8,'ex'=8,'ey'=4] {'ex','ey'}, dimensions={0} | all-to-all | bytes 32768 | tf_op jit(solution)/shard_map/all_to_all | solution.py:490
  66.4 0.0 copy-start.4
  66.4 1.0 %finish_kernel.1 = f32[1408,128]{1,0:T(8,128)S(1)} custom-call(f32[32,1,128]{2,1,0:T(1,128)S(1)} %all_to_all.27.gathered, f32[3,16,32,256]{3,2,1,0:T(8,128)S(1)} %get-tuple-element.45.basis, f32[16,56,128]{2,1,0:T(8,128)S(1)} %get-tuple-element.46.base, f32[4,56,128]{2,1,0:T(8,128)S(1)} %get-tuple-element.47.couple, s32[8,128]{1,0:T(8,128)S(1)} %get-tuple-element.48.cell), custom_call_target="tpu_custom_call" | custom-call | tf_op jit(solution)/shard_map/finish_kernel/pallas_call | solution.py:412
  67.4 19.1 %all_to_all.28 = f32[88,16,128]{2,1,0:T(8,128)S(1)} all-to-all(f32[88,16,128]{2,1,0:T(8,128)S(1)} %bitcast.20), channel_id=1, replica_groups=mesh['fourier'=8,'ex'=8,'ey'=4] {'fourier'}, dimensions={0} | all-to-all | bytes 1441792 | tf_op jit(solution)/shard_map/all_to_all | solution.py:426
  86.6 0.0 copy-done.4
  86.6 0.4 transform_kernel.3
  87.0 14.9 %all_to_all.29.planes = f32[88,16,128]{2,1,0:T(8,128)S(1)} all-to-all(f32[88,16,128]{2,1,0:T(8,128)S(1)} %bitcast.19), channel_id=1, replica_groups=mesh['fourier'=8,'ex'=8,'ey'=4] {'fourier'}, dimensions={0} | all-to-all | bytes 1441792 | tf_op jit(solution)/shard_map/all_to_all | solution.py:426
  101.9 0.8 leave_kernel.1
Async XLA Ops:
  0.0 18.4 %copy-start.5 = (f32[128,128]{1,0:T(8,128)S(1)}, f32[128,128]{1,0:T(8,128)}, u32[]{:S(2)}) copy-start(f32[128,128]{1,0:T(8,128)} %constant.4.clone.table) | copy-start | bytes 196612
  18.4 15.6 %copy-start = (f32[16,32,49]{2,1,0:T(8,128)S(1)}, f32[16,32,49]{2,1,0:T(8,128)}, u32[]{:S(2)}) copy-start(f32[16,32,49]{2,1,0:T(8,128)} %couple.3) | copy-start | bytes 301060
  18.9 21.5 %copy-start.1 = (f32[16,49,49]{2,0,1:T(8,128)S(1)}, f32[16,49,49]{2,0,1:T(8,128)}, u32[]{:S(2)}) copy-start(f32[16,49,49]{2,0,1:T(8,128)} %param.12) | copy-start | bytes 460996
  18.9 23.1 %copy-start.3 = (s32[8,256]{1,0:T(8,128)S(1)}, s32[8,256]{1,0:T(8,128)}, u32[]{:S(2)}) copy-start(s32[8,256]{1,0:T(8,128)} %constant.5.clone.table) | copy-start | bytes 24580
  34.7 11.4 %copy-start.2 = (f32[16,32,32]{2,1,0:T(8,128)S(1)}, f32[16,32,32]{2,1,0:T(8,128)}, u32[]{:S(2)}) copy-start(f32[16,32,32]{2,1,0:T(8,128)} %schur) | copy-start | bytes 196612
  34.7 7.3 %collective-permute-start = (f32[17,8,128]{2,1,0:T(8,128)S(1)}, f32[17,8,128]{2,1,0:T(8,128)S(1)}, u32[]{:S(2)}, u32[]{:S(2)}) collective-permute-start(f32[17,8,128]{2,1,0:T(8,128)S(1)} %get-tuple-element.31), channel_id=1, source_target_pairs={{0,4},{4,8},{8,12},{12,16},{16,20},{20,24},{24,28},{28,0},{1,5},{5... | collective-permute-start | bytes 208904 | tf_op jit(solution)/shard_map/ppermute | solution.py:435
  36.3 5.6 %collective-permute-start.1 = (f32[17,8,128]{2,1,0:T(8,128)S(1)}, f32[17,8,128]{2,1,0:T(8,128)S(1)}, u32[]{:S(2)}, u32[]{:S(2)}) collective-permute-start(f32[17,8,128]{2,1,0:T(8,128)S(1)} %get-tuple-element.32), channel_id=1, source_target_pairs={{0,28},{4,0},{8,4},{12,8},{16,12},{20,16},{24,20},{28,24},{1,29},{... | collective-permute-start | bytes 208904 | tf_op jit(solution)/shard_map/ppermute | solution.py:435
  42.8 4.6 %collective-permute-start.2 = (f32[17,8,128]{2,1,0:T(8,128)S(1)}, f32[17,8,128]{2,1,0:T(8,128)S(1)}, u32[]{:S(2)}, u32[]{:S(2)}) collective-permute-start(f32[17,8,128]{2,1,0:T(8,128)S(1)} %get-tuple-element.39), channel_id=1, source_target_pairs={{0,1},{1,2},{2,3},{3,0},{4,5},{5,6},{6,7},{7,4},{8,9},{9,10},{10,1... | collective-permute-start | bytes 208904 | tf_op jit(solution)/shard_map/ppermute | solution.py:435
  44.1 3.3 %collective-permute-start.3 = (f32[17,8,128]{2,1,0:T(8,128)S(1)}, f32[17,8,128]{2,1,0:T(8,128)S(1)}, u32[]{:S(2)}, u32[]{:S(2)}) collective-permute-start(f32[17,8,128]{2,1,0:T(8,128)S(1)} %get-tuple-element.40), channel_id=1, source_target_pairs={{0,3},{1,0},{2,1},{3,2},{4,7},{5,4},{6,5},{7,6},{8,11},{9,8},{10,9... | collective-permute-start | bytes 208904 | tf_op jit(solution)/shard_map/ppermute | solution.py:435
  66.4 20.2 %copy-start.4 = (f32[128,128]{1,0:T(8,128)S(1)}, f32[128,128]{1,0:T(8,128)}, u32[]{:S(2)}) copy-start(f32[128,128]{1,0:T(8,128)} %constant.6.table) | copy-start | bytes 196612
